TPU v7x, 32 devices: a whole 2x2x4 slice. The times are simulated.
32 devices in a mesh: batch: 4 (over z), gy: 2 (over x), gx: 4 (over y, core).
Axes of the slice: x: 2, y: 2, z: 4, core: 2. Of those that a mesh axis runs over, the one named last changes fastest.
Arguments:
- tokens: bfloat16 [16, 32, 32, 768], P('batch', 'gy', 'gx'), may hold values from -6 to 6
- timesteps: int32 [16], P('batch'), may hold values from 0 to 999
- labels: int32 [16], P('batch'), may hold values from 0 to 1000
- class_table: bfloat16 [1001, 768], replicated, may hold values from -3 to 3
- modulate_weight: bfloat16 [768, 4608], replicated, may hold values from -0.21875 to 0.21875
- modulate_bias: bfloat16 [4608], replicated, may hold values from -1.796875 to 1.796875
- inproj_weight: bfloat16 [768, 2304], replicated, may hold values from -0.21875 to 0.21875
- inproj_bias: bfloat16 [2304], replicated, may hold values from -3 to 3
- query_gain: bfloat16 [64], replicated, may hold values from 0.796875 to 1.796875
- key_gain: bfloat16 [64], replicated, may hold values from 0.796875 to 1.796875
- outproj_weight: bfloat16 [768, 768], replicated, may hold values from -0.875 to 0.875
- outproj_bias: bfloat16 [768], replicated, may hold values from -1.796875 to 1.796875
- gate_up_weight: bfloat16 [768, 4096], replicated, may hold values from -0.21875 to 0.21875
- gate_up_bias: bfloat16 [4096], replicated, may hold values from -3 to 3
- down_weight: bfloat16 [2048, 768], replicated, may hold values from -0.125 to 0.125
- down_bias: bfloat16 [768], replicated, may hold values from -1.796875 to 1.796875
- cotangent: bfloat16 [16, 32, 32, 768], P('batch', 'gy', 'gx'), may hold values from -6 to 6
Outputs:
- output: bfloat16 [16, 32, 32, 768], P('batch', 'gy', 'gx')
- grad_tokens: bfloat16 [16, 32, 32, 768], P('batch', 'gy', 'gx')
- grad_condition: float32 [16, 768], P('batch')
- grad_class_table: float32 [1001, 768], replicated
- grad_modulate_weight: float32 [768, 4608], P('batch')
- grad_modulate_bias: float32 [4608], P('batch')
- grad_inproj_weight: float32 [768, 2304], P('batch')
- grad_inproj_bias: float32 [2304], P('batch')
- grad_query_gain: float32 [64], P('batch')
- grad_key_gain: float32 [64], P('batch')
- grad_outproj_weight: float32 [768, 768], P('batch')
- grad_outproj_bias: float32 [768], P('batch')
- grad_gate_up_weight: float32 [768, 4096], P('batch')
- grad_gate_up_bias: float32 [4096], P('batch')
- grad_down_weight: float32 [2048, 768], P('batch')
- grad_down_bias: float32 [768], P('batch')
All inputs are finite; a program needn't handle non-finite values.
Results may differ from a plain program's by a relative error of at most 0.025.
Values may be sent and summed in bfloat16 or wider, within the bound.
A program may use at most 256 MiB of HBM per device.

v0:
```python
import math

import jax
import jax.numpy as jnp
from jax import lax
from jax.sharding import PartitionSpec as P

NORM_EPSILON = 1e-06


def mean_norm(values):
    factor = lax.rsqrt(jnp.mean(values * values, axis=-1, keepdims=True) + NORM_EPSILON)
    return (values * factor, factor)


def norm_back(normed, factor, grad_normed):
    return factor * (grad_normed - normed * jnp.mean(grad_normed * normed, axis=-1, keepdims=True))


def time_features(step_values, model_width):
    half_width = model_width // 2
    frequencies = jnp.exp(
        -math.log(10000.0) * jnp.arange(half_width, dtype=jnp.float32) / half_width
    )
    angles = step_values.astype(jnp.float32)[:, None] * frequencies[None, :]
    return jnp.concatenate([jnp.cos(angles), jnp.sin(angles)], axis=-1)


def rotary_tables(row_places, column_places, head_size):
    quarter = head_size // 4
    frequencies = jnp.exp(-math.log(10000.0) * jnp.arange(quarter, dtype=jnp.float32) / quarter)
    angles = jnp.stack(
        [row_places[:, None] * frequencies[None, :], column_places[:, None] * frequencies[None, :]],
        axis=1,
    )
    return (jnp.cos(angles)[:, None], jnp.sin(angles)[:, None])


def rotate(values, cosine_table, sine_table):
    full_shape = values.shape
    split_parts = values.reshape(full_shape[:-1] + (2, 2, full_shape[-1] // 4))
    leading = split_parts[..., 0, :]
    trailing = split_parts[..., 1, :]
    turned = jnp.stack(
        [
            leading * cosine_table - trailing * sine_table,
            trailing * cosine_table + leading * sine_table,
        ],
        axis=-2,
    )
    return turned.reshape(full_shape)


def rotate_back(grads, cosine_table, sine_table):
    full_shape = grads.shape
    split_parts = grads.reshape(full_shape[:-1] + (2, 2, full_shape[-1] // 4))
    leading = split_parts[..., 0, :]
    trailing = split_parts[..., 1, :]
    turned = jnp.stack(
        [
            leading * cosine_table + trailing * sine_table,
            trailing * cosine_table - leading * sine_table,
        ],
        axis=-2,
    )
    return turned.reshape(full_shape)


def inner_rows(left_side, right_side):
    return lax.dot_general(
        left_side, right_side, (((0,), (0,)), ((), ())), preferred_element_type=jnp.float32
    )


def times_transposed(left_side, right_side):
    return lax.dot_general(
        left_side, right_side, (((1,), (1,)), ((), ())), preferred_element_type=jnp.float32
    )


def to_blocks(array_in, block_count):
    return array_in.reshape((block_count, array_in.shape[0] // block_count) + array_in.shape[1:])


def from_blocks(array_in):
    return array_in.reshape((array_in.shape[0] * array_in.shape[1],) + array_in.shape[2:])


def attend(queries, key_rows, value_rows, score_scale):
    scores = (
        jnp.einsum("bqhd,bkhd->bhqk", queries, key_rows, preferred_element_type=jnp.float32)
        * score_scale
    )
    row_peak = jnp.max(scores, axis=-1, keepdims=True)
    row_total = jnp.sum(jnp.exp(scores - row_peak), axis=-1, keepdims=True)
    logsum = row_peak + jnp.log(row_total)
    probabilities = jnp.exp(scores - logsum).astype(jnp.bfloat16)
    mixed_heads = jnp.einsum(
        "bhqk,bkhd->bqhd", probabilities, value_rows, preferred_element_type=jnp.float32
    )
    return (mixed_heads, logsum[..., 0])


def attend_back(queries, key_rows, value_rows, grad_mixed, logsum, score_scale):
    scores = (
        jnp.einsum("bqhd,bkhd->bhqk", queries, key_rows, preferred_element_type=jnp.float32)
        * score_scale
    )
    probabilities = jnp.exp(scores - logsum[..., None])
    grad_probs = jnp.einsum(
        "bqhd,bkhd->bhqk", grad_mixed, value_rows, preferred_element_type=jnp.float32
    )
    inner_sums = jnp.sum(probabilities * grad_probs, axis=-1, keepdims=True)
    grad_scores = (probabilities * (grad_probs - inner_sums)).astype(jnp.bfloat16)
    grad_queries = (
        jnp.einsum("bhqk,bkhd->bqhd", grad_scores, key_rows, preferred_element_type=jnp.float32)
        * score_scale
    )
    grad_keys = (
        jnp.einsum("bhqk,bqhd->bkhd", grad_scores, queries, preferred_element_type=jnp.float32)
        * score_scale
    )
    grad_values = jnp.einsum(
        "bhqk,bqhd->bkhd",
        probabilities.astype(jnp.bfloat16),
        grad_mixed,
        preferred_element_type=jnp.float32,
    )
    return (grad_queries, grad_keys, grad_values)


def body(
    tokens,
    timesteps,
    labels,
    class_table,
    modulate_weight,
    modulate_bias,
    inproj_weight,
    inproj_bias,
    query_gain,
    key_gain,
    outproj_weight,
    outproj_bias,
    gate_up_weight,
    gate_up_bias,
    down_weight,
    down_bias,
    cotangent,
):
    image_count, tile_rows, tile_cols, model_width = tokens.shape
    cell_count = tile_rows * tile_cols
    row_count = image_count * cell_count
    head_size = query_gain.shape[0]
    head_count = model_width // head_size
    hidden_width = down_weight.shape[0]
    score_scale = head_size ** (-0.5)
    block_size = math.gcd(image_count, max(1, 512 // cell_count))
    block_count = image_count // block_size
    highest = lax.Precision.HIGHEST
    positions = jnp.arange(cell_count, dtype=jnp.int32)
    row_places = (lax.axis_index("gy") * tile_rows + positions // tile_cols).astype(jnp.float32)
    column_places = (lax.axis_index("gx") * tile_cols + positions % tile_cols).astype(jnp.float32)
    cosine_table, sine_table = rotary_tables(row_places, column_places, head_size)
    picked = jnp.take(class_table, labels, axis=0).astype(jnp.float32)
    condition = time_features(timesteps, model_width) + picked
    cond_act = jax.nn.silu(condition).astype(jnp.bfloat16)
    modulation = jnp.dot(
        cond_act, modulate_weight, preferred_element_type=jnp.float32
    ) + modulate_bias.astype(jnp.float32)
    shift_one, scale_one, gate_one, shift_two, scale_two, gate_two = [
        portion[:, None, :] for portion in jnp.split(modulation, 6, axis=-1)
    ]
    inputs = tokens.reshape(image_count, cell_count, model_width).astype(jnp.float32)
    normed_one, factor_one = mean_norm(inputs)
    hidden_one = (
        (normed_one * (1.0 + scale_one) + shift_one)
        .astype(jnp.bfloat16)
        .reshape(row_count, model_width)
    )
    projected = jnp.dot(
        hidden_one, inproj_weight, preferred_element_type=jnp.float32
    ) + inproj_bias.astype(jnp.float32)
    projected = projected.reshape(image_count, cell_count, 3, head_count, head_size)
    query_normed, query_factor = mean_norm(projected[:, :, 0])
    key_normed, key_factor = mean_norm(projected[:, :, 1])
    queries = rotate(
        query_normed * query_gain.astype(jnp.float32), cosine_table, sine_table
    ).astype(jnp.bfloat16)
    key_rows = rotate(key_normed * key_gain.astype(jnp.float32), cosine_table, sine_table).astype(
        jnp.bfloat16
    )
    value_rows = projected[:, :, 2].astype(jnp.bfloat16)
    key_all, value_all = (
        lax.all_gather(key_rows, ("gy", "gx"), axis=1, tiled=True),
        lax.all_gather(value_rows, ("gy", "gx"), axis=1, tiled=True),
    )
    mixed_heads, logsum = lax.map(
        lambda operands: attend(operands[0], operands[1], operands[2], score_scale),
        (
            to_blocks(queries, block_count),
            to_blocks(key_all, block_count),
            to_blocks(value_all, block_count),
        ),
    )
    mixed_heads = from_blocks(mixed_heads)
    logsum = from_blocks(logsum)
    mixed_low = mixed_heads.astype(jnp.bfloat16).reshape(row_count, model_width)
    attended = jnp.dot(
        mixed_low, outproj_weight, preferred_element_type=jnp.float32
    ) + outproj_bias.astype(jnp.float32)
    attended = attended.reshape(image_count, cell_count, model_width)
    middle = inputs + gate_one * attended
    normed_two, factor_two = mean_norm(middle)
    hidden_two = (
        (normed_two * (1.0 + scale_two) + shift_two)
        .astype(jnp.bfloat16)
        .reshape(row_count, model_width)
    )
    gate_up = jnp.dot(
        hidden_two, gate_up_weight, preferred_element_type=jnp.float32
    ) + gate_up_bias.astype(jnp.float32)
    gate_part = gate_up[:, :hidden_width]
    up_part = gate_up[:, hidden_width:]
    gate_sigmoid = jax.nn.sigmoid(gate_part)
    activated = gate_part * gate_sigmoid
    product = (activated * up_part).astype(jnp.bfloat16)
    feed_out = jnp.dot(product, down_weight, preferred_element_type=jnp.float32) + down_bias.astype(
        jnp.float32
    )
    feed_out = feed_out.reshape(image_count, cell_count, model_width)
    output = (middle + gate_two * feed_out).astype(jnp.bfloat16).reshape(tokens.shape)
    grad_out = cotangent.reshape(image_count, cell_count, model_width).astype(jnp.float32)
    grad_gate_two = jnp.sum(grad_out * feed_out, axis=1)
    grad_feed = (gate_two * grad_out).astype(jnp.bfloat16).reshape(row_count, model_width)
    grad_down_w = inner_rows(product, grad_feed)
    grad_down_b = jnp.sum(grad_feed.astype(jnp.float32), axis=0)
    grad_product = times_transposed(grad_feed, down_weight)
    grad_gate_part = (
        grad_product * up_part * gate_sigmoid * (1.0 + gate_part * (1.0 - gate_sigmoid))
    )
    grad_up_part = grad_product * activated
    grad_gate_up = jnp.concatenate([grad_gate_part, grad_up_part], axis=-1).astype(jnp.bfloat16)
    grad_gu_w = inner_rows(hidden_two, grad_gate_up)
    grad_gu_b = jnp.sum(grad_gate_up.astype(jnp.float32), axis=0)
    grad_hidden_two = times_transposed(grad_gate_up, gate_up_weight).reshape(
        image_count, cell_count, model_width
    )
    grad_shift_two = jnp.sum(grad_hidden_two, axis=1)
    grad_scale_two = jnp.sum(grad_hidden_two * normed_two, axis=1)
    grad_middle = grad_out + norm_back(normed_two, factor_two, grad_hidden_two * (1.0 + scale_two))
    grad_gate_one = jnp.sum(grad_middle * attended, axis=1)
    grad_attended = (gate_one * grad_middle).astype(jnp.bfloat16).reshape(row_count, model_width)
    grad_out_w = inner_rows(mixed_low, grad_attended)
    grad_out_b = jnp.sum(grad_attended.astype(jnp.float32), axis=0)
    grad_mixed = (
        times_transposed(grad_attended, outproj_weight)
        .astype(jnp.bfloat16)
        .reshape(image_count, cell_count, head_count, head_size)
    )
    grad_queries, grad_keys_all, grad_values_all = lax.map(
        lambda operands: attend_back(
            operands[0], operands[1], operands[2], operands[3], operands[4], score_scale
        ),
        (
            to_blocks(queries, block_count),
            to_blocks(key_all, block_count),
            to_blocks(value_all, block_count),
            to_blocks(grad_mixed, block_count),
            to_blocks(logsum, block_count),
        ),
    )
    grad_queries = from_blocks(grad_queries)
    grad_key_rows, grad_values = (
        lax.psum_scatter(
            from_blocks(grad_keys_all).astype(jnp.bfloat16),
            ("gy", "gx"),
            scatter_dimension=1,
            tiled=True,
        ).astype(jnp.float32),
        lax.psum_scatter(
            from_blocks(grad_values_all).astype(jnp.bfloat16),
            ("gy", "gx"),
            scatter_dimension=1,
            tiled=True,
        ).astype(jnp.float32),
    )
    grad_query_turned = rotate_back(grad_queries, cosine_table, sine_table)
    grad_key_turned = rotate_back(grad_key_rows, cosine_table, sine_table)
    grad_query_gain = jnp.sum(grad_query_turned * query_normed, axis=(0, 1, 2))
    grad_key_gain = jnp.sum(grad_key_turned * key_normed, axis=(0, 1, 2))
    grad_query_raw = norm_back(
        query_normed, query_factor, grad_query_turned * query_gain.astype(jnp.float32)
    )
    grad_key_raw = norm_back(key_normed, key_factor, grad_key_turned * key_gain.astype(jnp.float32))
    grad_projected = (
        jnp.stack([grad_query_raw, grad_key_raw, grad_values], axis=2)
        .astype(jnp.bfloat16)
        .reshape(row_count, 3 * model_width)
    )
    grad_in_w = inner_rows(hidden_one, grad_projected)
    grad_in_b = jnp.sum(grad_projected.astype(jnp.float32), axis=0)
    grad_hidden_one = times_transposed(grad_projected, inproj_weight).reshape(
        image_count, cell_count, model_width
    )
    grad_shift_one = jnp.sum(grad_hidden_one, axis=1)
    grad_scale_one = jnp.sum(grad_hidden_one * normed_one, axis=1)
    grad_inputs = grad_middle + norm_back(
        normed_one, factor_one, grad_hidden_one * (1.0 + scale_one)
    )
    grad_tokens = grad_inputs.astype(jnp.bfloat16).reshape(tokens.shape)
    grad_modulation = jnp.concatenate(
        [
            grad_shift_one,
            grad_scale_one,
            grad_gate_one,
            grad_shift_two,
            grad_scale_two,
            grad_gate_two,
        ],
        axis=-1,
    )
    grad_mod_w = jnp.dot(cond_act.astype(jnp.float32).T, grad_modulation, precision=highest)
    grad_mod_b = jnp.sum(grad_modulation, axis=0)
    full_modulation = lax.psum(grad_modulation.astype(jnp.bfloat16), ("gy", "gx")).astype(
        jnp.float32
    )
    grad_cond_act = jnp.dot(
        full_modulation, modulate_weight.astype(jnp.float32).T, precision=highest
    )
    cond_sigmoid = jax.nn.sigmoid(condition)
    grad_condition = grad_cond_act * cond_sigmoid * (1.0 + condition * (1.0 - cond_sigmoid))
    onehot = (labels[:, None] == jnp.arange(class_table.shape[0], dtype=jnp.int32)[None, :]).astype(
        jnp.float32
    )
    grad_table = lax.psum(
        jnp.dot(onehot.T, grad_condition, precision=highest).astype(jnp.bfloat16), "batch"
    ).astype(jnp.float32)
    shards = (
        lax.psum_scatter(
            grad_mod_w.astype(jnp.bfloat16), "batch", scatter_dimension=0, tiled=True
        ).astype(jnp.float32),
        lax.psum_scatter(
            grad_mod_b.astype(jnp.bfloat16), "batch", scatter_dimension=0, tiled=True
        ).astype(jnp.float32),
        lax.psum_scatter(
            grad_in_w.astype(jnp.bfloat16), "batch", scatter_dimension=0, tiled=True
        ).astype(jnp.float32),
        lax.psum_scatter(
            grad_in_b.astype(jnp.bfloat16), "batch", scatter_dimension=0, tiled=True
        ).astype(jnp.float32),
        lax.psum_scatter(
            grad_query_gain.astype(jnp.bfloat16), "batch", scatter_dimension=0, tiled=True
        ).astype(jnp.float32),
        lax.psum_scatter(
            grad_key_gain.astype(jnp.bfloat16), "batch", scatter_dimension=0, tiled=True
        ).astype(jnp.float32),
        lax.psum_scatter(
            grad_out_w.astype(jnp.bfloat16), "batch", scatter_dimension=0, tiled=True
        ).astype(jnp.float32),
        lax.psum_scatter(
            grad_out_b.astype(jnp.bfloat16), "batch", scatter_dimension=0, tiled=True
        ).astype(jnp.float32),
        lax.psum_scatter(
            grad_gu_w.astype(jnp.bfloat16), "batch", scatter_dimension=0, tiled=True
        ).astype(jnp.float32),
        lax.psum_scatter(
            grad_gu_b.astype(jnp.bfloat16), "batch", scatter_dimension=0, tiled=True
        ).astype(jnp.float32),
        lax.psum_scatter(
            grad_down_w.astype(jnp.bfloat16), "batch", scatter_dimension=0, tiled=True
        ).astype(jnp.float32),
        lax.psum_scatter(
            grad_down_b.astype(jnp.bfloat16), "batch", scatter_dimension=0, tiled=True
        ).astype(jnp.float32),
    )
    totals = (
        lax.psum(shards[0].astype(jnp.bfloat16), ("gy", "gx")).astype(jnp.float32),
        lax.psum(shards[1].astype(jnp.bfloat16), ("gy", "gx")).astype(jnp.float32),
        lax.psum(shards[2].astype(jnp.bfloat16), ("gy", "gx")).astype(jnp.float32),
        lax.psum(shards[3].astype(jnp.bfloat16), ("gy", "gx")).astype(jnp.float32),
        lax.psum(shards[4].astype(jnp.bfloat16), ("gy", "gx")).astype(jnp.float32),
        lax.psum(shards[5].astype(jnp.bfloat16), ("gy", "gx")).astype(jnp.float32),
        lax.psum(shards[6].astype(jnp.bfloat16), ("gy", "gx")).astype(jnp.float32),
        lax.psum(shards[7].astype(jnp.bfloat16), ("gy", "gx")).astype(jnp.float32),
        lax.psum(shards[8].astype(jnp.bfloat16), ("gy", "gx")).astype(jnp.float32),
        lax.psum(shards[9].astype(jnp.bfloat16), ("gy", "gx")).astype(jnp.float32),
        lax.psum(shards[10].astype(jnp.bfloat16), ("gy", "gx")).astype(jnp.float32),
        lax.psum(shards[11].astype(jnp.bfloat16), ("gy", "gx")).astype(jnp.float32),
    )
    return (
        output,
        grad_tokens,
        grad_condition,
        grad_table,
        totals[0],
        totals[1],
        totals[2],
        totals[3],
        totals[4],
        totals[5],
        totals[6],
        totals[7],
        totals[8],
        totals[9],
        totals[10],
        totals[11],
    )


def solution(mesh):
    placed = (
        P("batch", "gy", "gx", None),
        P("batch"),
        P("batch"),
        P(),
        P(),
        P(),
        P(),
        P(),
        P(),
        P(),
        P(),
        P(),
        P(),
        P(),
        P(),
        P(),
        P("batch", "gy", "gx", None),
    )
    return jax.shard_map(
        body,
        mesh=mesh,
        in_specs=placed,
        out_specs=(
            P("batch", "gy", "gx", None),
            P("batch", "gy", "gx", None),
            P("batch", None),
            P(),
            P("batch", None),
            P("batch"),
            P("batch", None),
            P("batch"),
            P("batch"),
            P("batch"),
            P("batch", None),
            P("batch"),
            P("batch", None),
            P("batch"),
            P("batch", None),
            P("batch"),
        ),
        check_vma=False,
    )
```

profile of v0, /device:TPU:0, one launch (start us, length us, event | category | flops | bytes accessed | tf_op | source)
XLA Modules:
  0.0 1005.4 jit_solution(17262244903814229039)
XLA Ops:
  34.2 6.1 copy.64
  40.3 6.3 reshape.520
  60.6 42.5 %all-gather.4.cloned.1.call-done = bf16[4,1024,12,64]{1,3,2,0:T(8,128)(2,1)} async-done(((bf16[4,128,12,64]{1,3,2,0:T(8,128)(2,1)}), bf16[4,1024,12,64]{1,3,2,0:T(8,128)(2,1)}) %all-gather.4.cloned.1.call-update) | async-done | bytes 6291472 | tf_op jit(solution)/shard_map/all_gather | solution.py:195
  103.1 15.6 %multiply_reduce_fusion.1 = (f32[4,12,128]{2,1,0:T(8,128)S(1)}, f32[4,12,128,1024]{3,2,1,0:T(8,128)}) fusion(bf16[4,128,12,64]{1,3,2,0:T(8,128)(2,1)} %bitcast.235, bf16[4,1024,12,64]{1,3,2,0:T(8,128)(2,1)} %all-gather.4.cloned.1.call-done), kind=kOutput, calls=%fused_computation.5 | convolution fusion | flops 817883136 | bytes 32268288 | tf_op jit(solution)/shard_map/while/body/eval_jaxpr/bqhd,bkhd->bhqk/dot_general | solution.py:91
  118.8 11.1 %exponential_reduce_fusion = f32[4,12,128]{2,1,0:T(8,128)S(1)} fusion(f32[4,12,128,1024]{3,2,1,0:T(8,128)} %get-tuple-element.141, f32[4,12,128]{2,1,0:T(8,128)S(1)} %get-tuple-element.140), kind=kLoop, calls=%fused_computation.4 | loop fusion | flops 18868224 | bytes 25214976 | tf_op jit(solution)/shard_map/while/body/eval_jaxpr/reduce_sum | solution.py:95
  130.5 21.6 %all-gather.6.cloned.1.call-done = bf16[4,1024,1,12,64]{1,4,3,0,2:T(8,128)(2,1)} async-done(((bf16[4,128,1,12,64]{1,4,3,0,2:T(8,128)(2,1)}), bf16[4,1024,1,12,64]{1,4,3,0,2:T(8,128)(2,1)}) %all-gather.6.cloned.1.call-update) | async-done | bytes 6291472 | tf_op jit(solution)/shard_map/all_gather | solution.py:196
  152.2 12.5 %fusion.47 = bf16[4,128,12,64]{1,3,2,0:T(8,128)(2,1)S(1)} fusion(f32[4,12,128,1024]{3,2,1,0:T(8,128)} %get-tuple-element.141, f32[4,12,128]{2,1,0:T(8,128)} %log_add_fusion, bf16[4,1024,1,12,64]{1,4,3,0,2:T(8,128)(2,1)} %all-gather.6.cloned.1.call-done), kind=kOutput, calls=%fused_computation.102 | convolution fusion | flops 824573952 | bytes 32268288 | tf_op jit(solution)/shard_map/while/body/eval_jaxpr/bhqk,bkhd->bqhd/dot_general | solution.py:98
  172.1 9.0 convolution_add_fusion
  181.1 6.9 multiply_convert_fusion.3
  201.0 12.8 %convert_bitcast_fusion = bf16[4,1024,12,64]{1,3,2,0:T(8,128)(2,1)} fusion(f32[4,12,128,1024]{3,2,1,0:T(8,128)} %get-tuple-element.141, f32[4,12,128]{2,1,0:T(8,128)} %log_add_fusion, bf16[4,128,12,64]{1,0,3,2:T(4,128)(2,1)} %squeeze.40), kind=kOutput, calls=%fused_computation.15 | convolution fusion | flops 827326464 | bytes 32268288 | tf_op jit(solution)/shard_map/while/body/eval_jaxpr/bhqk,bqhd->bkhd/dot_general | solution.py:123
  213.9 23.7 %copy.85 = bf16[4,1024,12,64]{3,2,0,1:T(8,128)(2,1)} copy(bf16[4,1024,12,64]{1,3,2,0:T(8,128)(2,1)} %convert_bitcast_fusion) | data formatting | bytes 12582912
  237.5 21.4 %reshape.551 = bf16[1024,3072]{1,0:T(8,128)(2,1)} reshape(bf16[1024,4,12,64]{3,2,1,0:T(8,128)(2,1)} %bitcast.224) | data formatting | bytes 12582912
  259.0 24.7 %multiply_reduce_fusion = (f32[4,12,128]{2,1,0:T(8,128)}, f32[4,12,128,1024]{3,2,1,0:T(8,128)}) fusion(f32[4,12,128,1024]{3,2,1,0:T(8,128)} %get-tuple-element.141, f32[4,12,128]{2,1,0:T(8,128)} %log_add_fusion, bf16[4,1024,1,12,64]{1,4,3,0,2:T(8,128)(2,1)} %all-gather.6.cloned.1.call-done, bf16[4,128,12,64]{1,0,3,2:T(4,128)(2,1)} %squeeze.40), kind=kOutput, calls=%fused_computation.2 | convolution fusion | flops 830466048 | bytes 57458688 | tf_op jit(solution)/shard_map/while/body/eval_jaxpr/bqhd,bkhd->bhqk/dot_general | solution.py:110
  283.7 17.1 %multiply_convert_fusion = bf16[4,12,128,1024]{3,2,1,0:T(8,128)(2,1)S(1)} fusion(f32[4,12,128,1024]{3,2,1,0:T(8,128)} %get-tuple-element.145, f32[4,12,128,1024]{3,2,1,0:T(8,128)} %get-tuple-element.141, f32[4,12,128]{2,1,0:T(8,128)} %get-tuple-element.144, f32[4,12,128]{2,1,0:T(8,128)} %log_add_fusion), kind=kLoop, calls=%fused_computation.1 | loop fusion | flops 31457280 | bytes 62963712 | tf_op jit(solution)/shard_map/while/body/eval_jaxpr/convert_element_type | solution.py:114
  300.8 4.5 copy-done.1
  309.0 23.7 %copy.83 = bf16[4,1024,12,64]{3,2,0,1:T(8,128)(2,1)} copy(bf16[4,1024,12,64]{1,3,2,0:T(8,128)(2,1)} %fusion.1) | data formatting | bytes 12582912
  332.6 21.4 %reshape.549 = bf16[1024,3072]{1,0:T(8,128)(2,1)} reshape(bf16[1024,4,12,64]{3,2,1,0:T(8,128)(2,1)} %bitcast.225) | data formatting | bytes 12582912
  357.4 5.3 convolution_convert_fusion.3
  363.2 9.4 convolution_convert_fusion.1
  378.4 12.2 %convolution_multiply_fusion = f32[4,12,64,128]{3,2,1,0:T(8,128)} fusion(bf16[4,1024,12,64]{1,3,2,0:T(8,128)(2,1)} %all-gather.4.cloned.1.call-done, bf16[4,12,128,1024]{3,2,1,0:T(8,128)(2,1)} %copy-done.1), kind=kOutput, calls=%fused_computation.98 | convolution fusion | flops 805699584 | bytes 20447232 | tf_op jit(solution)/shard_map/while/body/eval_jaxpr/bhqk,bkhd->bqhd/dot_general | solution.py:116
  399.2 16.9 %reduce-scatter.22.cloned.1.call-done = bf16[128,3072]{1,0:T(8,128)(2,1)} async-done(((bf16[1024,3072]{1,0:T(8,128)(2,1)}), bf16[128,3072]{1,0:T(8,128)(2,1)}) %reduce-scatter.22.cloned.1.call-update) | async-done | bytes 786448
  433.6 17.9 %fusion.77 = (bf16[3,12,64]{2,1,0:T(8,128)(2,1)}, bf16[4,128,3,12,64]{1,0,4,3,2:T(4,128)(2,1)S(1)}) fusion(bf16[4,128,1,12,64]{1,0,4,3,2:T(4,128)(2,1)S(1)} %bitcast.245, bf16[4,128,1,12,64]{1,0,4,3,2:T(4,128)(2,1)S(1)} %get-tuple-element.107, bf16[4,128,1,12,64]{1,0,4,3,2:T(4,128)(2,1)S(1)} %get-tuple-element.106), kind=kLoop, calls=%fused_computation.175 | loop fusion | flops 3536640 | bytes 4723200 | tf_op jit(solution)/shard_map/reduce_sum | solution.py:302
  455.9 4.6 fusion.25
  471.5 8.7 convolution_convert_fusion
  494.0 21.0 %all-reduce.9 = (bf16[4608]{0:T(1024)(128)(2,1)}, bf16[2304]{0:T(1024)(128)(2,1)}, bf16[64]{0:T(256)(128)(2,1)}, bf16[64]{0:T(256)(128)(2,1)}, bf16[768]{0:T(102...) all-reduce(bf16[4608]{0:T(1024)(128)(2,1)} %get-tuple-element.120, ...), channel_id=6, replica_groups=mesh['batch'=4,'gy'=2,'gx'=4] {'batch'}, use_global_device_ids=true, to_apply=%region_24.25.clone | all-reduce | flops 12672 | bytes 50688
  523.4 24.6 %all-reduce.7 = (bf16[4,4608]{1,0:T(4,128)(2,1)}, bf16[1152]{0:T(1024)(128)(2,1)}, bf16[576]{0:T(1024)(128)(2,1)}, bf16[16]{0:T(256)(128)(2,1)}, bf16[16]{0:T(25...) all-reduce(bf16[4,4608]{1,0:T(4,128)(2,1)} %get-tuple-element.121, ...), channel_id=1, replica_groups=mesh['batch'=4,'gy'=2,'gx'=4] {'gy','gx'}, use_global_device_ids=true, to_apply=%region_19.20 | all-reduce | flops 21600 | bytes 86400 | tf_op jit(solution)/shard_map/psum | solution.py:325
  548.0 5.0 fusion.54
  556.4 66.9 %reduce-scatter.18.cloned.1.call-done = bf16[192,4096]{1,0:T(8,128)(2,1)} async-done(((bf16[768,4096]{1,0:T(8,128)(2,1)}), bf16[192,4096]{1,0:T(8,128)(2,1)}) %reduce-scatter.18.cloned.1.call-update) | async-done | bytes 1572880 | tf_op jit(solution)/shard_map/reduce_scatter | solution.py:364
  623.3 69.9 %reduce-scatter.14.cloned.1.call-done = bf16[192,2304]{1,0:T(8,128)(2,1)} async-done(((bf16[768,2304]{1,0:T(8,128)(2,1)}), bf16[192,2304]{1,0:T(8,128)(2,1)}) %reduce-scatter.14.cloned.1.call-update) | async-done | bytes 884752 | tf_op jit(solution)/shard_map/reduce_scatter | solution.py:346
  693.2 126.0 %reduce-scatter.12.cloned.1.call-done = bf16[192,4608]{1,0:T(8,128)(2,1)} async-done(((bf16[768,4608]{1,0:T(8,128)(2,1)}), bf16[192,4608]{1,0:T(8,128)(2,1)}) %reduce-scatter.12.cloned.1.call-update) | async-done | bytes 1769488 | tf_op jit(solution)/shard_map/reduce_scatter | solution.py:340
  830.7 60.5 %all-reduce.13.cloned.1.call-done = bf16[1001,768]{1,0:T(8,128)(2,1)} async-done(((bf16[1001,768]{1,0:T(8,128)(2,1)}), bf16[1001,768]{1,0:T(8,128)(2,1)}) %all-reduce.13.cloned.1.call-update) | async-done | bytes 1537552 | tf_op jit(solution)/shard_map/psum | solution.py:336
  894.5 93.3 %all-reduce.15.cloned.1.call-done = (bf16[192,4608]{1,0:T(8,128)(2,1)}, bf16[192,2304]{1,0:T(8,128)(2,1)}, bf16[192,768]{1,0:T(8,128)(2,1)}, bf16[192,4096]{1,0:T(8,128)(2,1)}, bf16[512,768]{1,0:T(8,128)(2,1)}) async-done(((bf16[192,4608]{1,0:T(8,128)(2,1)}, bf16[192,2304]{1,0:T(8,128)(2,1)}, bf16[192,768]{1,0:T(8,128)(2,1)}, bf16[192,4096]{1,0:T(8,128)(2,1)}, bf16[512,768]{1,0:T(8,128)(2,1)}), ...) | async-done | bytes 5308432 | tf_op jit(solution)/shard_map/psum | solution.py:378
  (276 shorter events, 163.9 us)
Async XLA Ops:
  7.2 22.8 %copy-start = (bf16[768,2304]{1,0:T(8,128)(2,1)S(1)}, bf16[768,2304]{1,0:T(8,128)(2,1)}, u32[]{:S(2)}) copy-start(bf16[768,2304]{1,0:T(8,128)(2,1)} %param.23) | copy-start | bytes 10616836
  7.2 95.9 %all-gather.4.cloned.1.call-start = ((), (), s32[]{:S(2)}) async-start(), calls=%async_computation.7 | async-start | bytes 7077888 | tf_op jit(solution)/shard_map/all_gather | solution.py:195
  24.3 5.4 copy-start.5
  53.7 98.5 %all-gather.6.cloned.1.call-start = ((), (), s32[]{:S(2)}) async-start(), calls=%async_computation.14 | async-start | bytes 7077888 | tf_op jit(solution)/shard_map/all_gather | solution.py:196
  56.5 334.1 %reduce-scatter.24.cloned.1.call-start = ((), (), s32[]{:S(2)}) async-start(), calls=%async_computation.16 | async-start | bytes 7077888
  172.1 9.0 copy-start.25
  172.1 9.0 copy-start.26
  172.1 9.0 copy-start.17
  181.1 7.0 slice-start.2
  181.1 7.0 copy-start.3
  181.1 7.0 copy-start.7
  181.1 7.0 slice-start.3
  181.1 7.0 copy-start.28
  258.9 157.2 %reduce-scatter.22.cloned.1.call-start = ((), (), s32[]{:S(2)}) async-start(), calls=%async_computation.15 | async-start | bytes 7077888
  283.7 21.6 %copy-start.15 = (bf16[4,128,12,2,2,16]{1,5,4,3,2,0:T(8,128)(2,1)S(1)}, bf16[4,128,12,2,2,16]{1,5,4,3,2,0:T(8,128)(2,1)}, u32[]{:S(2)}) copy-start(bf16[4,128,12,2,2,16]{1,5,4,3,2,0:T(8,128)(2,1)} %pad_maximum_fusion.5) | copy-start | bytes 2359300
  300.8 4.5 copy-start.1
  354.0 202.3 %reduce-scatter.16.cloned.1.call-start = ((), (), s32[]{:S(2)}) async-start(), calls=%async_computation.11 | async-start | bytes 1474560 | tf_op jit(solution)/shard_map/reduce_scatter | solution.py:358
  357.3 199.1 %reduce-scatter.20.cloned.1.call-start = ((), (), s32[]{:S(2)}) async-start(), calls=%async_computation.13 | async-start | bytes 3932160 | tf_op jit(solution)/shard_map/reduce_scatter | solution.py:370
  362.6 260.6 %reduce-scatter.18.cloned.1.call-start = ((), (), s32[]{:S(2)}) async-start(), calls=%async_computation.12 | async-start | bytes 7864320 | tf_op jit(solution)/shard_map/reduce_scatter | solution.py:364
  372.6 320.6 %reduce-scatter.14.cloned.1.call-start = ((), (), s32[]{:S(2)}) async-start(), calls=%async_computation.10 | async-start | bytes 4423680 | tf_op jit(solution)/shard_map/reduce_scatter | solution.py:346
  451.5 4.4 copy-start.20
  451.5 4.4 copy-start.29
  451.6 4.4 copy-start.36
  451.6 4.3 copy-start.47
  455.9 4.6 copy-start.43
  466.5 5.0 copy-start.55
  466.5 352.7 %reduce-scatter.12.cloned.1.call-start = ((), (), s32[]{:S(2)}) async-start(), calls=%async_computation.9 | async-start | bytes 8847360 | tf_op jit(solution)/shard_map/reduce_scatter | solution.py:340
  480.2 411.1 %all-reduce.13.cloned.1.call-start = ((), (), s32[]{:S(2)}) async-start(), calls=%async_computation.8 | async-start | bytes 3096576 | tf_op jit(solution)/shard_map/psum | solution.py:336
  486.6 7.4 copy-start.52
  548.0 5.6 copy-start.59
  556.3 431.5 %all-reduce.15.cloned.1.call-start = ((), (), s32[]{:S(2)}) async-start(), calls=%async_computation.17 | async-start | bytes 10616832 | tf_op jit(solution)/shard_map/psum | solution.py:378
  819.2 7.4 copy-start.56
  (50 other events, 98.1 us)
Sparse Core Ops, SparseCore 0:
  53.8 49.2 all-gather.3
  105.6 46.5 all-gather.5
  259.0 61.7 reduce-scatter.23
  354.2 61.8 reduce-scatter.21
  418.2 29.3 reduce-scatter.15
  450.3 59.7 reduce-scatter.19
  512.5 110.7 reduce-scatter.17
  626.2 66.9 reduce-scatter.13
  695.5 123.6 reduce-scatter.11
  822.0 69.1 all-reduce.12
  895.1 92.6 all-reduce.14
where the time goes:
time: 1020 us; the launch traced here: 1010 us
  waiting for transfers between devices  498 us (49%)
  local copies, waits for them, and re-layouts  168 us (16%)
  matrix products  156 us (15%)
  other arithmetic  118 us (12%)
  blocking collectives  45.7 us (4%)
  between operations  18.4 us (2%)
    unnamed x163, local copies, waits for them, and re-layouts  130 us
    reduce_scatter x1, waiting for transfers between devices, body(): lax.psum_scatter(grad_mod_w.astype(jnp.bfloat16), 'batch', scatter_dimens...  126 us
    psum x1, waiting for transfers between devices, body(): lax.psum(shards[0].astype(jnp.bfloat16), ('gy', 'gx')).astype(jnp.float32)  93.3 us
    reduce_scatter x1, waiting for transfers between devices, body(): lax.psum_scatter(grad_in_w.astype(jnp.bfloat16), 'batch', scatter_dimensi...  69.9 us
    reduce_scatter x1, waiting for transfers between devices, body(): lax.psum_scatter(grad_gu_w.astype(jnp.bfloat16), 'batch', scatter_dimensi...  66.9 us
    psum x1, waiting for transfers between devices, body(): lax.psum(jnp.dot(onehot.T, grad_condition, precision=highest).astype(jnp....  60.5 us
    all_gather x1, waiting for transfers between devices, body(): lax.all_gather(key_rows, ('gy', 'gx'), axis=1, tiled=True)  42.5 us
    dot_general x1, matrix products, attend_back(): jnp.einsum('bqhd,bkhd->bhqk', grad_mixed, value_rows, preferred_element_t...  24.7 us
  transfers between devices with their start and end apart: 11, of which 8 were waited for; matrix products, arithmetic and copies ran while one was open for 27% of the time, Pallas kernels for 0%

commit v1 on v0

v1 whole, which is shorter than its diff:
```python
import functools
import math

import jax
import jax.numpy as jnp
from jax import lax
from jax.experimental import pallas as pl
from jax.experimental.pallas import tpu as pltpu
from jax.sharding import PartitionSpec as P

NORM_EPSILON = 1e-06
AXES = ("batch", "gy", "gx")
BF16 = jnp.bfloat16
F32 = jnp.float32
VMEM_LIMIT = 60 * 1024 * 1024


def mm(left, right):
    return lax.dot_general(left, right, (((1,), (0,)), ((), ())), preferred_element_type=F32)


def mm_nt(left, right):
    return lax.dot_general(left, right, (((1,), (1,)), ((), ())), preferred_element_type=F32)


def mm_tn(left, right):
    return lax.dot_general(left, right, (((0,), (0,)), ((), ())), preferred_element_type=F32)


def params():
    return pltpu.CompilerParams(vmem_limit_bytes=VMEM_LIMIT)


def full(shape):
    return pl.BlockSpec(shape, lambda *_: (0,) * len(shape))


def col_sum(values):
    return jnp.sum(values, axis=0, keepdims=True)


def modulation_kernel(act_ref, weight_ref, bias_ref, out_ref):
    out_ref[...] = mm(act_ref[...], weight_ref[...]) + bias_ref[...].astype(F32)


def modulation_call(act, weight, bias):
    rows, width = act.shape
    wide = weight.shape[1]
    return pl.pallas_call(
        modulation_kernel,
        grid=(wide // width,),
        in_specs=[
            full((rows, width)),
            pl.BlockSpec((width, width), lambda j: (0, j)),
            pl.BlockSpec((1, width), lambda j: (0, j)),
        ],
        out_specs=pl.BlockSpec((rows, width), lambda j: (0, j)),
        out_shape=jax.ShapeDtypeStruct((rows, wide), F32),
        compiler_params=params(),
        name="modulation",
    )(act, weight, bias)


def head_sum(values, head):
    width = 256
    row = lax.broadcasted_iota(jnp.int32, (width, width), 0) // head
    col = lax.broadcasted_iota(jnp.int32, (width, width), 1) // head
    ones = jnp.where(row == col, 1.0, 0.0).astype(BF16)
    parts = [
        mm(values[:, i : i + width].astype(BF16), ones) for i in range(0, values.shape[1], width)
    ]
    return jnp.concatenate(parts, axis=1)


def turn(values, cosine, sine, head):
    quarter = head // 4
    lane = lax.broadcasted_iota(jnp.int32, (1, 128), 1)
    first = (lane % (2 * quarter)) < quarter
    parts = []
    for i in range(0, values.shape[1], 128):
        part = values[:, i : i + 128]
        partner = jnp.where(
            first, pltpu.roll(part, 128 - quarter, 1), pltpu.roll(part, quarter, 1)
        )
        parts.append(part * cosine + partner * sine)
    return jnp.concatenate(parts, axis=1)


def project_kernel(
    head, x_ref, mod_ref, weight_ref, bias_ref, qgain_ref, kgain_ref, cos_ref, sin_ref,
    hid_ref, q_ref, k_ref, v_ref, raw_ref,
):
    width = x_ref.shape[1]
    x = x_ref[...].astype(F32)
    normed = x * lax.rsqrt(jnp.mean(x * x, axis=-1, keepdims=True) + NORM_EPSILON)
    hidden = (normed * (1.0 + mod_ref[:, width : 2 * width]) + mod_ref[:, :width]).astype(BF16)
    hid_ref[...] = hidden
    for part, (out_ref, gain_ref) in enumerate(((q_ref, qgain_ref), (k_ref, kgain_ref))):
        raw = mm(hidden, weight_ref[:, part * width : (part + 1) * width])
        raw = raw + bias_ref[:, part * width : (part + 1) * width].astype(F32)
        raw_ref[:, part * width : (part + 1) * width] = raw.astype(BF16)
        factor = lax.rsqrt(head_sum(raw * raw, head) * (1.0 / head) + NORM_EPSILON)
        scaled = raw * factor * gain_ref[...]
        out_ref[...] = turn(scaled, cos_ref[...], sin_ref[...], head).astype(BF16)
    value = mm(hidden, weight_ref[:, 2 * width :]) + bias_ref[:, 2 * width :].astype(F32)
    v_ref[...] = value.astype(BF16)


def project_call(x, mod, weight, bias, qgain, kgain, cosine, sine, head):
    rows, width = x.shape
    block = rows // 2
    by_row = lambda wide: pl.BlockSpec((block, wide), lambda i: (i, 0))
    shape = jax.ShapeDtypeStruct((rows, width), BF16)
    return pl.pallas_call(
        functools.partial(project_kernel, head),
        grid=(2,),
        in_specs=[
            by_row(width),
            full(mod.shape),
            full(weight.shape),
            full(bias.shape),
            full(qgain.shape),
            full(kgain.shape),
            by_row(128),
            by_row(128),
        ],
        out_specs=[by_row(width)] * 4 + [by_row(2 * width)],
        out_shape=[shape] * 4 + [jax.ShapeDtypeStruct((rows, 2 * width), BF16)],
        compiler_params=params(),
        name="project",
    )(x, mod, weight, bias, qgain, kgain, cosine, sine)


def attend_kernel(scale, q_ref, k0_ref, k1_ref, v0_ref, v1_ref, mix_ref, e_ref, rl_ref):
    lane = lax.broadcasted_iota(jnp.int32, (1, 128), 1)
    q = q_ref[...]
    keys = jnp.concatenate([k0_ref[...], k1_ref[...]], axis=0)
    values = jnp.concatenate([v0_ref[...], v1_ref[...]], axis=0)
    values = jnp.concatenate([values, jnp.ones_like(values)], axis=1)
    outs = []
    for h in range(2):
        mine = (lane >= 64) if h else (lane < 64)
        scores = mm_nt(jnp.where(mine, q, jnp.zeros_like(q)), keys)
        grown = jnp.exp(scores * scale).astype(BF16)
        e_ref[h] = grown
        outs.append(mm(grown, values))
    inverse = 1.0 / jnp.where(lane < 64, outs[0][:, 128:], outs[1][:, 128:])
    mix_ref[...] = (jnp.where(lane < 64, outs[0][:, :128], outs[1][:, :128]) * inverse).astype(BF16)
    rl_ref[...] = inverse


def attend_call(q, k0, k1, v0, v1, head):
    rows, width = q.shape
    pair = pl.BlockSpec((rows, 128), lambda p: (0, p))
    return pl.pallas_call(
        functools.partial(attend_kernel, head**-0.5),
        grid=(width // 128,),
        in_specs=[pair] * 5,
        out_specs=[pair, pl.BlockSpec((2, rows, 2 * rows), lambda p: (p, 0, 0)), pair],
        out_shape=[
            jax.ShapeDtypeStruct((rows, width), BF16),
            jax.ShapeDtypeStruct((width // head, rows, 2 * rows), BF16),
            jax.ShapeDtypeStruct((rows, width), F32),
        ],
        compiler_params=params(),
        name="attend",
    )(q, k0, k1, v0, v1)


def attend_back_kernel(
    scale, q_ref, k0_ref, k1_ref, v0_ref, v1_ref, e_ref, gm_ref, mix_ref, rl_ref,
    dq_ref, dk0_ref, dk1_ref, dv0_ref, dv1_ref,
):
    rows = q_ref.shape[0]
    lane = lax.broadcasted_iota(jnp.int32, (1, 128), 1)
    keys = jnp.concatenate([k0_ref[...], k1_ref[...]], axis=0)
    values = jnp.concatenate([v0_ref[...], v1_ref[...]], axis=0)
    scaled = gm_ref[...].astype(F32) * rl_ref[...]
    products = scaled * mix_ref[...].astype(F32)
    scaled = scaled.astype(BF16)
    q_t = q_ref[...].T
    scaled_t = scaled.T
    dqs, dks, dvs = [], [], []
    for h in range(2):
        mine = (lane >= 64) if h else (lane < 64)
        inner = jnp.sum(jnp.where(mine, products, 0.0), axis=1, keepdims=True)
        grad_probs = mm_nt(jnp.where(mine, scaled, jnp.zeros_like(scaled)), values)
        grown = e_ref[h]
        grad_scores = (grown.astype(F32) * (grad_probs - inner) * scale).astype(BF16)
        dqs.append(mm(grad_scores, keys))
        dks.append(mm(q_t[64 * h : 64 * h + 64], grad_scores))
        dvs.append(mm(scaled_t[64 * h : 64 * h + 64], grown))
    dq_ref[...] = jnp.where(lane < 64, dqs[0], dqs[1]).astype(BF16)
    dk = jnp.concatenate(dks, axis=0).T.astype(BF16)
    dv = jnp.concatenate(dvs, axis=0).T.astype(BF16)
    dk0_ref[...] = dk[:rows]
    dk1_ref[...] = dk[rows:]
    dv0_ref[...] = dv[:rows]
    dv1_ref[...] = dv[rows:]


def attend_back_call(q, k0, k1, v0, v1, grown, grad_mixed, mixed, inverse, head):
    rows, width = q.shape
    pair = pl.BlockSpec((rows, 128), lambda p: (0, p))
    return pl.pallas_call(
        functools.partial(attend_back_kernel, head**-0.5),
        grid=(width // 128,),
        in_specs=[pair] * 5
        + [pl.BlockSpec((2, rows, 2 * rows), lambda p: (p, 0, 0))]
        + [pair] * 3,
        out_specs=[pair] * 5,
        out_shape=[jax.ShapeDtypeStruct((rows, width), BF16)] * 5,
        compiler_params=params(),
        name="attend_back",
    )(q, k0, k1, v0, v1, grown, grad_mixed, mixed, inverse)


def middle_kernel(
    mix_ref, x_ref, dy_ref, mod_ref, weight_ref, bias_ref, att_ref, mid_ref, h2_ref, h2t_ref, gf_ref
):
    width = x_ref.shape[1]
    attended = mm(mix_ref[...], weight_ref[...]) + bias_ref[...].astype(F32)
    middle = x_ref[...].astype(F32) + mod_ref[:, 2 * width : 3 * width] * attended
    normed = middle * lax.rsqrt(jnp.mean(middle * middle, axis=-1, keepdims=True) + NORM_EPSILON)
    hidden = normed * (1.0 + mod_ref[:, 4 * width : 5 * width]) + mod_ref[:, 3 * width : 4 * width]
    hidden = hidden.astype(BF16)
    att_ref[...] = attended.astype(BF16)
    mid_ref[...] = middle
    h2_ref[...] = hidden
    h2t_ref[...] = hidden.T
    gf_ref[...] = (mod_ref[:, 5 * width :] * dy_ref[...].astype(F32)).astype(BF16)


def middle_call(mixed, x, dy, mod, weight, bias):
    rows, width = x.shape
    block = rows // 2
    by_row = pl.BlockSpec((block, width), lambda i: (i, 0))
    low = jax.ShapeDtypeStruct((rows, width), BF16)
    return pl.pallas_call(
        middle_kernel,
        grid=(2,),
        in_specs=[by_row] * 3 + [full(mod.shape), full(weight.shape), full(bias.shape)],
        out_specs=[by_row] * 3 + [pl.BlockSpec((width, block), lambda i: (0, i)), by_row],
        out_shape=[low, jax.ShapeDtypeStruct((rows, width), F32), low]
        + [jax.ShapeDtypeStruct((width, rows), BF16), low],
        compiler_params=params(),
        name="middle",
    )(mixed, x, dy, mod, weight, bias)


def feed_kernel(
    h2_ref, h2t_ref, gf_ref, wg_ref, wu_ref, bg_ref, bu_ref, wd_ref, feed_in_ref, gh_in_ref,
    feed_ref, gh_ref, dd_ref, dg_ref, db_ref,
):
    @pl.when(pl.program_id(0) == 0)
    def _():
        feed_ref[...] = feed_in_ref[...]
        gh_ref[...] = gh_in_ref[...]

    hidden = h2_ref[...]
    grad_feed = gf_ref[...]
    gate = mm(hidden, wg_ref[...]) + bg_ref[...].astype(F32)
    up = mm(hidden, wu_ref[...]) + bu_ref[...].astype(F32)
    grad_product = mm_nt(grad_feed, wd_ref[...])
    sig = 1.0 / (1.0 + jnp.exp(-gate))
    active = gate * sig
    product = (active * up).astype(BF16)
    grad_gate = (grad_product * up * sig * (1.0 + gate * (1.0 - sig))).astype(BF16)
    grad_up = (grad_product * active).astype(BF16)
    dd_ref[...] = mm_tn(product, grad_feed).astype(BF16)
    dg_ref[0] = mm(h2t_ref[...], grad_gate).astype(BF16)
    dg_ref[1] = mm(h2t_ref[...], grad_up).astype(BF16)
    db_ref[0] = col_sum(grad_gate.astype(F32))
    db_ref[1] = col_sum(grad_up.astype(F32))
    feed_ref[...] += mm(product, wd_ref[...])
    gh_ref[...] += mm_nt(grad_gate, wg_ref[...]) + mm_nt(grad_up, wu_ref[...])


def feed_call(hidden, hidden_t, grad_feed, weight, bias, down, feed, grad_hidden, first, step, unit):
    rows, width = hidden.shape
    blocks = down.shape[0] // unit
    steps = len(range(first, blocks, step))
    pick = lambda s: first + step * s
    acc = jax.ShapeDtypeStruct((rows, width), F32)
    return pl.pallas_call(
        feed_kernel,
        grid=(steps,),
        in_specs=[
            full((rows, width)),
            full((width, rows)),
            full((rows, width)),
            pl.BlockSpec((width, unit), lambda s: (0, pick(s))),
            pl.BlockSpec((width, unit), lambda s: (0, blocks + pick(s))),
            pl.BlockSpec((1, unit), lambda s: (0, pick(s))),
            pl.BlockSpec((1, unit), lambda s: (0, blocks + pick(s))),
            pl.BlockSpec((unit, width), lambda s: (pick(s), 0)),
            full((rows, width)),
            full((rows, width)),
        ],
        out_specs=[
            full((rows, width)),
            full((rows, width)),
            pl.BlockSpec((None, unit, width), lambda s: (s, 0, 0)),
            pl.BlockSpec((None, 2, width, unit), lambda s: (s, 0, 0, 0)),
            pl.BlockSpec((None, 2, 1, unit), lambda s: (s, 0, 0, 0)),
        ],
        out_shape=[
            acc,
            acc,
            jax.ShapeDtypeStruct((steps, unit, width), BF16),
            jax.ShapeDtypeStruct((steps, 2, width, unit), BF16),
            jax.ShapeDtypeStruct((steps, 2, 1, unit), F32),
        ],
        compiler_params=params(),
        name="feed",
    )(hidden, hidden_t, grad_feed, weight, weight, bias, bias, down, feed, grad_hidden)


def turn_kernel(
    feed_ref, gh_ref, mid_ref, att_ref, dy_ref, gf_ref, mix_ref, mod_ref, weight_ref, dbias_ref,
    out_ref, gmid_ref, gmix_ref, dw_ref, sums_ref,
):
    width = mid_ref.shape[1]
    half = width // 2
    dy = dy_ref[...].astype(F32)
    feed = feed_ref[...] + dbias_ref[...].astype(F32)
    middle = mid_ref[...]
    out_ref[...] = (middle + mod_ref[:, 5 * width :] * feed).astype(BF16)
    factor = lax.rsqrt(jnp.mean(middle * middle, axis=-1, keepdims=True) + NORM_EPSILON)
    normed = middle * factor
    grad_hidden = gh_ref[...]
    product = grad_hidden * normed
    grad_normed = grad_hidden * (1.0 + mod_ref[:, 4 * width : 5 * width])
    back = factor * (
        grad_normed - normed * jnp.mean(grad_normed * normed, axis=-1, keepdims=True)
    )
    grad_middle = dy + back
    gmid_ref[...] = grad_middle
    grad_attended = (mod_ref[:, 2 * width : 3 * width] * grad_middle).astype(BF16)
    sums_ref[0:1, :] = col_sum(grad_middle * att_ref[...].astype(F32))
    sums_ref[1:2, :] = col_sum(grad_hidden)
    sums_ref[2:3, :] = col_sum(product)
    sums_ref[3:4, :] = col_sum(dy * feed)
    sums_ref[4:5, :] = col_sum(grad_attended.astype(F32))
    sums_ref[5:6, :] = col_sum(gf_ref[...].astype(F32))
    sums_ref[6:8, :] = jnp.zeros((2, width), F32)
    gmix_ref[...] = mm_nt(grad_attended, weight_ref[...]).astype(BF16)
    mixed_t = mix_ref[...].T
    dw_ref[0] = mm(mixed_t, grad_attended[:, :half]).astype(BF16)
    dw_ref[1] = mm(mixed_t, grad_attended[:, half:]).astype(BF16)


def turn_call(feed, grad_hidden, middle, attended, dy, grad_feed, mixed, mod, weight, down_bias):
    rows, width = middle.shape
    low = jax.ShapeDtypeStruct((rows, width), BF16)
    return pl.pallas_call(
        turn_kernel,
        out_shape=[
            low,
            jax.ShapeDtypeStruct((rows, width), F32),
            low,
            jax.ShapeDtypeStruct((2, width, width // 2), BF16),
            jax.ShapeDtypeStruct((8, width), F32),
        ],
        compiler_params=params(),
        name="turn",
    )(feed, grad_hidden, middle, attended, dy, grad_feed, mixed, mod, weight, down_bias)


def project_back_kernel(
    head, dq_ref, dk0_ref, dk1_ref, dv0_ref, dv1_ref, raw_ref, hid_ref, x_ref, gmid_ref, mod_ref,
    weight_ref, qgain_ref, kgain_ref, cos_ref, sin_ref,
    gx_ref, dw_ref, sums_ref, bias_ref, proj_ref,
):
    width = x_ref.shape[1]
    cosine, sine = cos_ref[...], -sin_ref[...]
    for part in range(3):
        span = slice(part * width, (part + 1) * width)
        if part == 2:
            grad = dv0_ref[...].astype(F32) + dv1_ref[...].astype(F32)
        else:
            grad = dq_ref[...].astype(F32)
            if part == 1:
                grad = dk0_ref[...].astype(F32) + dk1_ref[...].astype(F32)
            gain = (qgain_ref, kgain_ref)[part][...]
            raw = raw_ref[:, span].astype(F32)
            factor = lax.rsqrt(head_sum(raw * raw, head) * (1.0 / head) + NORM_EPSILON)
            normed = raw * factor
            turned = turn(grad, cosine, sine, head)
            sums_ref[2 + part : 3 + part, :] = col_sum(turned * normed)
            turned = turned * gain
            mean = head_sum(turned * normed, head) * (1.0 / head)
            grad = factor * (turned - normed * mean)
        low = grad.astype(BF16)
        proj_ref[:, span] = low
        bias_ref[:, span] = col_sum(low.astype(F32))
    hidden_t = hid_ref[...].T
    half = 3 * width // 2
    dw_ref[0] = mm(hidden_t, proj_ref[:, :half]).astype(BF16)
    dw_ref[1] = mm(hidden_t, proj_ref[:, half:]).astype(BF16)
    grad_hidden = mm_nt(proj_ref[...], weight_ref[...])
    x = x_ref[...].astype(F32)
    factor = lax.rsqrt(jnp.mean(x * x, axis=-1, keepdims=True) + NORM_EPSILON)
    normed = x * factor
    sums_ref[0:1, :] = col_sum(grad_hidden)
    sums_ref[1:2, :] = col_sum(grad_hidden * normed)
    sums_ref[4:8, :] = jnp.zeros((4, width), F32)
    grad_normed = grad_hidden * (1.0 + mod_ref[:, width : 2 * width])
    back = factor * (
        grad_normed - normed * jnp.mean(grad_normed * normed, axis=-1, keepdims=True)
    )
    gx_ref[...] = (gmid_ref[...] + back).astype(BF16)


def project_back_call(
    dq, dk0, dk1, dv0, dv1, raw, hidden, x, grad_middle, mod, weight, qgain, kgain, cosine, sine, head
):
    rows, width = x.shape
    return pl.pallas_call(
        functools.partial(project_back_kernel, head),
        out_shape=[
            jax.ShapeDtypeStruct((rows, width), BF16),
            jax.ShapeDtypeStruct((2, width, 3 * width // 2), BF16),
            jax.ShapeDtypeStruct((8, width), F32),
            jax.ShapeDtypeStruct((1, 3 * width), F32),
        ],
        scratch_shapes=[pltpu.VMEM((rows, 3 * width), BF16)],
        compiler_params=params(),
        name="project_back",
    )(dq, dk0, dk1, dv0, dv1, raw, hidden, x, grad_middle, mod, weight, qgain, kgain, cosine, sine)


def take(array_in, index, axis=0):
    return lax.dynamic_index_in_dim(array_in, index, axis, keepdims=False)


def add(*terms):
    return sum(term.astype(F32) for term in terms)


class Moves:
    def __init__(self, mesh):
        self.sizes = tuple(mesh.shape[name] for name in AXES)

    def flip(self, value, batch=0, gy=0, gx=0):
        nb, ny, nx = self.sizes
        pairs = []
        for b in range(nb):
            for y in range(ny):
                for x in range(nx):
                    here = (b * ny + y) * nx + x
                    there = ((b ^ batch) * ny + (y ^ gy)) * nx + (x ^ gx)
                    pairs.append((here, there))
        return lax.ppermute(value, AXES, pairs)

    def plane(self, value, k):
        return self.flip(value, gy=k >> 1, gx=2 * (k & 1))

    def pair(self, value):
        return self.flip(value, gx=1)

    def gather(self, value):
        value = value[None]
        value = jnp.concatenate([value, self.plane(value, 1)], axis=0)
        value = jnp.concatenate([value, self.plane(value, 2)], axis=0)
        bit = 1
        while bit < self.sizes[0]:
            value = jnp.concatenate([value, self.flip(value, batch=bit)], axis=0)
            bit *= 2
        return value


def regroup(parts, place):
    stacked = jnp.stack(parts)
    return jnp.stack([take(stacked, place ^ k) for k in range(len(parts))])


def reduce_pieces(moves, pieces, c, first, second, order, z):
    one, two = order
    arrived = moves.pair(take(pieces, 1 - c))
    mine = take(pieces, c)
    near = moves.plane(add(take(mine, 1 - first), take(arrived, 1 - first)).astype(BF16), one)
    mine, arrived = take(mine, first), take(arrived, first)
    far = moves.plane(
        add(take(mine, 1 - second), take(arrived, 1 - second), take(near, 1 - second)).astype(BF16),
        two,
    )
    total = add(take(mine, second), take(arrived, second), take(near, second), far)
    low = total.astype(BF16)
    own = take(total, z)
    for d in range(1, moves.sizes[0]):
        own = add(own, moves.flip(take(low, z ^ d), batch=d))
    own = own.astype(BF16)
    quarter = [own, moves.plane(own, two), moves.plane(own, one), moves.plane(own, one ^ two)]
    quarter = regroup(quarter, 2 * first + second)
    halves = [quarter, moves.pair(quarter)]
    return regroup(halves, c)


def body(mesh, *operands):
    (
        tokens, timesteps, labels, class_table, modulate_weight, modulate_bias, inproj_weight,
        inproj_bias, query_gain, key_gain, outproj_weight, outproj_bias, gate_up_weight,
        gate_up_bias, down_weight, down_bias, cotangent,
    ) = operands
    image_count, tile_rows, tile_cols, width = tokens.shape
    cells = tile_rows * tile_cols
    rows = image_count * cells
    head = query_gain.shape[0]
    heads = width // head
    hidden_width = down_weight.shape[0]
    class_count = class_table.shape[0]
    highest = lax.Precision.HIGHEST
    moves = Moves(mesh)
    nb, ny, nx = moves.sizes
    assert ny == 2 and nx == 4 and image_count == 4
    z, gy, gx = (lax.axis_index(name) for name in AXES)
    side, core = gx // 2, gx % 2
    place = 2 * gy + side

    tiles = tokens.reshape(image_count, cells, width)
    grads = cotangent.reshape(image_count, cells, width)

    def exchange(blocks):
        return [take(blocks, place)] + [
            moves.plane(take(blocks, place ^ k), k) for k in range(1, 4)
        ]

    x = jnp.concatenate(exchange(tiles), axis=0)

    half_width = width // 2
    step = take(timesteps, place).astype(F32)
    label = take(labels, place)
    rates = jnp.exp(-math.log(10000.0) * jnp.arange(half_width, dtype=F32) / half_width)
    features = jnp.concatenate([jnp.cos(step * rates), jnp.sin(step * rates)])
    condition = features + take(class_table, label).astype(F32)
    cond_act = jax.nn.silu(condition).astype(BF16)
    mod = modulation_call(
        jnp.broadcast_to(cond_act[None], (16, width)), modulate_weight, modulate_bias[None]
    )[:1]

    quarter = head // 4
    cell = jnp.arange(cells, dtype=jnp.int32)
    row_places, col_places = [], []
    for k in range(4):
        there = place ^ k
        row_places.append((there // 2) * tile_rows + cell // tile_cols)
        col_places.append((2 * (there % 2) + core) * tile_cols + cell % tile_cols)
    row_places = jnp.concatenate(row_places).astype(F32)[:, None]
    col_places = jnp.concatenate(col_places).astype(F32)[:, None]
    lane = jnp.arange(128, dtype=jnp.int32)
    turn_rate = jnp.exp(-math.log(10000.0) * (lane % quarter).astype(F32) / quarter)[None]
    angles = jnp.where((lane % head)[None] < head // 2, row_places, col_places) * turn_rate
    cosine = jnp.cos(angles)
    sine = jnp.where((lane % (2 * quarter))[None] < quarter, -1.0, 1.0) * jnp.sin(angles)
    qgain = jnp.tile(query_gain.astype(F32), heads)[None]
    kgain = jnp.tile(key_gain.astype(F32), heads)[None]

    hidden_one, q, k0, v0, raw = project_call(
        x, mod, inproj_weight, inproj_bias[None], qgain, kgain, cosine, sine, head
    )
    k1, v1 = moves.pair(k0), moves.pair(v0)
    dy = jnp.concatenate(exchange(grads), axis=0)
    mixed, grown, inverse = attend_call(q, k0, k1, v0, v1, head)
    attended, middle, hidden_two, hidden_two_t, grad_feed = middle_call(
        mixed, x, dy, mod, outproj_weight, outproj_bias[None]
    )

    unit = 256
    blocks = hidden_width // unit
    quick = nb == 4
    chunks = 2 if quick else 1
    feed = jnp.zeros((rows, width), F32)
    grad_hidden = jnp.zeros((rows, width), F32)
    down_parts, gate_parts, gate_bias_parts = [], [], []
    for j in range(chunks):
        feed, grad_hidden, d_down, d_gate, d_bias = feed_call(
            hidden_two, hidden_two_t, grad_feed, gate_up_weight, gate_up_bias[None], down_weight,
            feed, grad_hidden, j, chunks, unit,
        )
        down_parts.append(d_down)
        gate_parts.append(d_gate)
        gate_bias_parts.append(d_bias)

    output_rows, grad_middle, grad_mixed, d_out, sums_two = turn_call(
        feed, grad_hidden, middle, attended, dy, grad_feed, mixed, mod, outproj_weight,
        down_bias[None],
    )
    dq, dk0, dk1, dv0, dv1 = attend_back_call(
        q, k0, k1, v0, v1, grown, grad_mixed, mixed, inverse, head
    )
    dk1, dv1 = moves.pair(dk1), moves.pair(dv1)
    grad_x, d_in, sums_one, in_bias = project_back_call(
        dq, dk0, dk1, dv0, dv1, raw, hidden_one, x, grad_middle, mod, inproj_weight, qgain, kgain,
        cosine, sine, head,
    )

    def give_back(rows_out):
        parts = rows_out.reshape(4, cells, width)
        got = [parts[0]] + [moves.plane(parts[k], k) for k in range(1, 4)]
        return regroup(got, place).reshape(tokens.shape)

    output = give_back(output_rows)
    grad_tokens = give_back(grad_x)

    slice_rows = width // nb
    if quick:
        downs, gates = [], []
        for j in range(chunks):
            order = (1, 2) if j % 2 == 0 else (2, 1)
            first, second = (side, gy) if j % 2 == 0 else (gy, side)
            d = down_parts[j].reshape(nb, 2, 2, 2, unit // 8, width).transpose(1, 2, 3, 0, 4, 5)
            g = gate_parts[j].reshape(2, 2, 2, nb, slice_rows, unit)
            d = reduce_pieces(moves, d, core, first, second, order, z)
            g = reduce_pieces(moves, g, core, first, second, order, z)
            downs.append(d.reshape(unit, width))
            gates.append(g.reshape(blocks // chunks, 2, slice_rows, unit))
        grad_down_w = jnp.stack(downs).reshape(hidden_width // nb, width).astype(F32)
        grad_gu_w = jnp.stack(gates, axis=1).reshape(blocks, 2, slice_rows, unit)
        grad_gu_w = grad_gu_w.transpose(2, 1, 0, 3).reshape(slice_rows, 2 * hidden_width).astype(F32)

        def by_rows(d, order, first, second):
            wide = d.shape[2]
            d = d.reshape(2, nb, 2, 2, slice_rows // 4, wide).transpose(0, 2, 3, 1, 4, 5)
            d = reduce_pieces(moves, d, core, first, second, order, z)
            d = d.reshape(2, slice_rows, wide)
            return jnp.concatenate([d[0], d[1]], axis=1).astype(F32)

        grad_out_w = by_rows(d_out, (1, 2), side, gy)
        grad_in_w = by_rows(d_in, (2, 1), gy, side)
    else:

        def scatter(d):
            d = lax.psum_scatter(d.astype(BF16), "batch", scatter_dimension=0, tiled=True)
            return lax.psum(d, ("gy", "gx")).astype(F32)

        def joined(d):
            return jnp.concatenate([d[0], d[1]], axis=1)

        grad_down_w = scatter(down_parts[0].reshape(hidden_width, width))
        grad_gu_w = scatter(
            gate_parts[0].transpose(2, 1, 0, 3).reshape(width, 2 * hidden_width)
        )
        grad_out_w = scatter(joined(d_out))
        grad_in_w = scatter(joined(d_in))

    gate_bias = jnp.stack(gate_bias_parts, axis=1).reshape(blocks, 2, unit).transpose(1, 0, 2)
    gain_sums = sums_one[2:4].reshape(2, heads, head).sum(axis=1)
    early = jnp.concatenate([sums_two[:6].reshape(-1), gate_bias.reshape(-1)])
    late = jnp.concatenate([sums_one[:2].reshape(-1), in_bias.reshape(-1), gain_sums.reshape(-1)])

    def everywhere(vector):
        halves = vector.reshape(2, -1)
        half = add(take(halves, core), moves.pair(take(halves, 1 - core)))
        half = moves.gather(half)
        both = regroup([half, moves.pair(half)], core)
        return both.transpose(1, 0, 2).reshape(half.shape[0], -1)

    known = jnp.concatenate([condition, jnp.broadcast_to(label.astype(F32), (128,))])
    known = moves.gather(known)
    early = everywhere(early)
    late = everywhere(late)
    grad_modulation = jnp.concatenate([late[:, : 2 * width], early[:, : 4 * width]], axis=1)
    conditions = known[:, :width]
    all_labels = known[:, width].astype(jnp.int32)
    cond_acts = jax.nn.silu(conditions).astype(BF16)
    my_acts = lax.dynamic_slice_in_dim(cond_acts, z * slice_rows, slice_rows, axis=1)
    low_mod = grad_modulation.astype(BF16)
    grad_mod_w = mm_tn(my_acts, low_mod)
    wide = 6 * width
    grad_mod_b = lax.dynamic_slice_in_dim(
        jnp.sum(grad_modulation, axis=0), z * (wide // nb), wide // nb, axis=0
    )
    grad_cond_act = mm_nt(low_mod, modulate_weight)
    sig = jax.nn.sigmoid(conditions)
    grad_conditions = grad_cond_act * sig * (1.0 + conditions * (1.0 - sig))
    grad_condition = regroup([grad_conditions[k] for k in range(4)], place)
    onehot = (all_labels[:, None] == jnp.arange(class_count, dtype=jnp.int32)[None, :]).astype(F32)
    grad_table = lax.dot_general(
        onehot, grad_conditions, (((0,), (0,)), ((), ())), precision=highest,
        preferred_element_type=F32,
    )

    early_sum = jnp.sum(early, axis=0)
    late_sum = jnp.sum(late, axis=0)

    def part(vector, start, size):
        return lax.dynamic_slice_in_dim(vector, start + z * (size // nb), size // nb, axis=0)

    grad_out_b = part(early_sum, 4 * width, width)
    grad_down_b = part(early_sum, 5 * width, width)
    grad_gu_b = part(early_sum, 6 * width, 2 * hidden_width)
    grad_in_b = part(late_sum, 2 * width, 3 * width)
    grad_q_gain = part(late_sum, 5 * width, head)
    grad_k_gain = part(late_sum, 5 * width + head, head)
    return (
        output, grad_tokens, grad_condition, grad_table, grad_mod_w, grad_mod_b, grad_in_w,
        grad_in_b, grad_q_gain, grad_k_gain, grad_out_w, grad_out_b, grad_gu_w, grad_gu_b,
        grad_down_w, grad_down_b,
    )


def solution(mesh):
    grid = P("batch", "gy", "gx", None)
    by_batch = P("batch")
    rows = P("batch", None)
    placed = (grid, by_batch, by_batch) + (P(),) * 13 + (grid,)
    return jax.shard_map(
        functools.partial(body, mesh),
        mesh=mesh,
        in_specs=placed,
        out_specs=(
            grid, grid, rows, P(), rows, by_batch, rows, by_batch, by_batch, by_batch, rows,
            by_batch, rows, by_batch, rows, by_batch,
        ),
        check_vma=False,
    )
```

time: 1020 us -> 403 us (0.40); the launches traced: 1010 us -> 399 us
  waiting for transfers between devices: 498 us -> 84.9 us
  matrix products: 156 us -> 11.4 us
  local copies, waits for them, and re-layouts: 168 us -> 48.8 us
  Pallas kernels: 0 us -> 107 us
  starting transfers between devices: 0.92 us -> 97.5 us
  other arithmetic: 118 us -> 44.4 us
  blocking collectives: 45.7 us -> 0 us
  between operations: 18.4 us -> 5.32 us
    reduce_scatter x5 -> x0, waiting for transfers between devices: 263 us -> none  [the longest x1 126 us: body(): lax.psum_scatter(grad_mod_w.astype(jnp.bfloat16), 'batch', scatter_dimens...]
    psum x2 -> x0, waiting for transfers between devices: 154 us -> none  [the longest x1 93.3 us: body(): lax.psum(shards[0].astype(jnp.bfloat16), ('gy', 'gx')).astype(jnp.float32)]
    dot_general x22 -> x3, matrix products: 156 us -> 11.4 us  [the longest x1 4.95 us: mm_nt(): lax.dot_general(left, right, (((1,), (1,)), ((), ())), preferred_element_...]
    unnamed x163 -> x58, local copies, waits for them, and re-layouts: 130 us -> 7 us
    pallas_call x0 -> x9, Pallas kernels: none -> 107 us  [the longest x2 41.5 us: feed_call(): pl.pallas_call(feed_kernel, grid=(steps,), in_specs=[full((rows, width)),...]
    ppermute x0 -> x92, starting transfers between devices: none -> 97.5 us  [flip(): return lax.ppermute(value, AXES, pairs)]
    ppermute x0 -> x92, waiting for transfers between devices: none -> 84.9 us  [flip(): return lax.ppermute(value, AXES, pairs)]
    all_gather x2 -> x0, waiting for transfers between devices: 64.2 us -> none  [the longest x1 42.5 us: body(): lax.all_gather(key_rows, ('gy', 'gx'), axis=1, tiled=True)]
  transfers between devices with their start and end apart: 11 -> 92, of which waited for: 8 -> 40; matrix products, arithmetic and copies ran while one was open for 27% -> 24% of each run, Pallas kernels for 0% -> 10%
where the time goes in v1:
time: 403 us; the launch traced here: 399 us
  Pallas kernels  107 us (27%)
  starting transfers between devices  97.5 us (24%)
  waiting for transfers between devices  84.9 us (21%)
  local copies, waits for them, and re-layouts  48.8 us (12%)
  other arithmetic  44.4 us (11%)
  matrix products  11.4 us (3%)
  between operations  5.32 us (1%)
    ppermute x92, starting transfers between devices, flip(): return lax.ppermute(value, AXES, pairs)  97.5 us
    ppermute x92, waiting for transfers between devices, flip(): return lax.ppermute(value, AXES, pairs)  84.9 us
    pallas_call x2, Pallas kernels, feed_call(): pl.pallas_call(feed_kernel, grid=(steps,), in_specs=[full((rows, width)),...  41.5 us
    pallas_call x1, Pallas kernels, attend_back_call(): pl.pallas_call(functools.partial(attend_back_kernel, head ** (-0.5)), gri...  15.9 us
    pallas_call x1, Pallas kernels, project_back_call(): pl.pallas_call(functools.partial(project_back_kernel, head), out_shape=[j...  12.7 us
    pallas_call x1, Pallas kernels, attend_call(): pl.pallas_call(functools.partial(attend_kernel, head ** (-0.5)), grid=(wi...  12 us
    squeeze x14, local copies, waits for them, and re-layouts, take(): return lax.dynamic_index_in_dim(array_in, index, axis, keepdims=False)  11.5 us
  transfers between devices with their start and end apart: 92, of which 40 were waited for; matrix products, arithmetic and copies ran while one was open for 24% of the time, Pallas kernels for 10%

profile of v1, /device:TPU:0, one launch (start us, length us, event | category | flops | bytes accessed | tf_op | source)
XLA Modules:
  0.0 399.5 jit_solution(147813477203215700)
XLA Ops:
  7.3 3.1 collective-permute-start.28
  21.3 6.5 %modulation.1 = f32[16,4608]{1,0:T(8,128)} custom-call(bf16[16,768]{1,0:T(8,128)(2,1)} %broadcast_in_dim.74.act_ref, bf16[768,4608]{1,0:T(8,128)(2,1)} %weight_ref.5, bf16[1,4608]{1,0:T(2,128)(2,1)} %broadcast_in_dim.75.bias_ref), custom_call_target="tpu_custom_call" | custom-call | tf_op jit(solution)/shard_map/modulation/pallas_call | solution.py:49
  31.8 6.5 %project.1 = (bf16[512,768]{1,0:T(8,128)(2,1)}, bf16[512,768]{1,0:T(8,128)(2,1)}, bf16[512,768]{1,0:T(8,128)(2,1)}, bf16[512,768]{1,0:T(8,128)(2,1)}, bf16[512,1536]{1,0:T(8,128)(2,1)}) custom-call(bf16[512,768]{1,0:T(8,128)(2,1)} %pad_maximum_fusion.x_ref, f32[1,4608]{1,0:T(1,128)} %slice.94.mod_ref, bf16[768,2304]{1,0:T(8,128)(2,1)} %weight_ref.9, ...), custom_call_target="tpu_custom_call" | custom-call | tf_op jit(solution)/shard_map/project/pallas_call | solution.py:114
  42.8 2.6 collective-permute-start.31
  58.5 12.0 %attend.1 = (bf16[512,768]{1,0:T(8,128)(2,1)}, bf16[12,512,1024]{2,1,0:T(8,128)(2,1)}, f32[512,768]{1,0:T(8,128)}) custom-call(bf16[512,768]{1,0:T(8,128)(2,1)} %get-tuple-element.53.q_ref, bf16[512,768]{1,0:T(8,128)(2,1)} %get-tuple-element.54.k0_ref, bf16[512,768]{1,0:T(8,128)(2,1)} %copy-done.1, bf16[512,768]{1,0:T(8,128)(2,1)} %get-tuple-element.55.v0_ref, ...), custom_call_target="tpu_custom_call" | custom-call | tf_op jit(solution)/shard_map/attend/pallas_call | solution.py:155
  70.5 4.4 %middle.1 = (bf16[512,768]{1,0:T(8,128)(2,1)}, f32[512,768]{1,0:T(8,128)}, bf16[512,768]{1,0:T(8,128)(2,1)}, bf16[768,512]{1,0:T(8,128)(2,1)}, bf16[512,768]{1,0:T(8,128)(2,1)}) custom-call(bf16[512,768]{1,0:T(8,128)(2,1)} %get-tuple-element.56.mix_ref, bf16[512,768]{1,0:T(8,128)(2,1)} %pad_maximum_fusion.x_ref, bf16[512,768]{1,0:T(8,128)(2,1)} %pad_maximum_fusion.1.dy_ref, ...), custom_call_target="tpu_custom_call" | custom-call | tf_op jit(solution)/shard_map/middle/pallas_call | solution.py:239
  76.2 14.6 %feed.2 = (f32[512,768]{1,0:T(8,128)}, f32[512,768]{1,0:T(8,128)}, bf16[4,256,768]{2,1,0:T(8,128)(2,1)}, bf16[4,2,768,256]{3,2,1,0:T(8,128)(2,1)}, f32[4,2,1,256]{3,2,1,0:T(1,128)}) custom-call(bf16[512,768]{1,0:T(8,128)(2,1)} %get-tuple-element.57.h2_ref, bf16[768,512]{1,0:T(8,128)(2,1)} %get-tuple-element.58.h2t_ref, ...), custom_call_target="tpu_custom_call" | custom-call | tf_op jit(solution)/shard_map/feed/pallas_call | solution.py:285
  90.8 27.0 %feed.3 = (f32[512,768]{1,0:T(8,128)}, f32[512,768]{1,0:T(8,128)}, bf16[4,256,768]{2,1,0:T(8,128)(2,1)}, bf16[4,2,768,256]{3,2,1,0:T(8,128)(2,1)}, f32[4,2,1,256]{3,2,1,0:T(1,128)}) custom-call(bf16[512,768]{1,0:T(8,128)(2,1)} %get-tuple-element.57.h2_ref, bf16[768,512]{1,0:T(8,128)(2,1)} %get-tuple-element.58.h2t_ref, ...), custom_call_target="tpu_custom_call" | custom-call | tf_op jit(solution)/shard_map/feed/pallas_call | solution.py:285
  118.5 7.6 %turn.1 = (bf16[512,768]{1,0:T(8,128)(2,1)}, f32[512,768]{1,0:T(8,128)}, bf16[512,768]{1,0:T(8,128)(2,1)}, bf16[2,768,384]{2,1,0:T(8,128)(2,1)}, f32[8,768]{1,0:T(8,128)}) custom-call(f32[512,768]{1,0:T(8,128)} %get-tuple-element.62.feed_ref, f32[512,768]{1,0:T(8,128)} %get-tuple-element.63.gh_ref, f32[512,768]{1,0:T(8,128)} %get-tuple-element.64.mid_ref, ...), custom_call_target="tpu_custom_call" | custom-call | tf_op jit(solution)/shard_map/turn/pallas_call | solution.py:356
  143.8 15.9 %attend_back.1 = (bf16[512,768]{1,0:T(8,128)(2,1)}, bf16[512,768]{1,0:T(8,128)(2,1)}, bf16[512,768]{1,0:T(8,128)(2,1)}, bf16[512,768]{1,0:T(8,128)(2,1)}, bf16[512,768]{1,0:T(8,128)(2,1)}) custom-call(bf16[512,768]{1,0:T(8,128)(2,1)} %get-tuple-element.53.q_ref, bf16[512,768]{1,0:T(8,128)(2,1)} %get-tuple-element.54.k0_ref, bf16[512,768]{1,0:T(8,128)(2,1)} %copy-done.1, ...), custom_call_target="tpu_custom_call" | custom-call | tf_op jit(solution)/shard_map/attend_back/pallas_call | solution.py:205
  175.3 12.7 %project_back.1 = (bf16[512,768]{1,0:T(8,128)(2,1)}, bf16[2,768,1152]{2,1,0:T(8,128)(2,1)}, f32[8,768]{1,0:T(8,128)}, f32[1,2304]{1,0:T(1,128)}) custom-call(bf16[512,768]{1,0:T(8,128)(2,1)} %get-tuple-element.70.dq_ref, bf16[512,768]{1,0:T(8,128)(2,1)} %get-tuple-element.71.dk0_ref, bf16[512,768]{1,0:T(8,128)(2,1)} %collective-permute-done.11.dk1_ref, ...), custom_call_target="tpu_custom_call" | custom-call | tf_op jit(solution)/shard_map/project_back/pallas_call | solution.py:419
  190.0 2.9 copy_bitcast_fusion
  201.4 2.6 collective-permute-done.18
  210.9 3.0 collective-permute-start.20
  217.8 2.9 concatenate.98
  231.4 2.8 collective-permute-start.47
  239.5 4.9 %add_multiply_fusion = f32[16,768]{1,0:T(8,128)S(1)} fusion(bf16[768,4608]{1,0:T(8,128)(2,1)} %weight_ref.5, f32[16,3072]{1,0:T(8,128)S(1)} %slice.96, f32[16,1536]{1,0:T(8,128)S(1)} %slice.95, f32[16,896]{1,0:T(8,128)S(1)} %copy-done.12), kind=kOutput, calls=%fused_computation.193 | convolution fusion | flops 113639424 | bytes 7471104 | tf_op jit(solution)/shard_map/dot_general | solution.py:23
  244.5 3.1 fusion.55
  247.7 3.3 fusion.60
  261.9 8.6 %collective-permute-done.83 = bf16[2,4,32,768]{3,2,1,0:T(8,128)(2,1)S(1)} collective-permute-done((bf16[2,4,32,768]{3,2,1,0:T(8,128)(2,1)}, bf16[2,4,32,768]{3,2,1,0:T(8,128)(2,1)S(1)}, u32[]{:S(2)}, u32[]{:S(2)}) %collective-permute-start.83) | collective-permute-done | bytes 393248 | tf_op jit(solution)/shard_map/ppermute | solution.py:454
  276.6 2.8 collective-permute-start.77
  282.7 2.8 collective-permute-start.87
  298.8 2.9 collective-permute-done.88
  306.1 14.2 %collective-permute-done.53 = bf16[2,4,192,256]{3,2,1,0:T(8,128)(2,1)S(1)} collective-permute-done((bf16[2,4,192,256]{3,2,1,0:T(8,128)(2,1)S(1)}, bf16[2,4,192,256]{3,2,1,0:T(8,128)(2,1)S(1)}, u32[]{:S(2)}, u32[]{:S(2)}) %collective-permute-start.53) | collective-permute-done | bytes 786464 | tf_op jit(solution)/shard_map/ppermute | solution.py:454
  327.3 6.2 %collective-permute-done.54 = bf16[4,192,256]{2,1,0:T(8,128)(2,1)S(1)} collective-permute-done((bf16[4,192,256]{2,1,0:T(8,128)(2,1)S(1)}, bf16[4,192,256]{2,1,0:T(8,128)(2,1)S(1)}, u32[]{:S(2)}, u32[]{:S(2)}) %collective-permute-start.54) | collective-permute-done | bytes 393248 | tf_op jit(solution)/shard_map/ppermute | solution.py:454
  341.3 4.1 %collective-permute-start.67 = (bf16[192,256]{1,0:T(8,128)(2,1)S(1)}, bf16[192,256]{1,0:T(8,128)(2,1)S(1)}, u32[]{:S(2)}, u32[]{:S(2)}) collective-permute-start(bf16[192,256]{1,0:T(8,128)(2,1)S(1)} %get-tuple-element.169), channel_id=1, source_target_pairs={{0,24},{1,25},{2,26},{3,27},{4,28},{5,29},{6,30},{7,31},{8,16},{9,... | collective-permute-start | bytes 294920 | tf_op jit(solution)/shard_map/ppermute | solution.py:454
  345.4 2.9 collective-permute-start.66
  348.3 3.4 collective-permute-done.56
  362.5 3.0 collective-permute-done.68
  365.8 6.3 %collective-permute-done.34 = bf16[4,48,1152]{2,1,0:T(8,128)(2,1)S(1)} collective-permute-done((bf16[4,48,1152]{2,1,0:T(8,128)(2,1)S(1)}, bf16[4,48,1152]{2,1,0:T(8,128)(2,1)S(1)}, u32[]{:S(2)}, u32[]{:S(2)}) %collective-permute-start.34) | collective-permute-done | bytes 442400 | tf_op jit(solution)/shard_map/ppermute | solution.py:454
  379.2 3.6 collective-permute-done.36
  393.2 4.4 %copy.108 = f32[24,8,16,256]{3,1,2,0:T(8,128)} copy(f32[24,8,16,256]{3,2,1,0:T(8,128)S(1)} %bitcast.401) | data formatting | bytes 6291456
  (392 shorter events, 190.6 us)
Async XLA Ops:
  7.3 22.0 %collective-permute-start.28 = (f32[1,896]{1,0:T(1,128)S(1)}, f32[1,896]{1,0:T(1,128)S(1)}, u32[]{:S(2)}, u32[]{:S(2)}) collective-permute-start(f32[1,896]{1,0:T(1,128)S(1)} %broadcast_in_dim.87), channel_id=1, source_target_pairs={{0,2},{1,3},{2,0},{3,1},{4,6},{5,7},{6,4},{7,5},{8,10},{9,11},{10,... | collective-permute-start | bytes 10760 | tf_op jit(solution)/shard_map/ppermute | solution.py:454
  11.6 19.2 %collective-permute-start.2 = (bf16[128,768]{1,0:T(8,128)(2,1)S(1)}, bf16[128,768]{1,0:T(8,128)(2,1)S(1)}, u32[]{:S(2)}, u32[]{:S(2)}) collective-permute-start(bf16[128,768]{1,0:T(8,128)(2,1)S(1)} %get-tuple-element.135), channel_id=1, source_target_pairs={{0,6},{1,7},{2,4},{3,5},{4,2},{5,3},{6,0},{7,1},{8,14},{9,15},{10,... | collective-permute-start | bytes 589832 | tf_op jit(solution)/shard_map/ppermute | solution.py:454
  13.1 17.7 %collective-permute-start.1 = (bf16[128,768]{1,0:T(8,128)(2,1)S(1)}, bf16[128,768]{1,0:T(8,128)(2,1)S(1)}, u32[]{:S(2)}, u32[]{:S(2)}) collective-permute-start(bf16[128,768]{1,0:T(8,128)(2,1)S(1)} %get-tuple-element.136), channel_id=1, source_target_pairs={{0,4},{1,5},{2,6},{3,7},{4,0},{5,1},{6,2},{7,3},{8,12},{9,13},{10,... | collective-permute-start | bytes 589832 | tf_op jit(solution)/shard_map/ppermute | solution.py:454
  13.2 17.6 %collective-permute-start = (bf16[128,768]{1,0:T(8,128)(2,1)S(1)}, bf16[128,768]{1,0:T(8,128)(2,1)S(1)}, u32[]{:S(2)}, u32[]{:S(2)}) collective-permute-start(bf16[128,768]{1,0:T(8,128)(2,1)S(1)} %get-tuple-element.137), channel_id=1, source_target_pairs={{0,2},{1,3},{2,0},{3,1},{4,6},{5,7},{6,4},{7,5},{8,10},{9,11},{10,... | collective-permute-start | bytes 589832 | tf_op jit(solution)/shard_map/ppermute | solution.py:454
  38.4 19.0 %collective-permute-start.3 = (bf16[512,768]{1,0:T(8,128)(2,1)}, bf16[512,768]{1,0:T(8,128)(2,1)S(1)}, u32[]{:S(2)}, u32[]{:S(2)}) collective-permute-start(bf16[512,768]{1,0:T(8,128)(2,1)} %get-tuple-element.54.k0_ref), channel_id=1, source_target_pairs={{0,1},{1,0},{2,3},{3,2},{4,5},{5,4},{6,7},{7,6},{8,9},{9,8},{10,11... | collective-permute-start | bytes 2359304 | tf_op jit(solution)/shard_map/ppermute | solution.py:454
  38.4 18.9 %collective-permute-start.4 = (bf16[512,768]{1,0:T(8,128)(2,1)}, bf16[512,768]{1,0:T(8,128)(2,1)S(1)}, u32[]{:S(2)}, u32[]{:S(2)}) collective-permute-start(bf16[512,768]{1,0:T(8,128)(2,1)} %get-tuple-element.55.v0_ref), channel_id=1, source_target_pairs={{0,1},{1,0},{2,3},{3,2},{4,5},{5,4},{6,7},{7,6},{8,9},{9,8},{10,11... | collective-permute-start | bytes 2359304 | tf_op jit(solution)/shard_map/ppermute | solution.py:454
  128.2 70.6 %collective-permute-start.72 = (bf16[2,2,4,32,768]{4,3,2,1,0:T(8,128)(2,1)}, bf16[2,2,4,32,768]{4,3,2,1,0:T(8,128)(2,1)}, u32[]{:S(2)}, u32[]{:S(2)}) collective-permute-start(bf16[2,2,4,32,768]{4,3,2,1,0:T(8,128)(2,1)} %copy_bitcast_fusion.2), channel_id=1, source_target_pairs={{0,1},{1,0},{2,3},{3,2},{4,5},{5,4},{6,7},{7,6},{8,9},{9,8},{10,11... | collective-permute-start | bytes 2359304 | tf_op jit(solution)/shard_map/ppermute | solution.py:454
  134.4 30.0 %collective-permute-start.10 = (bf16[128,768]{1,0:T(8,128)(2,1)}, bf16[128,768]{1,0:T(8,128)(2,1)}, u32[]{:S(2)}, u32[]{:S(2)}) collective-permute-start(bf16[128,768]{1,0:T(8,128)(2,1)} %get-tuple-element.127), channel_id=1, source_target_pairs={{0,6},{1,7},{2,4},{3,5},{4,2},{5,3},{6,0},{7,1},{8,14},{9,15},{10,... | collective-permute-start | bytes 589832 | tf_op jit(solution)/shard_map/ppermute | solution.py:454
  136.3 28.6 %collective-permute-start.9 = (bf16[128,768]{1,0:T(8,128)(2,1)}, bf16[128,768]{1,0:T(8,128)(2,1)}, u32[]{:S(2)}, u32[]{:S(2)}) collective-permute-start(bf16[128,768]{1,0:T(8,128)(2,1)} %get-tuple-element.128), channel_id=1, source_target_pairs={{0,4},{1,5},{2,6},{3,7},{4,0},{5,1},{6,2},{7,3},{8,12},{9,13},{10,... | collective-permute-start | bytes 589832 | tf_op jit(solution)/shard_map/ppermute | solution.py:454
  136.9 28.1 %collective-permute-start.8 = (bf16[128,768]{1,0:T(8,128)(2,1)}, bf16[128,768]{1,0:T(8,128)(2,1)}, u32[]{:S(2)}, u32[]{:S(2)}) collective-permute-start(bf16[128,768]{1,0:T(8,128)(2,1)} %get-tuple-element.129), channel_id=1, source_target_pairs={{0,2},{1,3},{2,0},{3,1},{4,6},{5,7},{6,4},{7,5},{8,10},{9,11},{10,... | collective-permute-start | bytes 589832 | tf_op jit(solution)/shard_map/ppermute | solution.py:454
  142.4 19.4 %collective-permute-start.26 = (f32[8,4352]{1,0:T(8,128)S(1)}, f32[8,4352]{1,0:T(8,128)S(1)}, u32[]{:S(2)}, u32[]{:S(2)}) collective-permute-start(f32[8,4352]{1,0:T(8,128)S(1)} %pad_maximum_fusion.23), channel_id=1, source_target_pairs={{0,16},{1,17},{2,18},{3,19},{4,20},{5,21},{6,22},{7,23},{8,24},{9,... | collective-permute-start | bytes 417800 | tf_op jit(solution)/shard_map/ppermute | solution.py:454
  162.4 139.4 %collective-permute-start.52 = (bf16[2,2,4,192,256]{4,3,2,1,0:T(8,128)(2,1)}, bf16[2,2,4,192,256]{4,3,2,1,0:T(8,128)(2,1)}, u32[]{:S(2)}, u32[]{:S(2)}) collective-permute-start(bf16[2,2,4,192,256]{4,3,2,1,0:T(8,128)(2,1)} %dynamic-slice_bitcast_fusion.1), channel_id=1, source_target_pairs={{0,1},{1,0},{2,3},{3,2},{4,5},{5,4},{6,7},{7,6},{8,9},{9,8},{10,11... | collective-permute-start | bytes 4718600 | tf_op jit(solution)/shard_map/ppermute | solution.py:454
  172.5 33.1 %collective-permute-start.82 = (bf16[2,2,4,32,768]{4,3,2,1,0:T(8,128)(2,1)}, bf16[2,2,4,32,768]{4,3,2,1,0:T(8,128)(2,1)}, u32[]{:S(2)}, u32[]{:S(2)}) collective-permute-start(bf16[2,2,4,32,768]{4,3,2,1,0:T(8,128)(2,1)} %copy_bitcast_fusion.1), channel_id=1, source_target_pairs={{0,1},{1,0},{2,3},{3,2},{4,5},{5,4},{6,7},{7,6},{8,9},{9,8},{10,11... | collective-permute-start | bytes 2359304 | tf_op jit(solution)/shard_map/ppermute | solution.py:454
  174.6 36.3 %collective-permute-start.43 = (bf16[2,4,48,384]{3,2,1,0:T(8,128)(2,1)}, bf16[2,4,48,384]{3,2,1,0:T(8,128)(2,1)}, u32[]{:S(2)}, u32[]{:S(2)}) collective-permute-start(bf16[2,4,48,384]{3,2,1,0:T(8,128)(2,1)} %fusion.11), channel_id=1, source_target_pairs={{0,2},{1,3},{2,0},{3,1},{4,6},{5,7},{6,4},{7,5},{8,10},{9,11},{10,... | collective-permute-start | bytes 884744 | tf_op jit(solution)/shard_map/ppermute | solution.py:454
  196.6 25.2 %collective-permute-start.15 = (bf16[128,768]{1,0:T(8,128)(2,1)}, bf16[128,768]{1,0:T(8,128)(2,1)}, u32[]{:S(2)}, u32[]{:S(2)}) collective-permute-start(bf16[128,768]{1,0:T(8,128)(2,1)} %get-tuple-element.119), channel_id=1, source_target_pairs={{0,6},{1,7},{2,4},{3,5},{4,2},{5,3},{6,0},{7,1},{8,14},{9,15},{10,... | collective-permute-start | bytes 589832 | tf_op jit(solution)/shard_map/ppermute | solution.py:454
  204.0 18.4 %collective-permute-start.14 = (bf16[128,768]{1,0:T(8,128)(2,1)}, bf16[128,768]{1,0:T(8,128)(2,1)}, u32[]{:S(2)}, u32[]{:S(2)}) collective-permute-start(bf16[128,768]{1,0:T(8,128)(2,1)} %get-tuple-element.120), channel_id=1, source_target_pairs={{0,4},{1,5},{2,6},{3,7},{4,0},{5,1},{6,2},{7,3},{8,12},{9,13},{10,... | collective-permute-start | bytes 589832 | tf_op jit(solution)/shard_map/ppermute | solution.py:454
  216.8 42.5 %collective-permute-start.73 = (bf16[2,4,32,768]{3,2,1,0:T(8,128)(2,1)}, bf16[2,4,32,768]{3,2,1,0:T(8,128)(2,1)}, u32[]{:S(2)}, u32[]{:S(2)}) collective-permute-start(bf16[2,4,32,768]{3,2,1,0:T(8,128)(2,1)} %fusion.6), channel_id=1, source_target_pairs={{0,2},{1,3},{2,0},{3,1},{4,6},{5,7},{6,4},{7,5},{8,10},{9,11},{10,... | collective-permute-start | bytes 1179656 | tf_op jit(solution)/shard_map/ppermute | solution.py:454
  229.8 21.9 %collective-permute-start.45 = (bf16[48,384]{1,0:T(8,128)(2,1)}, bf16[48,384]{1,0:T(8,128)(2,1)S(1)}, u32[]{:S(2)}, u32[]{:S(2)}) collective-permute-start(bf16[48,384]{1,0:T(8,128)(2,1)} %get-tuple-element.199), channel_id=1, source_target_pairs={{0,8},{1,9},{2,10},{3,11},{4,12},{5,13},{6,14},{7,15},{8,0},{9,1},... | collective-permute-start | bytes 110600 | tf_op jit(solution)/shard_map/ppermute | solution.py:454
  231.4 20.2 %collective-permute-start.47 = (bf16[48,384]{1,0:T(8,128)(2,1)}, bf16[48,384]{1,0:T(8,128)(2,1)}, u32[]{:S(2)}, u32[]{:S(2)}) collective-permute-start(bf16[48,384]{1,0:T(8,128)(2,1)} %get-tuple-element.200), channel_id=1, source_target_pairs={{0,24},{1,25},{2,26},{3,27},{4,28},{5,29},{6,30},{7,31},{8,16},{9,... | collective-permute-start | bytes 110600 | tf_op jit(solution)/shard_map/ppermute | solution.py:454
  234.3 17.4 %collective-permute-start.46 = (bf16[48,384]{1,0:T(8,128)(2,1)}, bf16[48,384]{1,0:T(8,128)(2,1)}, u32[]{:S(2)}, u32[]{:S(2)}) collective-permute-start(bf16[48,384]{1,0:T(8,128)(2,1)} %get-tuple-element.201), channel_id=1, source_target_pairs={{0,16},{1,17},{2,18},{3,19},{4,20},{5,21},{6,22},{7,23},{8,24},{9,... | collective-permute-start | bytes 110600 | tf_op jit(solution)/shard_map/ppermute | solution.py:454
  258.2 46.2 %collective-permute-start.62 = (bf16[2,2,4,192,256]{4,3,2,1,0:T(8,128)(2,1)}, bf16[2,2,4,192,256]{4,3,2,1,0:T(8,128)(2,1)S(1)}, u32[]{:S(2)}, u32[]{:S(2)}) collective-permute-start(bf16[2,2,4,192,256]{4,3,2,1,0:T(8,128)(2,1)} %dynamic-slice_bitcast_fusion), channel_id=1, source_target_pairs={{0,1},{1,0},{2,3},{3,2},{4,5},{5,4},{6,7},{7,6},{8,9},{9,8},{10,11... | collective-permute-start | bytes 4718600 | tf_op jit(solution)/shard_map/ppermute | solution.py:454
  259.2 13.4 %collective-permute-start.51 = (bf16[4,48,384]{2,1,0:T(8,128)(2,1)S(1)}, bf16[4,48,384]{2,1,0:T(8,128)(2,1)S(1)}, u32[]{:S(2)}, u32[]{:S(2)}) collective-permute-start(bf16[4,48,384]{2,1,0:T(8,128)(2,1)S(1)} %get-tuple-element.193), channel_id=1, source_target_pairs={{0,1},{1,0},{2,3},{3,2},{4,5},{5,4},{6,7},{7,6},{8,9},{9,8},{10,11... | collective-permute-start | bytes 442376 | tf_op jit(solution)/shard_map/ppermute | solution.py:454
  260.5 13.6 %collective-permute-start.74 = (bf16[4,32,768]{2,1,0:T(8,128)(2,1)S(1)}, bf16[4,32,768]{2,1,0:T(8,128)(2,1)S(1)}, u32[]{:S(2)}, u32[]{:S(2)}) collective-permute-start(bf16[4,32,768]{2,1,0:T(8,128)(2,1)S(1)} %fusion.20), channel_id=1, source_target_pairs={{0,4},{1,5},{2,6},{3,7},{4,0},{5,1},{6,2},{7,3},{8,12},{9,13},{10,... | collective-permute-start | bytes 589832 | tf_op jit(solution)/shard_map/ppermute | solution.py:454
  291.3 35.0 %collective-permute-start.32 = (bf16[2,2,4,48,1152]{4,3,2,1,0:T(8,128)(2,1)S(1)}, bf16[2,2,4,48,1152]{4,3,2,1,0:T(8,128)(2,1)S(1)}, u32[]{:S(2)}, u32[]{:S(2)}) collective-permute-start(bf16[2,2,4,48,1152]{4,3,2,1,0:T(8,128)(2,1)S(1)} %copy-done.6), channel_id=1, source_target_pairs={{0,1},{1,0},{2,3},{3,2},{4,5},{5,4},{6,7},{7,6},{8,9},{9,8},{10,11... | collective-permute-start | bytes 5308424 | tf_op jit(solution)/shard_map/ppermute | solution.py:454
  303.2 17.1 %collective-permute-start.53 = (bf16[2,4,192,256]{3,2,1,0:T(8,128)(2,1)S(1)}, bf16[2,4,192,256]{3,2,1,0:T(8,128)(2,1)S(1)}, u32[]{:S(2)}, u32[]{:S(2)}) collective-permute-start(bf16[2,4,192,256]{3,2,1,0:T(8,128)(2,1)S(1)} %fusion.2), channel_id=1, source_target_pairs={{0,2},{1,3},{2,0},{3,1},{4,6},{5,7},{6,4},{7,5},{8,10},{9,11},{10,... | collective-permute-start | bytes 2359304 | tf_op jit(solution)/shard_map/ppermute | solution.py:454
  304.6 20.5 %collective-permute-start.63 = (bf16[2,4,192,256]{3,2,1,0:T(8,128)(2,1)S(1)}, bf16[2,4,192,256]{3,2,1,0:T(8,128)(2,1)S(1)}, u32[]{:S(2)}, u32[]{:S(2)}) collective-permute-start(bf16[2,4,192,256]{3,2,1,0:T(8,128)(2,1)S(1)} %fusion.1), channel_id=1, source_target_pairs={{0,4},{1,5},{2,6},{3,7},{4,0},{5,1},{6,2},{7,3},{8,12},{9,13},{10,... | collective-permute-start | bytes 2359304 | tf_op jit(solution)/shard_map/ppermute | solution.py:454
  325.3 13.1 %collective-permute-start.64 = (bf16[4,192,256]{2,1,0:T(8,128)(2,1)S(1)}, bf16[4,192,256]{2,1,0:T(8,128)(2,1)S(1)}, u32[]{:S(2)}, u32[]{:S(2)}) collective-permute-start(bf16[4,192,256]{2,1,0:T(8,128)(2,1)S(1)} %fusion.7), channel_id=1, source_target_pairs={{0,2},{1,3},{2,0},{3,1},{4,6},{5,7},{6,4},{7,5},{8,10},{9,11},{10,... | collective-permute-start | bytes 1179656 | tf_op jit(solution)/shard_map/ppermute | solution.py:454
  326.6 34.5 %collective-permute-start.33 = (bf16[2,4,48,1152]{3,2,1,0:T(8,128)(2,1)S(1)}, bf16[2,4,48,1152]{3,2,1,0:T(8,128)(2,1)S(1)}, u32[]{:S(2)}, u32[]{:S(2)}) collective-permute-start(bf16[2,4,48,1152]{3,2,1,0:T(8,128)(2,1)S(1)} %fusion), channel_id=1, source_target_pairs={{0,4},{1,5},{2,6},{3,7},{4,0},{5,1},{6,2},{7,3},{8,12},{9,13},{10,... | collective-permute-start | bytes 2654216 | tf_op jit(solution)/shard_map/ppermute | solution.py:454
  337.8 13.8 %collective-permute-start.56 = (bf16[192,256]{1,0:T(8,128)(2,1)S(1)}, bf16[192,256]{1,0:T(8,128)(2,1)S(1)}, u32[]{:S(2)}, u32[]{:S(2)}) collective-permute-start(bf16[192,256]{1,0:T(8,128)(2,1)S(1)} %get-tuple-element.161), channel_id=1, source_target_pairs={{0,16},{1,17},{2,18},{3,19},{4,20},{5,21},{6,22},{7,23},{8,24},{9,... | collective-permute-start | bytes 294920 | tf_op jit(solution)/shard_map/ppermute | solution.py:454
  338.6 14.5 %collective-permute-start.65 = (bf16[192,256]{1,0:T(8,128)(2,1)S(1)}, bf16[192,256]{1,0:T(8,128)(2,1)S(1)}, u32[]{:S(2)}, u32[]{:S(2)}) collective-permute-start(bf16[192,256]{1,0:T(8,128)(2,1)S(1)} %get-tuple-element.168), channel_id=1, source_target_pairs={{0,8},{1,9},{2,10},{3,11},{4,12},{5,13},{6,14},{7,15},{8,0},{9,1},... | collective-permute-start | bytes 294920 | tf_op jit(solution)/shard_map/ppermute | solution.py:454
  362.3 13.6 %collective-permute-start.61 = (bf16[4,192,256]{2,1,0:T(8,128)(2,1)S(1)}, bf16[4,192,256]{2,1,0:T(8,128)(2,1)S(1)}, u32[]{:S(2)}, u32[]{:S(2)}) collective-permute-start(bf16[4,192,256]{2,1,0:T(8,128)(2,1)S(1)} %get-tuple-element.153), channel_id=1, source_target_pairs={{0,1},{1,0},{2,3},{3,2},{4,5},{5,4},{6,7},{7,6},{8,9},{9,8},{10,11... | collective-permute-start | bytes 1179656 | tf_op jit(solution)/shard_map/ppermute | solution.py:454
  365.7 24.8 %collective-permute-start.71 = (bf16[4,192,256]{2,1,0:T(8,128)(2,1)S(1)}, bf16[4,192,256]{2,1,0:T(8,128)(2,1)S(1)}, u32[]{:S(2)}, u32[]{:S(2)}) collective-permute-start(bf16[4,192,256]{2,1,0:T(8,128)(2,1)S(1)} %get-tuple-element.162), channel_id=1, source_target_pairs={{0,1},{1,0},{2,3},{3,2},{4,5},{5,4},{6,7},{7,6},{8,9},{9,8},{10,11... | collective-permute-start | bytes 1179656 | tf_op jit(solution)/shard_map/ppermute | solution.py:454
  (87 other events, 658.0 us)

commit v2 on v1

--- a/solution.py
+++ b/solution.py
@@ -430,6 +430,268 @@
     )(dq, dk0, dk1, dv0, dv1, raw, hidden, x, grad_middle, mod, weight, qgain, kgain, cosine, sine)
 
 
+class Place:
+    def __init__(self):
+        self.z, self.gy, self.gx = (lax.axis_index(name) for name in AXES)
+        self.core = lax.rem(self.gx, 2)
+        self.side = self.gx // 2
+        self.chip = 2 * self.gy + self.side
+
+    def flipped(self, k):
+        return 2 * lax.rem(self.gy + k // 2, 2) + lax.rem(self.side + lax.rem(k, 2), 2)
+
+    def pair(self):
+        return {"gx": self.gx + 1 - 2 * self.core}
+
+    def plane(self, k):
+        device = {}
+        if k & 2:
+            device["gy"] = 1 - self.gy
+        if k & 1:
+            device["gx"] = lax.rem(self.gx + 2, 4)
+        return device
+
+    def depth(self, d):
+        return {"batch": self.flipped_z(d)}
+
+    def flipped_z(self, d):
+        return {1: self.z + 1 - 2 * lax.rem(self.z, 2), 2: lax.rem(self.z + 2, 4), 3: 3 - self.z}[d]
+
+
+def meet(devices):
+    barrier = pltpu.get_barrier_semaphore()
+    for device in devices:
+        pl.semaphore_signal(barrier, inc=1, device_id=device, device_id_type=pl.DeviceIdType.MESH)
+    pl.semaphore_wait(barrier, len(devices))
+
+
+def send(source, target, send_sem, recv_sem, device):
+    return pltpu.make_async_remote_copy(
+        src_ref=source, dst_ref=target, send_sem=send_sem, recv_sem=recv_sem, device_id=device,
+        device_id_type=pl.DeviceIdType.MESH,
+    )
+
+
+def feed_order(step):
+    owner = jnp.where(
+        step < 2, 3, jnp.where((step == 2) | (step == 5), 2, jnp.where(step < 5, 1, 0))
+    )
+    return owner, lax.rem(step, 2)
+
+
+def feed_block(step, i):
+    step = jnp.minimum(step, 7)
+    owner, half = feed_order(step)
+    return (2 * half + i) * 4 + Place().flipped(owner)
+
+
+def feed_turn_kernel(
+    h2_ref, h2t_ref, gf_ref, wg0, wg1, wu0, wu1, bg0, bg1, bu0, bu1, wd0, wd1,
+    mid_ref, att_ref, dy_ref, mix_ref, mod_ref, weight_ref, dbias_ref,
+    out_ref, gmid_ref, gmix_ref, dw_ref, sums_ref, db_ref, total_ref,
+    feed_ref, gh_ref, made, paired, near, pair_send, pair_recv, near_send, near_recv,
+):
+    place = Place()
+    core = place.core
+    step = pl.program_id(0)
+    slot = lax.rem(step, 2)
+    width = h2_ref.shape[1]
+    unit = 128
+    g_rows = width
+
+    @pl.when(step == 0)
+    def _():
+        feed_ref[...] = jnp.zeros_like(feed_ref)
+        gh_ref[...] = jnp.zeros_like(gh_ref)
+        meet([place.pair(), place.plane(1), place.plane(2)])
+
+    def pair_copy(of):
+        return send(
+            made.at[lax.rem(of, 2), 1 - core], paired.at[of], pair_send.at[lax.rem(of, 2)],
+            pair_recv.at[of], place.pair(),
+        )
+
+    def near_copy(of, k):
+        return send(paired.at[of], near.at[of], near_send.at[of], near_recv.at[of], place.plane(k))
+
+    @pl.when(step >= 1)
+    def _():
+        pair_copy(step - 1).start()
+
+    @pl.when(step < 8)
+    def _():
+        owner, half = feed_order(step)
+        hidden = h2_ref[...]
+        grad_feed = gf_ref[...]
+        wg = jnp.concatenate([wg0[...], wg1[...]], axis=1)
+        wu = jnp.concatenate([wu0[...], wu1[...]], axis=1)
+        wd = jnp.concatenate([wd0[...], wd1[...]], axis=0)
+        gate = mm(hidden, wg) + jnp.concatenate([bg0[...], bg1[...]], axis=1).astype(F32)
+        up = mm(hidden, wu) + jnp.concatenate([bu0[...], bu1[...]], axis=1).astype(F32)
+        grad_product = mm_nt(grad_feed, wd)
+        sig = 1.0 / (1.0 + jnp.exp(-gate))
+        active = gate * sig
+        product = (active * up).astype(BF16)
+        grad_gate = (grad_product * up * sig * (1.0 + gate * (1.0 - sig))).astype(BF16)
+        grad_up = (grad_product * active).astype(BF16)
+        feed_ref[...] += mm(product, wd)
+        gh_ref[...] += mm_nt(grad_gate, wg) + mm_nt(grad_up, wu)
+        for e, grad in enumerate((grad_gate, grad_up)):
+            total = col_sum(grad.astype(F32))
+            for i in range(2):
+                row = 16 * e + (2 * half + i) * 4 + place.flipped(owner)
+                db_ref[pl.ds(row, 1), :] = total[:, i * unit : (i + 1) * unit]
+
+        @pl.when(step >= 2)
+        def _():
+            pair_copy(step - 2).wait_send()
+
+        for e, grad in enumerate((grad_gate, grad_up)):
+            made[slot, e, :g_rows] = mm(h2t_ref[...], grad).astype(BF16)
+        product_t = product.T
+        for b in range(3):
+            d = mm(product_t, grad_feed[:, 256 * b : 256 * b + 256]).astype(BF16)
+            for i in range(2):
+                for c in range(2):
+                    made[slot, c, pl.ds(g_rows + b * 128 + i * 64, 64)] = d[
+                        i * 128 + c * 64 : i * 128 + c * 64 + 64
+                    ]
+
+    @pl.when(step >= 1)
+    def _():
+        of = step - 1
+        copy = pair_copy(of)
+        copy.wait_recv()
+        late = (of == 4) | (of == 5)
+
+        @pl.when(jnp.logical_not(late))
+        def _():
+            paired[of] = (made[1 - slot, core].astype(F32) + paired[of].astype(F32)).astype(BF16)
+
+        @pl.when(late)
+        def _():
+            near_copy(of - 4, 1).wait_recv()
+            paired[of] = (
+                made[1 - slot, core].astype(F32)
+                + paired[of].astype(F32)
+                + near[of - 4].astype(F32)
+            ).astype(BF16)
+
+        @pl.when((of == 0) | (of == 2) | (of == 5))
+        def _():
+            near_copy(of, 2).start()
+
+        @pl.when((of == 1) | (of == 3) | (of == 4))
+        def _():
+            near_copy(of, 1).start()
+
+    @pl.when(step == 8)
+    def _():
+        half = width // 2
+        dy = dy_ref[...].astype(F32)
+        feed = feed_ref[...] + dbias_ref[...].astype(F32)
+        middle = mid_ref[...]
+        out_ref[...] = (middle + mod_ref[:, 5 * width :] * feed).astype(BF16)
+        factor = lax.rsqrt(jnp.mean(middle * middle, axis=-1, keepdims=True) + NORM_EPSILON)
+        normed = middle * factor
+        grad_hidden = gh_ref[...]
+        product = grad_hidden * normed
+        grad_normed = grad_hidden * (1.0 + mod_ref[:, 4 * width : 5 * width])
+        back = factor * (
+            grad_normed - normed * jnp.mean(grad_normed * normed, axis=-1, keepdims=True)
+        )
+        grad_middle = dy + back
+        gmid_ref[...] = grad_middle
+        grad_attended = (mod_ref[:, 2 * width : 3 * width] * grad_middle).astype(BF16)
+        sums_ref[0:1, :] = col_sum(grad_middle * att_ref[...].astype(F32))
+        sums_ref[1:2, :] = col_sum(grad_hidden)
+        sums_ref[2:3, :] = col_sum(product)
+        sums_ref[3:4, :] = col_sum(dy * feed)
+        sums_ref[4:5, :] = col_sum(grad_attended.astype(F32))
+        sums_ref[5:6, :] = col_sum(gf_ref[...].astype(F32))
+        sums_ref[6:8, :] = jnp.zeros((2, width), F32)
+        gmix_ref[...] = mm_nt(grad_attended, weight_ref[...]).astype(BF16)
+        mixed_t = mix_ref[...].T
+        dw_ref[0] = mm(mixed_t, grad_attended[:, :half]).astype(BF16)
+        dw_ref[1] = mm(mixed_t, grad_attended[:, half:]).astype(BF16)
+        for of in (6, 7):
+            pair_copy(of).wait_send()
+        for of in (2, 3, 4, 5):
+            near_copy(of, 1).wait_recv()
+        for of in range(6):
+            near_copy(of, 1).wait_send()
+        rows = width // 4
+        for f in range(2):
+            for z in range(4):
+                span = slice(z * rows, (z + 1) * rows)
+                total_ref[z, f] = sum(
+                    part.astype(F32)
+                    for part in (paired[6 + f, span], near[2 + f, span], near[4 + f, span])
+                ).astype(BF16)
+            for i in range(2):
+                for b in range(3):
+                    span = slice(g_rows + b * 128 + i * 64, g_rows + b * 128 + i * 64 + 64)
+                    total_ref[2 * f + i, 2, b * 64 : b * 64 + 64] = sum(
+                        part.astype(F32)
+                        for part in (paired[6 + f, span], near[2 + f, span], near[4 + f, span])
+                    ).astype(BF16)
+
+
+def once(shape):
+    return pl.BlockSpec(shape, lambda *_: (0,) * len(shape), pipeline_mode=pl.Buffered(1))
+
+
+def feed_turn_call(
+    hidden, hidden_t, grad_feed, gate_up, gate_up_bias, down, middle, attended, dy, mixed, mod,
+    weight, down_bias,
+):
+    rows, width = hidden.shape
+    low = jax.ShapeDtypeStruct((rows, width), BF16)
+    wide = jax.ShapeDtypeStruct((rows, width), F32)
+    cols = lambda i, e: pl.BlockSpec((width, 128), lambda s: (0, 16 * e + feed_block(s, i)))
+    bias = lambda i, e: pl.BlockSpec((1, 128), lambda s: (0, 16 * e + feed_block(s, i)))
+    deep = lambda i: pl.BlockSpec((128, width), lambda s: (feed_block(s, i), 0))
+    piece = (width + 384, 256)
+    out_shape = [
+        low, wide, low,
+        jax.ShapeDtypeStruct((2, width, width // 2), BF16),
+        jax.ShapeDtypeStruct((8, width), F32),
+        jax.ShapeDtypeStruct((32, 128), F32),
+        jax.ShapeDtypeStruct((4, 3, width // 4, 256), BF16),
+    ]
+    return pl.pallas_call(
+        feed_turn_kernel,
+        grid=(9,),
+        in_specs=[once((rows, width)), once((width, rows)), once((rows, width))]
+        + [cols(0, 0), cols(1, 0), cols(0, 1), cols(1, 1)]
+        + [bias(0, 0), bias(1, 0), bias(0, 1), bias(1, 1)]
+        + [deep(0), deep(1)]
+        + [once((rows, width))] * 4
+        + [once(mod.shape), once(weight.shape), once(down_bias.shape)],
+        out_specs=[full(shape.shape) for shape in out_shape],
+        out_shape=out_shape,
+        scratch_shapes=[
+            pltpu.VMEM((rows, width), F32),
+            pltpu.VMEM((rows, width), F32),
+            pltpu.VMEM((2, 2) + piece, BF16),
+            pltpu.VMEM((8,) + piece, BF16),
+            pltpu.VMEM((6,) + piece, BF16),
+            pltpu.SemaphoreType.DMA((2,)),
+            pltpu.SemaphoreType.DMA((8,)),
+            pltpu.SemaphoreType.DMA((6,)),
+            pltpu.SemaphoreType.DMA((6,)),
+        ],
+        compiler_params=pltpu.CompilerParams(
+            vmem_limit_bytes=VMEM_LIMIT, collective_id=1, has_side_effects=True
+        ),
+        name="feed_turn",
+    )(
+        hidden, hidden_t, grad_feed, gate_up, gate_up, gate_up, gate_up, gate_up_bias,
+        gate_up_bias, gate_up_bias, gate_up_bias, down, down, middle, attended, dy, mixed, mod,
+        weight, down_bias,
+    )
+
+
 def take(array_in, index, axis=0):
     return lax.dynamic_index_in_dim(array_in, index, axis, keepdims=False)
 
@@ -568,24 +830,22 @@
 
     unit = 256
     blocks = hidden_width // unit
-    quick = nb == 4
-    chunks = 2 if quick else 1
-    feed = jnp.zeros((rows, width), F32)
-    grad_hidden = jnp.zeros((rows, width), F32)
-    down_parts, gate_parts, gate_bias_parts = [], [], []
-    for j in range(chunks):
+    quick = nb == 4 and hidden_width == 16 * 128
+    if quick:
+        output_rows, grad_middle, grad_mixed, d_out, sums_two, gate_bias, totals = feed_turn_call(
+            hidden_two, hidden_two_t, grad_feed, gate_up_weight, gate_up_bias[None], down_weight,
+            middle, attended, dy, mixed, mod, outproj_weight, down_bias[None],
+        )
+    else:
         feed, grad_hidden, d_down, d_gate, d_bias = feed_call(
             hidden_two, hidden_two_t, grad_feed, gate_up_weight, gate_up_bias[None], down_weight,
-            feed, grad_hidden, j, chunks, unit,
+            jnp.zeros((rows, width), F32), jnp.zeros((rows, width), F32), 0, 1, unit,
         )
-        down_parts.append(d_down)
-        gate_parts.append(d_gate)
-        gate_bias_parts.append(d_bias)
-
-    output_rows, grad_middle, grad_mixed, d_out, sums_two = turn_call(
-        feed, grad_hidden, middle, attended, dy, grad_feed, mixed, mod, outproj_weight,
-        down_bias[None],
-    )
+        output_rows, grad_middle, grad_mixed, d_out, sums_two = turn_call(
+            feed, grad_hidden, middle, attended, dy, grad_feed, mixed, mod, outproj_weight,
+            down_bias[None],
+        )
+        gate_bias = d_bias.reshape(blocks, 2, unit).transpose(1, 0, 2)
     dq, dk0, dk1, dv0, dv1 = attend_back_call(
         q, k0, k1, v0, v1, grown, grad_mixed, mixed, inverse, head
     )
@@ -605,19 +865,16 @@
 
     slice_rows = width // nb
     if quick:
-        downs, gates = [], []
-        for j in range(chunks):
-            order = (1, 2) if j % 2 == 0 else (2, 1)
-            first, second = (side, gy) if j % 2 == 0 else (gy, side)
-            d = down_parts[j].reshape(nb, 2, 2, 2, unit // 8, width).transpose(1, 2, 3, 0, 4, 5)
-            g = gate_parts[j].reshape(2, 2, 2, nb, slice_rows, unit)
-            d = reduce_pieces(moves, d, core, first, second, order, z)
-            g = reduce_pieces(moves, g, core, first, second, order, z)
-            downs.append(d.reshape(unit, width))
-            gates.append(g.reshape(blocks // chunks, 2, slice_rows, unit))
-        grad_down_w = jnp.stack(downs).reshape(hidden_width // nb, width).astype(F32)
-        grad_gu_w = jnp.stack(gates, axis=1).reshape(blocks, 2, slice_rows, unit)
-        grad_gu_w = grad_gu_w.transpose(2, 1, 0, 3).reshape(slice_rows, 2 * hidden_width).astype(F32)
+        own = take(totals, z).astype(F32)
+        for d in range(1, nb):
+            own = add(own, moves.flip(take(totals, z ^ d), batch=d))
+        own = own.astype(BF16)
+        own = regroup([own] + [moves.plane(own, k) for k in range(1, 4)], place)
+        own = regroup([own, moves.pair(own)], core)
+        gates = own[:, :, :2].reshape(2, 4, 2, slice_rows, 2, 128).transpose(3, 0, 2, 4, 1, 5)
+        grad_gu_w = gates.reshape(slice_rows, 2 * hidden_width).astype(F32)
+        downs = own[:, :, 2].reshape(2, 4, 3, 64, 256).transpose(1, 0, 3, 2, 4)
+        grad_down_w = downs.reshape(hidden_width // nb, width).astype(F32)
 
         def by_rows(d, order, first, second):
             wide = d.shape[2]
@@ -637,14 +894,13 @@
         def joined(d):
             return jnp.concatenate([d[0], d[1]], axis=1)
 
-        grad_down_w = scatter(down_parts[0].reshape(hidden_width, width))
+        grad_down_w = scatter(d_down.reshape(hidden_width, width))
         grad_gu_w = scatter(
-            gate_parts[0].transpose(2, 1, 0, 3).reshape(width, 2 * hidden_width)
+            d_gate.transpose(2, 1, 0, 3).reshape(width, 2 * hidden_width)
         )
         grad_out_w = scatter(joined(d_out))
         grad_in_w = scatter(joined(d_in))
 
-    gate_bias = jnp.stack(gate_bias_parts, axis=1).reshape(blocks, 2, unit).transpose(1, 0, 2)
     gain_sums = sums_one[2:4].reshape(2, heads, head).sum(axis=1)
     early = jnp.concatenate([sums_two[:6].reshape(-1), gate_bias.reshape(-1)])
     late = jnp.concatenate([sums_one[:2].reshape(-1), in_bias.reshape(-1), gain_sums.reshape(-1)])

time: 403 us -> 364 us (0.903)
  starting transfers between devices: 97.5 us -> 60 us
  Pallas kernels: 107 us -> 116 us
  other arithmetic: 44.4 us -> 38.4 us
  local copies, waits for them, and re-layouts: 48.8 us -> 44.3 us
    ppermute x92 -> x59, starting transfers between devices: 97.5 us -> 60 us  [flip(): return lax.ppermute(value, AXES, pairs)]
    convert_element_type x2 -> x4, local copies, waits for them, and re-layouts: 2.1 us -> 13.2 us  [the longest x3 12.5 us: body(): grad_gu_w = gates.reshape(slice_rows, 2 * hidden_width).astype(F32)]
    pallas_call x3 -> x1, Pallas kernels: 49.2 us -> 57.2 us  [feed_turn_call(): pl.pallas_call(feed_turn_kernel, grid=(9,), in_specs=[once((rows, width))...]
    squeeze x14 -> x7, local copies, waits for them, and re-layouts: 11.5 us -> 3.99 us  [take(): return lax.dynamic_index_in_dim(array_in, index, axis, keepdims=False)]
    convert_element_type x6 -> x2, other arithmetic: 7.99 us -> 3.4 us  [reduce_pieces(): add(take(mine, 1 - first), take(arrived, 1 - first)).astype(BF16)]
    ppermute x92 -> x59, waiting for transfers between devices: 84.9 us -> 82.2 us  [flip(): return lax.ppermute(value, AXES, pairs)]
    another operation x16 -> x10, other arithmetic: 6.54 us -> 8.61 us  [regroup(): stacked = jnp.stack(parts)]
  transfers between devices with their start and end apart: 92 -> 59, of which waited for: 40 -> 23; matrix products, arithmetic and copies ran while one was open for 24% -> 24% of each run, Pallas kernels for 10% -> 12%
where the time goes in v2:
time: 364 us; the launch traced here: 357 us
  Pallas kernels  116 us (32%)
  waiting for transfers between devices  82.2 us (23%)
  starting transfers between devices  60 us (16%)
  local copies, waits for them, and re-layouts  44.3 us (12%)
  other arithmetic  38.4 us (11%)
  matrix products  11.4 us (3%)
  between operations  5.11 us (1%)
    ppermute x59, waiting for transfers between devices, flip(): return lax.ppermute(value, AXES, pairs)  82.2 us
    ppermute x59, starting transfers between devices, flip(): return lax.ppermute(value, AXES, pairs)  60 us
    pallas_call x1, Pallas kernels, feed_turn_call(): pl.pallas_call(feed_turn_kernel, grid=(9,), in_specs=[once((rows, width))...  57.2 us
    pallas_call x1, Pallas kernels, attend_back_call(): pl.pallas_call(functools.partial(attend_back_kernel, head ** (-0.5)), gri...  16.1 us
    pallas_call x1, Pallas kernels, project_back_call(): pl.pallas_call(functools.partial(project_back_kernel, head), out_shape=[j...  13.2 us
    convert_element_type x3, local copies, waits for them, and re-layouts, body(): grad_gu_w = gates.reshape(slice_rows, 2 * hidden_width).astype(F32)  12.5 us
    pallas_call x1, Pallas kernels, attend_call(): pl.pallas_call(functools.partial(attend_kernel, head ** (-0.5)), grid=(wi...  11.9 us
    another operation x10, other arithmetic, regroup(): stacked = jnp.stack(parts)  8.61 us
  transfers between devices with their start and end apart: 59, of which 23 were waited for; matrix products, arithmetic and copies ran while one was open for 24% of the time, Pallas kernels for 12%

profile of v2, /device:TPU:0, one launch (start us, length us, event | category | flops | bytes accessed | tf_op | source)
XLA Modules:
  0.0 357.1 jit_solution(9084665132132572296)
XLA Ops:
  2.0 4.0 %collective-permute-start.2 = (bf16[128,768]{1,0:T(8,128)(2,1)S(1)}, bf16[128,768]{1,0:T(8,128)(2,1)S(1)}, u32[]{:S(2)}, u32[]{:S(2)}) collective-permute-start(bf16[128,768]{1,0:T(8,128)(2,1)S(1)} %get-tuple-element.118), channel_id=1, source_target_pairs={{0,6},{1,7},{2,4},{3,5},{4,2},{5,3},{6,0},{7,1},{8,14},{9,15},{10,... | collective-permute-start | bytes 589832 | tf_op jit(solution)/shard_map/ppermute | solution.py:716
  11.9 2.0 collective-permute-start.28
  16.1 6.4 %modulation.1 = f32[16,4608]{1,0:T(8,128)} custom-call(bf16[16,768]{1,0:T(8,128)(2,1)} %broadcast_in_dim.73.act_ref, bf16[768,4608]{1,0:T(8,128)(2,1)} %weight_ref.5, bf16[1,4608]{1,0:T(2,128)(2,1)} %broadcast_in_dim.74.bias_ref), custom_call_target="tpu_custom_call" | custom-call | tf_op jit(solution)/shard_map/modulation/pallas_call | solution.py:49
  28.9 6.5 %project.1 = (bf16[512,768]{1,0:T(8,128)(2,1)}, bf16[512,768]{1,0:T(8,128)(2,1)}, bf16[512,768]{1,0:T(8,128)(2,1)}, bf16[512,768]{1,0:T(8,128)(2,1)}, bf16[512,1536]{1,0:T(8,128)(2,1)}) custom-call(bf16[512,768]{1,0:T(8,128)(2,1)} %pad_maximum_fusion.3.x_ref, f32[1,4608]{1,0:T(1,128)} %slice.102.mod_ref, bf16[768,2304]{1,0:T(8,128)(2,1)} %weight_ref.9, ...), custom_call_target="tpu_custom_call" | custom-call | tf_op jit(solution)/shard_map/project/pallas_call | solution.py:114
  37.7 2.1 collective-permute-done.29
  41.5 2.1 collective-permute-done.30
  43.6 2.6 collective-permute-start.31
  58.1 11.9 %attend.1 = (bf16[512,768]{1,0:T(8,128)(2,1)}, bf16[12,512,1024]{2,1,0:T(8,128)(2,1)}, f32[512,768]{1,0:T(8,128)}) custom-call(bf16[512,768]{1,0:T(8,128)(2,1)} %get-tuple-element.45.q_ref, bf16[512,768]{1,0:T(8,128)(2,1)} %get-tuple-element.46.k0_ref, bf16[512,768]{1,0:T(8,128)(2,1)} %copy-done.5, bf16[512,768]{1,0:T(8,128)(2,1)} %get-tuple-element.47.v0_ref, ...), custom_call_target="tpu_custom_call" | custom-call | tf_op jit(solution)/shard_map/attend/pallas_call | solution.py:155
  70.1 4.4 %middle.1 = (bf16[512,768]{1,0:T(8,128)(2,1)}, f32[512,768]{1,0:T(8,128)}, bf16[512,768]{1,0:T(8,128)(2,1)}, bf16[768,512]{1,0:T(8,128)(2,1)}, bf16[512,768]{1,0:T(8,128)(2,1)}) custom-call(bf16[512,768]{1,0:T(8,128)(2,1)} %get-tuple-element.48.mix_ref, bf16[512,768]{1,0:T(8,128)(2,1)} %pad_maximum_fusion.3.x_ref, ...), custom_call_target="tpu_custom_call" | custom-call | tf_op jit(solution)/shard_map/middle/pallas_call | solution.py:239
  74.5 57.2 %feed_turn.1 = (bf16[512,768]{1,0:T(8,128)(2,1)}, f32[512,768]{1,0:T(8,128)}, bf16[512,768]{1,0:T(8,128)(2,1)}, bf16[2,768,384]{2,1,0:T(8,128)(2,1)}, f32[8,768]...) custom-call(bf16[512,768]{1,0:T(8,128)(2,1)} %get-tuple-element.49.h2_ref, ...), custom_call_target="tpu_custom_call" | custom-call | tf_op jit(solution)/shard_map/feed_turn/pallas_call | solution.py:662
  135.2 2.0 slice_bitcast_fusion.1
  140.6 16.1 %attend_back.1 = (bf16[512,768]{1,0:T(8,128)(2,1)}, bf16[512,768]{1,0:T(8,128)(2,1)}, bf16[512,768]{1,0:T(8,128)(2,1)}, bf16[512,768]{1,0:T(8,128)(2,1)}, bf16[512,768]{1,0:T(8,128)(2,1)}) custom-call(bf16[512,768]{1,0:T(8,128)(2,1)} %get-tuple-element.45.q_ref, bf16[512,768]{1,0:T(8,128)(2,1)} %get-tuple-element.46.k0_ref, bf16[512,768]{1,0:T(8,128)(2,1)} %copy-done.5, ...), custom_call_target="tpu_custom_call" | custom-call | tf_op jit(solution)/shard_map/attend_back/pallas_call | solution.py:205
  170.6 28.1 %collective-permute-done.26 = f32[8,4352]{1,0:T(8,128)} collective-permute-done((f32[8,4352]{1,0:T(8,128)S(1)}, f32[8,4352]{1,0:T(8,128)}, u32[]{:S(2)}, u32[]{:S(2)}) %collective-permute-start.26) | collective-permute-done | bytes 139296 | tf_op jit(solution)/shard_map/ppermute | solution.py:716
  216.3 4.3 %collective-permute-done.56 = bf16[3,192,256]{2,1,0:T(8,128)(2,1)S(1)} collective-permute-done((bf16[3,192,256]{2,1,0:T(8,128)(2,1)S(1)}, bf16[3,192,256]{2,1,0:T(8,128)(2,1)S(1)}, u32[]{:S(2)}, u32[]{:S(2)}) %collective-permute-start.56) | collective-permute-done | bytes 294944 | tf_op jit(solution)/shard_map/ppermute | solution.py:716
  222.6 13.2 %project_back.1 = (bf16[512,768]{1,0:T(8,128)(2,1)}, bf16[2,768,1152]{2,1,0:T(8,128)(2,1)}, f32[8,768]{1,0:T(8,128)}, f32[1,2304]{1,0:T(1,128)}) custom-call(bf16[512,768]{1,0:T(8,128)(2,1)} %get-tuple-element.58.dq_ref, bf16[512,768]{1,0:T(8,128)(2,1)} %get-tuple-element.59.dk0_ref, bf16[512,768]{1,0:T(8,128)(2,1)} %collective-permute-done.11.dk1_ref, ...), custom_call_target="tpu_custom_call" | custom-call | tf_op jit(solution)/shard_map/project_back/pallas_call | solution.py:419
  248.7 3.7 %collective-permute-done.19 = f32[4,1984]{1,0:T(4,128)S(1)} collective-permute-done((f32[4,1984]{1,0:T(4,128)S(1)}, f32[4,1984]{1,0:T(4,128)S(1)}, u32[]{:S(2)}, u32[]{:S(2)}) %collective-permute-start.19) | collective-permute-done | bytes 31776 | tf_op jit(solution)/shard_map/ppermute | solution.py:716
  254.3 4.5 %collective-permute-done.20 = f32[8,1984]{1,0:T(8,128)S(1)} collective-permute-done((f32[8,1984]{1,0:T(8,128)S(1)}, f32[8,1984]{1,0:T(8,128)S(1)}, u32[]{:S(2)}, u32[]{:S(2)}) %collective-permute-start.20) | collective-permute-done | bytes 63520 | tf_op jit(solution)/shard_map/ppermute | solution.py:716
  263.7 3.3 collective-permute-done.44
  271.2 2.6 collective-permute-start.45
  276.9 4.9 %add_multiply_fusion = f32[16,768]{1,0:T(8,128)S(1)} fusion(bf16[768,4608]{1,0:T(8,128)(2,1)} %weight_ref.5, f32[16,3072]{1,0:T(8,128)S(1)} %slice.104, f32[16,1536]{1,0:T(8,128)S(1)} %slice.103, f32[16,896]{1,0:T(8,128)S(1)} %copy-done.15), kind=kOutput, calls=%fused_computation.110 | convolution fusion | flops 113639424 | bytes 7471104 | tf_op jit(solution)/shard_map/dot_general | solution.py:23
  284.2 3.3 fusion.32
  287.5 3.1 fusion.30
  295.9 8.8 %collective-permute-done.33 = bf16[2,4,48,1152]{3,2,1,0:T(8,128)(2,1)S(1)} collective-permute-done((bf16[2,4,48,1152]{3,2,1,0:T(8,128)(2,1)S(1)}, bf16[2,4,48,1152]{3,2,1,0:T(8,128)(2,1)S(1)}, u32[]{:S(2)}, u32[]{:S(2)}) %collective-permute-start.33) | collective-permute-done | bytes 884768 | tf_op jit(solution)/shard_map/ppermute | solution.py:716
  309.1 6.1 %collective-permute-done.34 = bf16[4,48,1152]{2,1,0:T(8,128)(2,1)S(1)} collective-permute-done((bf16[4,48,1152]{2,1,0:T(8,128)(2,1)S(1)}, bf16[4,48,1152]{2,1,0:T(8,128)(2,1)S(1)}, u32[]{:S(2)}, u32[]{:S(2)}) %collective-permute-start.34) | collective-permute-done | bytes 442400 | tf_op jit(solution)/shard_map/ppermute | solution.py:716
  316.7 1.9 collective-permute-start.37
  318.8 2.4 collective-permute-start.35
  321.3 2.1 collective-permute-done.37
  323.4 2.3 collective-permute-done.36
  334.0 2.1 fusion.3
  339.4 3.7 %reshape.328 = f32[2,4,2,192,2,128]{5,4,3,2,1,0:T(2,128)S(1)} reshape(f32[2,4,2,192,256]{4,3,2,1,0:T(8,128)} %fusion.2) | data formatting | bytes 6291456 | tf_op jit(solution)/shard_map/convert_element_type | solution.py:875
  343.1 3.7 %copy.49 = f32[192,2,2,2,4,128]{5,4,3,2,1,0:T(4,128)} copy(f32[192,2,2,2,4,128]{5,3,0,2,4,1:T(2,128)S(1)} %bitcast.191) | data formatting | bytes 6291456 | tf_op jit(solution)/shard_map/convert_element_type | solution.py:875
  346.8 5.2 %reshape.326 = f32[192,4096]{1,0:T(8,128)} reshape(f32[192,2,2,2,4,128]{5,4,3,2,1,0:T(4,128)} %copy.49) | data formatting | bytes 6291456 | tf_op jit(solution)/shard_map/convert_element_type | solution.py:875
  (286 shorter events, 125.1 us)
Async XLA Ops:
  2.0 26.0 %collective-permute-start.2 = (bf16[128,768]{1,0:T(8,128)(2,1)S(1)}, bf16[128,768]{1,0:T(8,128)(2,1)S(1)}, u32[]{:S(2)}, u32[]{:S(2)}) collective-permute-start(bf16[128,768]{1,0:T(8,128)(2,1)S(1)} %get-tuple-element.118), channel_id=1, source_target_pairs={{0,6},{1,7},{2,4},{3,5},{4,2},{5,3},{6,0},{7,1},{8,14},{9,15},{10,... | collective-permute-start | bytes 589832 | tf_op jit(solution)/shard_map/ppermute | solution.py:716
  6.0 22.0 %collective-permute-start.1 = (bf16[128,768]{1,0:T(8,128)(2,1)S(1)}, bf16[128,768]{1,0:T(8,128)(2,1)S(1)}, u32[]{:S(2)}, u32[]{:S(2)}) collective-permute-start(bf16[128,768]{1,0:T(8,128)(2,1)S(1)} %get-tuple-element.119), channel_id=1, source_target_pairs={{0,4},{1,5},{2,6},{3,7},{4,0},{5,1},{6,2},{7,3},{8,12},{9,13},{10,... | collective-permute-start | bytes 589832 | tf_op jit(solution)/shard_map/ppermute | solution.py:716
  6.5 21.5 %collective-permute-start = (bf16[128,768]{1,0:T(8,128)(2,1)S(1)}, bf16[128,768]{1,0:T(8,128)(2,1)S(1)}, u32[]{:S(2)}, u32[]{:S(2)}) collective-permute-start(bf16[128,768]{1,0:T(8,128)(2,1)S(1)} %get-tuple-element.120), channel_id=1, source_target_pairs={{0,2},{1,3},{2,0},{3,1},{4,6},{5,7},{6,4},{7,5},{8,10},{9,11},{10,... | collective-permute-start | bytes 589832 | tf_op jit(solution)/shard_map/ppermute | solution.py:716
  11.9 24.2 %collective-permute-start.28 = (f32[1,896]{1,0:T(1,128)S(1)}, f32[1,896]{1,0:T(1,128)S(1)}, u32[]{:S(2)}, u32[]{:S(2)}) collective-permute-start(f32[1,896]{1,0:T(1,128)S(1)} %broadcast_in_dim.86), channel_id=1, source_target_pairs={{0,2},{1,3},{2,0},{3,1},{4,6},{5,7},{6,4},{7,5},{8,10},{9,11},{10,... | collective-permute-start | bytes 10760 | tf_op jit(solution)/shard_map/ppermute | solution.py:716
  35.5 21.5 %collective-permute-start.3 = (bf16[512,768]{1,0:T(8,128)(2,1)}, bf16[512,768]{1,0:T(8,128)(2,1)S(1)}, u32[]{:S(2)}, u32[]{:S(2)}) collective-permute-start(bf16[512,768]{1,0:T(8,128)(2,1)} %get-tuple-element.46.k0_ref), channel_id=1, source_target_pairs={{0,1},{1,0},{2,3},{3,2},{4,5},{5,4},{6,7},{7,6},{8,9},{9,8},{10,11... | collective-permute-start | bytes 2359304 | tf_op jit(solution)/shard_map/ppermute | solution.py:716
  35.6 21.4 %collective-permute-start.4 = (bf16[512,768]{1,0:T(8,128)(2,1)}, bf16[512,768]{1,0:T(8,128)(2,1)S(1)}, u32[]{:S(2)}, u32[]{:S(2)}) collective-permute-start(bf16[512,768]{1,0:T(8,128)(2,1)} %get-tuple-element.47.v0_ref), channel_id=1, source_target_pairs={{0,1},{1,0},{2,3},{3,2},{4,5},{5,4},{6,7},{7,6},{8,9},{9,8},{10,11... | collective-permute-start | bytes 2359304 | tf_op jit(solution)/shard_map/ppermute | solution.py:716
  134.6 22.3 %collective-permute-start.23 = (f32[1,4352]{1,0:T(1,128)S(1)}, f32[1,4352]{1,0:T(1,128)S(1)}, u32[]{:S(2)}, u32[]{:S(2)}) collective-permute-start(f32[1,4352]{1,0:T(1,128)S(1)} %broadcast_in_dim.85), channel_id=1, source_target_pairs={{0,2},{1,3},{2,0},{3,1},{4,6},{5,7},{6,4},{7,5},{8,10},{9,11},{10,... | collective-permute-start | bytes 52232 | tf_op jit(solution)/shard_map/ppermute | solution.py:716
  137.1 30.2 %collective-permute-start.10 = (bf16[128,768]{1,0:T(8,128)(2,1)}, bf16[128,768]{1,0:T(8,128)(2,1)S(1)}, u32[]{:S(2)}, u32[]{:S(2)}) collective-permute-start(bf16[128,768]{1,0:T(8,128)(2,1)} %get-tuple-element.110), channel_id=1, source_target_pairs={{0,6},{1,7},{2,4},{3,5},{4,2},{5,3},{6,0},{7,1},{8,14},{9,15},{10,... | collective-permute-start | bytes 589832 | tf_op jit(solution)/shard_map/ppermute | solution.py:716
  138.9 29.6 %collective-permute-start.9 = (bf16[128,768]{1,0:T(8,128)(2,1)S(1)}, bf16[128,768]{1,0:T(8,128)(2,1)S(1)}, u32[]{:S(2)}, u32[]{:S(2)}) collective-permute-start(bf16[128,768]{1,0:T(8,128)(2,1)S(1)} %get-tuple-element.111), channel_id=1, source_target_pairs={{0,4},{1,5},{2,6},{3,7},{4,0},{5,1},{6,2},{7,3},{8,12},{9,13},{10,... | collective-permute-start | bytes 589832 | tf_op jit(solution)/shard_map/ppermute | solution.py:716
  140.1 29.8 %collective-permute-start.8 = (bf16[128,768]{1,0:T(8,128)(2,1)S(1)}, bf16[128,768]{1,0:T(8,128)(2,1)S(1)}, u32[]{:S(2)}, u32[]{:S(2)}) collective-permute-start(bf16[128,768]{1,0:T(8,128)(2,1)S(1)} %get-tuple-element.112), channel_id=1, source_target_pairs={{0,2},{1,3},{2,0},{3,1},{4,6},{5,7},{6,4},{7,5},{8,10},{9,11},{10,... | collective-permute-start | bytes 589832 | tf_op jit(solution)/shard_map/ppermute | solution.py:716
  156.8 65.9 %collective-permute-start.11 = (bf16[512,768]{1,0:T(8,128)(2,1)}, bf16[512,768]{1,0:T(8,128)(2,1)}, u32[]{:S(2)}, u32[]{:S(2)}) collective-permute-start(bf16[512,768]{1,0:T(8,128)(2,1)} %get-tuple-element.60), channel_id=1, source_target_pairs={{0,1},{1,0},{2,3},{3,2},{4,5},{5,4},{6,7},{7,6},{8,9},{9,8},{10,11... | collective-permute-start | bytes 2359304 | tf_op jit(solution)/shard_map/ppermute | solution.py:716
  165.3 36.6 %collective-permute-start.54 = (bf16[3,192,256]{2,1,0:T(8,128)(2,1)}, bf16[3,192,256]{2,1,0:T(8,128)(2,1)}, u32[]{:S(2)}, u32[]{:S(2)}) collective-permute-start(bf16[3,192,256]{2,1,0:T(8,128)(2,1)} %get-tuple-element.93), channel_id=1, source_target_pairs={{0,24},{1,25},{2,26},{3,27},{4,28},{5,29},{6,30},{7,31},{8,16},{9,... | collective-permute-start | bytes 884744 | tf_op jit(solution)/shard_map/ppermute | solution.py:716
  167.3 35.2 %collective-permute-start.53 = (bf16[3,192,256]{2,1,0:T(8,128)(2,1)}, bf16[3,192,256]{2,1,0:T(8,128)(2,1)}, u32[]{:S(2)}, u32[]{:S(2)}) collective-permute-start(bf16[3,192,256]{2,1,0:T(8,128)(2,1)} %get-tuple-element.94), channel_id=1, source_target_pairs={{0,16},{1,17},{2,18},{3,19},{4,20},{5,21},{6,22},{7,23},{8,24},{9,... | collective-permute-start | bytes 884744 | tf_op jit(solution)/shard_map/ppermute | solution.py:716
  168.5 34.1 %collective-permute-start.52 = (bf16[3,192,256]{2,1,0:T(8,128)(2,1)}, bf16[3,192,256]{2,1,0:T(8,128)(2,1)}, u32[]{:S(2)}, u32[]{:S(2)}) collective-permute-start(bf16[3,192,256]{2,1,0:T(8,128)(2,1)} %get-tuple-element.92), channel_id=1, source_target_pairs={{0,8},{1,9},{2,10},{3,11},{4,12},{5,13},{6,14},{7,15},{8,0},{9,1},... | collective-permute-start | bytes 884744 | tf_op jit(solution)/shard_map/ppermute | solution.py:716
  169.9 28.8 %collective-permute-start.26 = (f32[8,4352]{1,0:T(8,128)S(1)}, f32[8,4352]{1,0:T(8,128)}, u32[]{:S(2)}, u32[]{:S(2)}) collective-permute-start(f32[8,4352]{1,0:T(8,128)S(1)} %pad_maximum_fusion.13), channel_id=1, source_target_pairs={{0,16},{1,17},{2,18},{3,19},{4,20},{5,21},{6,22},{7,23},{8,24},{9,... | collective-permute-start | bytes 417800 | tf_op jit(solution)/shard_map/ppermute | solution.py:716
  202.0 20.7 %collective-permute-start.12 = (bf16[512,768]{1,0:T(8,128)(2,1)}, bf16[512,768]{1,0:T(8,128)(2,1)}, u32[]{:S(2)}, u32[]{:S(2)}) collective-permute-start(bf16[512,768]{1,0:T(8,128)(2,1)} %get-tuple-element.62), channel_id=1, source_target_pairs={{0,1},{1,0},{2,3},{3,2},{4,5},{5,4},{6,7},{7,6},{8,9},{9,8},{10,11... | collective-permute-start | bytes 2359304 | tf_op jit(solution)/shard_map/ppermute | solution.py:716
  205.8 14.8 %collective-permute-start.56 = (bf16[3,192,256]{2,1,0:T(8,128)(2,1)S(1)}, bf16[3,192,256]{2,1,0:T(8,128)(2,1)S(1)}, u32[]{:S(2)}, u32[]{:S(2)}) collective-permute-start(bf16[3,192,256]{2,1,0:T(8,128)(2,1)S(1)} %fusion.9), channel_id=1, source_target_pairs={{0,4},{1,5},{2,6},{3,7},{4,0},{5,1},{6,2},{7,3},{8,12},{9,13},{10,... | collective-permute-start | bytes 884744 | tf_op jit(solution)/shard_map/ppermute | solution.py:716
  214.8 37.6 %collective-permute-start.43 = (bf16[2,4,48,384]{3,2,1,0:T(8,128)(2,1)}, bf16[2,4,48,384]{3,2,1,0:T(8,128)(2,1)}, u32[]{:S(2)}, u32[]{:S(2)}) collective-permute-start(bf16[2,4,48,384]{3,2,1,0:T(8,128)(2,1)} %fusion.10), channel_id=1, source_target_pairs={{0,2},{1,3},{2,0},{3,1},{4,6},{5,7},{6,4},{7,5},{8,10},{9,11},{10,... | collective-permute-start | bytes 884744 | tf_op jit(solution)/shard_map/ppermute | solution.py:716
  244.9 15.6 %collective-permute-start.15 = (bf16[128,768]{1,0:T(8,128)(2,1)}, bf16[128,768]{1,0:T(8,128)(2,1)}, u32[]{:S(2)}, u32[]{:S(2)}) collective-permute-start(bf16[128,768]{1,0:T(8,128)(2,1)} %get-tuple-element.102), channel_id=1, source_target_pairs={{0,6},{1,7},{2,4},{3,5},{4,2},{5,3},{6,0},{7,1},{8,14},{9,15},{10,... | collective-permute-start | bytes 589832 | tf_op jit(solution)/shard_map/ppermute | solution.py:716
  246.4 14.8 %collective-permute-start.14 = (bf16[128,768]{1,0:T(8,128)(2,1)}, bf16[128,768]{1,0:T(8,128)(2,1)}, u32[]{:S(2)}, u32[]{:S(2)}) collective-permute-start(bf16[128,768]{1,0:T(8,128)(2,1)} %get-tuple-element.103), channel_id=1, source_target_pairs={{0,4},{1,5},{2,6},{3,7},{4,0},{5,1},{6,2},{7,3},{8,12},{9,13},{10,... | collective-permute-start | bytes 589832 | tf_op jit(solution)/shard_map/ppermute | solution.py:716
  247.2 14.1 %collective-permute-start.13 = (bf16[128,768]{1,0:T(8,128)(2,1)}, bf16[128,768]{1,0:T(8,128)(2,1)}, u32[]{:S(2)}, u32[]{:S(2)}) collective-permute-start(bf16[128,768]{1,0:T(8,128)(2,1)} %get-tuple-element.104), channel_id=1, source_target_pairs={{0,2},{1,3},{2,0},{3,1},{4,6},{5,7},{6,4},{7,5},{8,10},{9,11},{10,... | collective-permute-start | bytes 589832 | tf_op jit(solution)/shard_map/ppermute | solution.py:716
  252.4 29.5 %collective-permute-start.32 = (bf16[2,2,4,48,1152]{4,3,2,1,0:T(8,128)(2,1)S(1)}, bf16[2,2,4,48,1152]{4,3,2,1,0:T(8,128)(2,1)}, u32[]{:S(2)}, u32[]{:S(2)}) collective-permute-start(bf16[2,2,4,48,1152]{4,3,2,1,0:T(8,128)(2,1)S(1)} %copy_bitcast_fusion), channel_id=1, source_target_pairs={{0,1},{1,0},{2,3},{3,2},{4,5},{5,4},{6,7},{7,6},{8,9},{9,8},{10,11... | collective-permute-start | bytes 5308424 | tf_op jit(solution)/shard_map/ppermute | solution.py:716
  259.4 74.6 %collective-permute-start.58 = (bf16[4,3,192,256]{3,2,1,0:T(8,128)(2,1)}, bf16[4,3,192,256]{3,2,1,0:T(8,128)(2,1)}, u32[]{:S(2)}, u32[]{:S(2)}) collective-permute-start(bf16[4,3,192,256]{3,2,1,0:T(8,128)(2,1)} %get-tuple-element.86), channel_id=1, source_target_pairs={{0,1},{1,0},{2,3},{3,2},{4,5},{5,4},{6,7},{7,6},{8,9},{9,8},{10,11... | collective-permute-start | bytes 3538952 | tf_op jit(solution)/shard_map/ppermute | solution.py:716
  269.5 21.9 %collective-permute-start.47 = (bf16[48,384]{1,0:T(8,128)(2,1)}, bf16[48,384]{1,0:T(8,128)(2,1)}, u32[]{:S(2)}, u32[]{:S(2)}) collective-permute-start(bf16[48,384]{1,0:T(8,128)(2,1)} %get-tuple-element.143), channel_id=1, source_target_pairs={{0,24},{1,25},{2,26},{3,27},{4,28},{5,29},{6,30},{7,31},{8,16},{9,... | collective-permute-start | bytes 110600 | tf_op jit(solution)/shard_map/ppermute | solution.py:716
  271.2 20.1 %collective-permute-start.46 = (bf16[48,384]{1,0:T(8,128)(2,1)}, bf16[48,384]{1,0:T(8,128)(2,1)}, u32[]{:S(2)}, u32[]{:S(2)}) collective-permute-start(bf16[48,384]{1,0:T(8,128)(2,1)} %get-tuple-element.144), channel_id=1, source_target_pairs={{0,16},{1,17},{2,18},{3,19},{4,20},{5,21},{6,22},{7,23},{8,24},{9,... | collective-permute-start | bytes 110600 | tf_op jit(solution)/shard_map/ppermute | solution.py:716
  271.2 20.1 %collective-permute-start.45 = (bf16[48,384]{1,0:T(8,128)(2,1)}, bf16[48,384]{1,0:T(8,128)(2,1)S(1)}, u32[]{:S(2)}, u32[]{:S(2)}) collective-permute-start(bf16[48,384]{1,0:T(8,128)(2,1)} %get-tuple-element.142), channel_id=1, source_target_pairs={{0,8},{1,9},{2,10},{3,11},{4,12},{5,13},{6,14},{7,15},{8,0},{9,1},... | collective-permute-start | bytes 110600 | tf_op jit(solution)/shard_map/ppermute | solution.py:716
  283.5 21.2 %collective-permute-start.33 = (bf16[2,4,48,1152]{3,2,1,0:T(8,128)(2,1)S(1)}, bf16[2,4,48,1152]{3,2,1,0:T(8,128)(2,1)S(1)}, u32[]{:S(2)}, u32[]{:S(2)}) collective-permute-start(bf16[2,4,48,1152]{3,2,1,0:T(8,128)(2,1)S(1)} %fusion), channel_id=1, source_target_pairs={{0,4},{1,5},{2,6},{3,7},{4,0},{5,1},{6,2},{7,3},{8,12},{9,13},{10,... | collective-permute-start | bytes 2654216 | tf_op jit(solution)/shard_map/ppermute | solution.py:716
  292.3 16.6 %collective-permute-start.50 = (bf16[48,384]{1,0:T(8,128)(2,1)S(1)}, bf16[48,384]{1,0:T(8,128)(2,1)S(1)}, u32[]{:S(2)}, u32[]{:S(2)}) collective-permute-start(bf16[48,384]{1,0:T(8,128)(2,1)S(1)} %fusion.29), channel_id=1, source_target_pairs={{0,6},{1,7},{2,4},{3,5},{4,2},{5,3},{6,0},{7,1},{8,14},{9,15},{10,... | collective-permute-start | bytes 110600 | tf_op jit(solution)/shard_map/ppermute | solution.py:716
  294.1 14.8 %collective-permute-start.49 = (bf16[48,384]{1,0:T(8,128)(2,1)S(1)}, bf16[48,384]{1,0:T(8,128)(2,1)S(1)}, u32[]{:S(2)}, u32[]{:S(2)}) collective-permute-start(bf16[48,384]{1,0:T(8,128)(2,1)S(1)} %fusion.29), channel_id=1, source_target_pairs={{0,2},{1,3},{2,0},{3,1},{4,6},{5,7},{6,4},{7,5},{8,10},{9,11},{10,... | collective-permute-start | bytes 110600 | tf_op jit(solution)/shard_map/ppermute | solution.py:716
  295.3 13.7 %collective-permute-start.48 = (bf16[48,384]{1,0:T(8,128)(2,1)S(1)}, bf16[48,384]{1,0:T(8,128)(2,1)S(1)}, u32[]{:S(2)}, u32[]{:S(2)}) collective-permute-start(bf16[48,384]{1,0:T(8,128)(2,1)S(1)} %fusion.29), channel_id=1, source_target_pairs={{0,4},{1,5},{2,6},{3,7},{4,0},{5,1},{6,2},{7,3},{8,12},{9,13},{10,... | collective-permute-start | bytes 110600 | tf_op jit(solution)/shard_map/ppermute | solution.py:716
  309.1 12.1 %collective-permute-start.51 = (bf16[4,48,384]{2,1,0:T(8,128)(2,1)S(1)}, bf16[4,48,384]{2,1,0:T(8,128)(2,1)S(1)}, u32[]{:S(2)}, u32[]{:S(2)}) collective-permute-start(bf16[4,48,384]{2,1,0:T(8,128)(2,1)S(1)} %get-tuple-element.136), channel_id=1, source_target_pairs={{0,1},{1,0},{2,3},{3,2},{4,5},{5,4},{6,7},{7,6},{8,9},{9,8},{10,11... | collective-permute-start | bytes 442376 | tf_op jit(solution)/shard_map/ppermute | solution.py:716
  334.0 20.2 %collective-permute-start.41 = (bf16[4,48,1152]{2,1,0:T(8,128)(2,1)}, bf16[4,48,1152]{2,1,0:T(8,128)(2,1)}, u32[]{:S(2)}, u32[]{:S(2)}) collective-permute-start(bf16[4,48,1152]{2,1,0:T(8,128)(2,1)} %get-tuple-element.123), channel_id=1, source_target_pairs={{0,1},{1,0},{2,3},{3,2},{4,5},{5,4},{6,7},{7,6},{8,9},{9,8},{10,11... | collective-permute-start | bytes 1327112 | tf_op jit(solution)/shard_map/ppermute | solution.py:716
  (56 other events, 431.4 us)

commit v3 on v2

--- a/solution.py
+++ b/solution.py
@@ -488,8 +488,8 @@
 def feed_turn_kernel(
     h2_ref, h2t_ref, gf_ref, wg0, wg1, wu0, wu1, bg0, bg1, bu0, bu1, wd0, wd1,
     mid_ref, att_ref, dy_ref, mix_ref, mod_ref, weight_ref, dbias_ref,
-    out_ref, gmid_ref, gmix_ref, dw_ref, sums_ref, db_ref, total_ref,
-    feed_ref, gh_ref, made, paired, near, pair_send, pair_recv, near_send, near_recv,
+    out_ref, gmid_ref, gmix_ref, dw_ref, sums_ref, total_ref,
+    feed_ref, gh_ref, bias_ref, made, paired, near, pair_send, pair_recv, near_send, near_recv,
 ):
     place = Place()
     core = place.core
@@ -502,6 +502,7 @@
     @pl.when(step == 0)
     def _():
         feed_ref[...] = jnp.zeros_like(feed_ref)
+        sums_ref[1] = jnp.zeros((8, width), F32)
         gh_ref[...] = jnp.zeros_like(gh_ref)
         meet([place.pair(), place.plane(1), place.plane(2)])
 
@@ -540,7 +541,7 @@
             total = col_sum(grad.astype(F32))
             for i in range(2):
                 row = 16 * e + (2 * half + i) * 4 + place.flipped(owner)
-                db_ref[pl.ds(row, 1), :] = total[:, i * unit : (i + 1) * unit]
+                bias_ref[pl.ds(row, 1), :] = total[:, i * unit : (i + 1) * unit]
 
         @pl.when(step >= 2)
         def _():
@@ -603,13 +604,16 @@
         grad_middle = dy + back
         gmid_ref[...] = grad_middle
         grad_attended = (mod_ref[:, 2 * width : 3 * width] * grad_middle).astype(BF16)
-        sums_ref[0:1, :] = col_sum(grad_middle * att_ref[...].astype(F32))
-        sums_ref[1:2, :] = col_sum(grad_hidden)
-        sums_ref[2:3, :] = col_sum(product)
-        sums_ref[3:4, :] = col_sum(dy * feed)
-        sums_ref[4:5, :] = col_sum(grad_attended.astype(F32))
-        sums_ref[5:6, :] = col_sum(gf_ref[...].astype(F32))
-        sums_ref[6:8, :] = jnp.zeros((2, width), F32)
+        sums_ref[0, 0:1, :] = col_sum(grad_middle * att_ref[...].astype(F32))
+        sums_ref[0, 1:2, :] = col_sum(grad_hidden)
+        sums_ref[0, 2:3, :] = col_sum(product)
+        sums_ref[0, 3:4, :] = col_sum(dy * feed)
+        sums_ref[0, 4:5, :] = col_sum(grad_attended.astype(F32))
+        sums_ref[0, 5:6, :] = col_sum(gf_ref[...].astype(F32))
+        sums_ref[0, 6:8, :] = jnp.zeros((2, width), F32)
+        for row in range(32):
+            col = (row % 6) * unit
+            sums_ref[1, row // 6 : row // 6 + 1, col : col + unit] = bias_ref[row : row + 1, :]
         gmix_ref[...] = mm_nt(grad_attended, weight_ref[...]).astype(BF16)
         mixed_t = mix_ref[...].T
         dw_ref[0] = mm(mixed_t, grad_attended[:, :half]).astype(BF16)
@@ -655,8 +659,7 @@
     out_shape = [
         low, wide, low,
         jax.ShapeDtypeStruct((2, width, width // 2), BF16),
-        jax.ShapeDtypeStruct((8, width), F32),
-        jax.ShapeDtypeStruct((32, 128), F32),
+        jax.ShapeDtypeStruct((2, 8, width), F32),
         jax.ShapeDtypeStruct((4, 3, width // 4, 256), BF16),
     ]
     return pl.pallas_call(
@@ -673,6 +676,7 @@
         scratch_shapes=[
             pltpu.VMEM((rows, width), F32),
             pltpu.VMEM((rows, width), F32),
+            pltpu.VMEM((32, 128), F32),
             pltpu.VMEM((2, 2) + piece, BF16),
             pltpu.VMEM((8,) + piece, BF16),
             pltpu.VMEM((6,) + piece, BF16),
@@ -692,6 +696,456 @@
     )
 
 
+Z_FIRST = (False, False, False, False)
+GROUPS = 4
+
+
+def back_kernel(
+    head, q_ref, k0_ref, k1_ref, v0_ref, v1_ref, gm_ref, mix_ref, rl_ref, e_ref,
+    mod_ref, qgain_ref, kgain_ref, cos_ref, sin_ref, dout_ref, totals_ref, early_ref,
+    raw_hbm, hid_hbm, x_hbm, gmid_hbm, weight_hbm, rows_hbm,
+    output_ref, gtok_ref, feeds_hbm, projs_hbm, early_hbm, late_hbm,
+    feeds_ref, projs_ref, early_all, late_all, raw_ref, hid_ref, x_ref, gmid_ref, weight_ref, hidt_ref, gh_ref, gx_ref, late_ref,
+    dq_s, dk0_s, dv0_s, dk1_s, dv1_s, dk_in, dv_in,
+    made, paired, first_out, first_in, second_out, second_in, z_in, early_in, late_in,
+    load_sem, own_sem, kv_send, kv_recv, pair_send, pair_recv, first_send, first_recv,
+    second_send, second_recv, z_send, z_recv, tok_send, tok_recv, feed_send, feed_recv,
+    proj_send, proj_recv, small_send, small_recv,
+):
+    place = Place()
+    core, chip, z = place.core, place.chip, place.z
+    step = pl.program_id(0)
+    rows, width = x_ref.shape
+    cells = rows // 4
+    scale = head**-0.5
+    lane = lax.broadcasted_iota(jnp.int32, (1, 128), 1)
+
+    loads = [
+        pltpu.make_async_copy(source, target, load_sem.at[i])
+        for i, (source, target) in enumerate(
+            (
+                (hid_hbm, hid_ref), (raw_hbm, raw_ref), (weight_hbm, weight_ref),
+                (x_hbm, x_ref), (gmid_hbm, gmid_ref),
+            )
+        )
+    ]
+
+    stores = [
+        pltpu.make_async_copy(source, target, load_sem.at[5 + i])
+        for i, (source, target) in enumerate(
+            (
+                (early_all, early_hbm), (late_all, late_hbm), (feeds_ref, feeds_hbm),
+                (projs_ref, projs_hbm),
+            )
+        )
+    ]
+
+    def z_copy(d):
+        return send(
+            totals_ref.at[place.flipped_z(d)], z_in.at[d - 1], z_send.at[d - 1], z_recv.at[d - 1],
+            place.depth(d),
+        )
+
+    def token_copy(which, k):
+        source, target = ((rows_hbm, output_ref), (gx_ref, gtok_ref))[which]
+        return send(
+            source.at[pl.ds(k * cells, cells)], target.at[chip], tok_send.at[which, k - 1],
+            tok_recv.at[which, k - 1], place.plane(k),
+        )
+
+    def own_tokens(which):
+        source, target = ((rows_hbm, output_ref), (gx_ref, gtok_ref))[which]
+        return pltpu.make_async_copy(source.at[pl.ds(0, cells)], target.at[chip], own_sem.at[which])
+
+    def kv_copy(which, p):
+        source, target = ((dk1_s, dk_in), (dv1_s, dv_in))[which]
+        return send(
+            source.at[p], target.at[p], kv_send.at[which, p], kv_recv.at[which, p], place.pair()
+        )
+
+    def pair_copy(g):
+        source = dout_ref.at[1 - core] if g == 3 else made.at[g % 2, 1 - core]
+        return send(source, paired.at[g], pair_send.at[g], pair_recv.at[g], place.pair())
+
+    def first_copy(g, k):
+        other = place.flipped_z(k) if Z_FIRST[g] else place.flipped(k)
+        device = place.depth(k) if Z_FIRST[g] else place.plane(k)
+        return send(
+            first_out.at[g, other], first_in.at[g, k - 1], first_send.at[g, k - 1],
+            first_recv.at[g, k - 1], device,
+        )
+
+    def second_copy(g, k):
+        other = place.flipped(k) if Z_FIRST[g] else place.flipped_z(k)
+        device = place.plane(k) if Z_FIRST[g] else place.depth(k)
+        return send(
+            second_out.at[g, other], second_in.at[g, k - 1], second_send.at[g, k - 1],
+            second_recv.at[g, k - 1], device,
+        )
+
+    def feed_copy(k):
+        here = feeds_ref.at[core, chip]
+        return send(here, here, feed_send.at[k - 1], feed_recv.at[k - 1], place.plane(k))
+
+    def feed_pair():
+        here = feeds_ref.at[core]
+        return send(here, here, feed_send.at[3], feed_recv.at[3], place.pair())
+
+    def proj_copy(k):
+        here = projs_ref.at[core, chip]
+        return send(here, here, proj_send.at[k - 1], proj_recv.at[k - 1], place.plane(k))
+
+    def proj_pair():
+        here = projs_ref.at[core]
+        return send(here, here, proj_send.at[3], proj_recv.at[3], place.pair())
+
+    smalls = ((early_ref, early_in, early_all, 8), (late_ref, late_in, late_all, 4))
+    hops = [place.plane(1), place.plane(2), place.depth(1), place.depth(2)]
+
+    def small_pair(which):
+        source, target, _, count = smalls[which]
+        return send(
+            source.at[1 - core], target, small_send.at[which, 0], small_recv.at[which, 0],
+            place.pair(),
+        )
+
+    def small_hop(which, i):
+        _, _, full_ref, _ = smalls[which]
+        have = 1 << i
+        return send(
+            full_ref.at[core, pl.ds(0, have)], full_ref.at[core, pl.ds(have, have)],
+            small_send.at[which, 1 + i], small_recv.at[which, 1 + i], hops[i],
+        )
+
+    def small_last(which):
+        here = smalls[which][2].at[core]
+        return send(
+            here, here, small_send.at[which, 5], small_recv.at[which, 5], place.pair()
+        )
+
+    def small_begin(which):
+        source, target, full_ref, _ = smalls[which]
+        small_pair(which).wait_recv()
+        full_ref[core, 0] = source[core] + target[...]
+        small_hop(which, 0).start()
+
+    def small_next(which, i):
+        small_hop(which, i).wait_recv()
+        (small_hop(which, i + 1) if i < 3 else small_last(which)).start()
+
+    def start_group(g):
+        pair_copy(g).wait_recv()
+        mine = dout_ref.at[core] if g == 3 else made.at[g % 2, core]
+        part = width // 16
+        for a in range(4):
+            for b in range(4):
+                span = pl.ds((a * 4 + b) * part, part)
+                total = (mine[span, :].astype(F32) + paired[g, span].astype(F32)).astype(BF16)
+                if Z_FIRST[g]:
+                    first_out[g, a, b] = total
+                else:
+                    first_out[g, b, a] = total
+        for k in (1, 2, 3):
+            first_copy(g, k).start()
+
+    def go_on(g):
+        for k in (1, 2, 3):
+            first_copy(g, k).wait_recv()
+        here = z if Z_FIRST[g] else chip
+        second_out[g] = (
+            first_out[g, here].astype(F32)
+            + first_in[g, 0].astype(F32)
+            + first_in[g, 1].astype(F32)
+            + first_in[g, 2].astype(F32)
+        ).astype(BF16)
+        for k in (1, 2, 3):
+            second_copy(g, k).start()
+
+    def finish(g):
+        for k in (1, 2, 3):
+            second_copy(g, k).wait_recv()
+        here = chip if Z_FIRST[g] else z
+        projs_ref[core, chip, g] = (
+            second_out[g, here].astype(F32)
+            + second_in[g, 0].astype(F32)
+            + second_in[g, 1].astype(F32)
+            + second_in[g, 2].astype(F32)
+        ).astype(BF16)
+
+    @pl.when(step == 0)
+    def _():
+        for load in loads:
+            load.start()
+        meet(
+            [place.pair()]
+            + [place.plane(k) for k in (1, 2, 3)]
+            + [place.depth(d) for d in (1, 2, 3)]
+        )
+        pair_copy(3).start()
+        small_pair(0).start()
+        for d in (1, 2, 3):
+            z_copy(d).start()
+        for k in (1, 2, 3):
+            token_copy(0, k).start()
+        own_tokens(0).start()
+        gh_ref[...] = jnp.zeros_like(gh_ref)
+
+    @pl.when(step >= 1)
+    def _():
+        for which in (0, 1):
+            kv_copy(which, step - 1).start()
+
+    @pl.when(step == 3)
+    def _():
+        pair_copy(0).start()
+
+    @pl.when(step == 5)
+    def _():
+        pair_copy(1).start()
+
+    @pl.when(step < 6)
+    def _():
+        keys = jnp.concatenate([k0_ref[...], k1_ref[...]], axis=0)
+        values = jnp.concatenate([v0_ref[...], v1_ref[...]], axis=0)
+        scaled = gm_ref[...].astype(F32) * rl_ref[...]
+        products = scaled * mix_ref[...].astype(F32)
+        scaled = scaled.astype(BF16)
+        q_t = q_ref[...].T
+        scaled_t = scaled.T
+        dqs, dks, dvs = [], [], []
+        for h in range(2):
+            mine = (lane >= 64) if h else (lane < 64)
+            inner = jnp.sum(jnp.where(mine, products, 0.0), axis=1, keepdims=True)
+            grad_probs = mm_nt(jnp.where(mine, scaled, jnp.zeros_like(scaled)), values)
+            grown = e_ref[h]
+            grad_scores = (grown.astype(F32) * (grad_probs - inner) * scale).astype(BF16)
+            dqs.append(mm(grad_scores, keys))
+            dks.append(mm(q_t[64 * h : 64 * h + 64], grad_scores))
+            dvs.append(mm(scaled_t[64 * h : 64 * h + 64], grown))
+        dq_s[step] = jnp.where(lane < 64, dqs[0], dqs[1]).astype(BF16)
+        dk = jnp.concatenate(dks, axis=0).T.astype(BF16)
+        dv = jnp.concatenate(dvs, axis=0).T.astype(BF16)
+        dk0_s[step] = dk[:rows]
+        dk1_s[step] = dk[rows:]
+        dv0_s[step] = dv[:rows]
+        dv1_s[step] = dv[rows:]
+
+    @pl.when(step == 0)
+    def _():
+        loads[0].wait()
+        hidt_ref[...] = hid_ref[...].T
+
+    @pl.when(step == 1)
+    def _():
+        loads[1].wait()
+        loads[2].wait()
+        start_group(3)
+        small_begin(0)
+
+    for i in range(4):
+
+        @pl.when(step == 2 + i)
+        def _(i=i):
+            small_next(0, i)
+
+    @pl.when(step == 3)
+    def _():
+        start_group(0)
+
+    @pl.when(step == 5)
+    def _():
+        start_group(1)
+        go_on(3)
+
+    @pl.when(step == 6)
+    def _():
+        for d in (1, 2, 3):
+            z_copy(d).wait_recv()
+        for i in range(3):
+            feeds_ref[core, chip, i] = (
+                totals_ref[z, i].astype(F32)
+                + z_in[0, i].astype(F32)
+                + z_in[1, i].astype(F32)
+                + z_in[2, i].astype(F32)
+            ).astype(BF16)
+        for k in (1, 2, 3):
+            feed_copy(k).start()
+
+    @pl.when((step >= 2) & (lax.rem(step, 2) == 0))
+    def _():
+        g = (step - 2) // 2
+        slot = lax.rem(g, 2)
+        cosine, sine = cos_ref[...], -sin_ref[...]
+        for i in range(2):
+            for which in (0, 1):
+                kv_copy(which, 2 * g + i).wait_recv()
+
+        def both(ref):
+            return jnp.concatenate([ref[2 * g], ref[2 * g + 1]], axis=1).astype(F32)
+
+        lows = []
+        for part in range(3):
+            span = pl.ds(pl.multiple_of(part * width + g * 256, 256), 256)
+            if part == 2:
+                grad = both(dv0_s) + both(dv_in)
+            else:
+                grad = both(dq_s) if part == 0 else both(dk0_s) + both(dk_in)
+                gain = (qgain_ref, kgain_ref)[part][:, :256]
+                raw = raw_ref[:, span].astype(F32)
+                factor = lax.rsqrt(head_sum(raw * raw, head) * (1.0 / head) + NORM_EPSILON)
+                normed = raw * factor
+                turned = turn(grad, cosine, sine, head)
+                late_ref[1, part : part + 1, pl.ds(pl.multiple_of(g * 256, 256), 256)] = col_sum(
+                    turned * normed
+                )
+                turned = turned * gain
+                mean = head_sum(turned * normed, head) * (1.0 / head)
+                grad = factor * (turned - normed * mean)
+            low = grad.astype(BF16)
+            lows.append(low)
+            total = col_sum(low.astype(F32))
+            where = pl.ds(pl.multiple_of(g * 256, 256), 256)
+            if part < 2:
+                late_ref[0, 2 + part : 3 + part, where] = total
+            else:
+                late_ref[1, 2:3, where] = total
+            gh_ref[...] += mm_nt(low, weight_ref[:, span])
+        grads = jnp.concatenate(
+            [low[:, 128 * c : 128 * c + 128] for c in range(2) for low in lows], axis=1
+        )
+
+        @pl.when(step == 6)
+        def _():
+            pair_copy(0).wait_send()
+
+        half = width // 2
+        made[slot, 0] = mm(hidt_ref[...], grads[:, :half]).astype(BF16)
+        made[slot, 1] = mm(hidt_ref[...], grads[:, half:]).astype(BF16)
+
+    @pl.when(step == 6)
+    def _():
+        pair_copy(2).start()
+        go_on(0)
+        go_on(1)
+        loads[3].wait()
+        loads[4].wait()
+        grad_hidden = gh_ref[...]
+        x = x_ref[...].astype(F32)
+        factor = lax.rsqrt(jnp.mean(x * x, axis=-1, keepdims=True) + NORM_EPSILON)
+        normed = x * factor
+        late_ref[0, 0:1, :] = col_sum(grad_hidden)
+        late_ref[0, 1:2, :] = col_sum(grad_hidden * normed)
+        late_ref[1, 3:4, :] = jnp.zeros((1, width), F32)
+        grad_normed = grad_hidden * (1.0 + mod_ref[:, width : 2 * width])
+        back = factor * (
+            grad_normed - normed * jnp.mean(grad_normed * normed, axis=-1, keepdims=True)
+        )
+        small_pair(1).start()
+        start_group(2)
+        gx_ref[...] = (gmid_ref[...] + back).astype(BF16)
+        small_begin(1)
+        for k in (1, 2, 3):
+            token_copy(1, k).start()
+        own_tokens(1).start()
+        finish(3)
+        small_next(1, 0)
+        finish(0)
+        finish(1)
+        small_next(1, 1)
+        go_on(2)
+        small_next(1, 2)
+        for k in (1, 2, 3):
+            feed_copy(k).wait_recv()
+        for k in (1, 2, 3):
+            feed_copy(k).wait_send()
+        feed_pair().start()
+        finish(2)
+        for k in (1, 2, 3):
+            proj_copy(k).start()
+        small_next(1, 3)
+        for k in (1, 2, 3):
+            proj_copy(k).wait()
+        proj_pair().start()
+        for which in (0, 1):
+            own_tokens(which).wait()
+            for k in (1, 2, 3):
+                token_copy(which, k).wait()
+            small_pair(which).wait_send()
+            for i in range(4):
+                small_hop(which, i).wait_send()
+            small_last(which).wait()
+            stores[which].start()
+            for p in range(6):
+                kv_copy(which, p).wait_send()
+        for k in (1, 2, 3):
+            z_copy(k).wait_send()
+            for g in range(4):
+                first_copy(g, k).wait_send()
+                second_copy(g, k).wait_send()
+        for g in (1, 2, 3):
+            pair_copy(g).wait_send()
+        feed_pair().wait()
+        stores[2].start()
+        proj_pair().wait()
+        stores[3].start()
+        for store in stores:
+            store.wait()
+
+
+def back_call(
+    q, k0, k1, v0, v1, grad_mixed, mixed, inverse, grown, mod, qgain, kgain, cosine, sine, d_out,
+    totals, early, raw, hidden, x, grad_middle, weight, output_rows, head,
+):
+    rows, width = q.shape
+    half, part = width // 2, width // 16
+    low = lambda *shape: jax.ShapeDtypeStruct(shape, BF16)
+    pair = pl.BlockSpec((rows, 128), lambda s: (0, jnp.minimum(s, 5)))
+    anywhere = pl.BlockSpec(memory_space=pl.ANY)
+    small = [mod, qgain, kgain, cosine, sine, d_out, totals, early]
+    out_shape = [
+        low(4, rows // 4, width), low(4, rows // 4, width),
+        low(2, 4, 3, width // 4, 256), low(2, 4, GROUPS, part, half),
+        jax.ShapeDtypeStruct((2, 16, 8, width), F32), jax.ShapeDtypeStruct((2, 16, 4, width), F32),
+    ]
+    vmem = lambda *shape: pltpu.VMEM(shape, BF16)
+    sems = lambda *shape: pltpu.SemaphoreType.DMA(shape)
+    return pl.pallas_call(
+        functools.partial(back_kernel, head),
+        grid=(7,),
+        in_specs=[pair] * 8
+        + [pl.BlockSpec((2, rows, 2 * rows), lambda s: (jnp.minimum(s, 5), 0, 0))]
+        + [once(each.shape) for each in small]
+        + [anywhere] * 6,
+        out_specs=[anywhere] * 6,
+        out_shape=out_shape,
+        scratch_shapes=[pltpu.VMEM(shape.shape, shape.dtype) for shape in out_shape[2:]]
+        + [
+            vmem(rows, 2 * width), vmem(rows, width), vmem(rows, width),
+            pltpu.VMEM((rows, width), F32), vmem(width, 3 * width), vmem(width, rows),
+            pltpu.VMEM((rows, width), F32), vmem(rows, width), pltpu.VMEM((2, 4, width), F32),
+        ]
+        + [vmem(6, rows, 128)] * 7
+        + [
+            vmem(2, 2, width, half), vmem(GROUPS, width, half),
+            vmem(GROUPS, 4, 4, part, half), vmem(GROUPS, 3, 4, part, half),
+            vmem(GROUPS, 4, part, half), vmem(GROUPS, 3, part, half),
+            vmem(3, 3, width // 4, 256),
+            pltpu.VMEM((8, width), F32), pltpu.VMEM((4, width), F32),
+            sems(9), sems(2), sems(2, 6), sems(2, 6), sems(GROUPS), sems(GROUPS),
+            sems(GROUPS, 3), sems(GROUPS, 3), sems(GROUPS, 3), sems(GROUPS, 3),
+            sems(3), sems(3), sems(2, 3), sems(2, 3), sems(4), sems(4), sems(4), sems(4),
+            sems(2, 6), sems(2, 6),
+        ],
+        compiler_params=pltpu.CompilerParams(
+            vmem_limit_bytes=VMEM_LIMIT, collective_id=2, has_side_effects=True
+        ),
+        name="back",
+    )(
+        q, k0, k1, v0, v1, grad_mixed, mixed, inverse, grown, *small, raw, hidden, x, grad_middle,
+        weight, output_rows,
+    )
+
+
 def take(array_in, index, axis=0):
     return lax.dynamic_index_in_dim(array_in, index, axis, keepdims=False)
 
@@ -735,28 +1189,6 @@
 def regroup(parts, place):
     stacked = jnp.stack(parts)
     return jnp.stack([take(stacked, place ^ k) for k in range(len(parts))])
-
-
-def reduce_pieces(moves, pieces, c, first, second, order, z):
-    one, two = order
-    arrived = moves.pair(take(pieces, 1 - c))
-    mine = take(pieces, c)
-    near = moves.plane(add(take(mine, 1 - first), take(arrived, 1 - first)).astype(BF16), one)
-    mine, arrived = take(mine, first), take(arrived, first)
-    far = moves.plane(
-        add(take(mine, 1 - second), take(arrived, 1 - second), take(near, 1 - second)).astype(BF16),
-        two,
-    )
-    total = add(take(mine, second), take(arrived, second), take(near, second), far)
-    low = total.astype(BF16)
-    own = take(total, z)
-    for d in range(1, moves.sizes[0]):
-        own = add(own, moves.flip(take(low, z ^ d), batch=d))
-    own = own.astype(BF16)
-    quarter = [own, moves.plane(own, two), moves.plane(own, one), moves.plane(own, one ^ two)]
-    quarter = regroup(quarter, 2 * first + second)
-    halves = [quarter, moves.pair(quarter)]
-    return regroup(halves, c)
 
 
 def body(mesh, *operands):
@@ -832,9 +1264,38 @@
     blocks = hidden_width // unit
     quick = nb == 4 and hidden_width == 16 * 128
     if quick:
-        output_rows, grad_middle, grad_mixed, d_out, sums_two, gate_bias, totals = feed_turn_call(
+        output_rows, grad_middle, grad_mixed, d_out, sums_two, totals = feed_turn_call(
             hidden_two, hidden_two_t, grad_feed, gate_up_weight, gate_up_bias[None], down_weight,
             middle, attended, dy, mixed, mod, outproj_weight, down_bias[None],
+        )
+        output, grad_tokens, feeds, projs, early, late = back_call(
+            q, k0, k1, v0, v1, grad_mixed, mixed, inverse, grown, mod, qgain, kgain, cosine, sine,
+            d_out, totals, sums_two, raw, hidden_one, x, grad_middle, inproj_weight, output_rows,
+            head,
+        )
+        output = output.reshape(tokens.shape)
+        grad_tokens = grad_tokens.reshape(tokens.shape)
+        slice_rows = width // nb
+        gates = feeds[:, :, :2].reshape(2, 4, 2, slice_rows, 2, 128).transpose(3, 0, 2, 4, 1, 5)
+        grad_gu_w = gates.reshape(slice_rows, 2 * hidden_width).astype(F32)
+        downs = feeds[:, :, 2].reshape(2, 4, 3, 64, 256).transpose(1, 0, 3, 2, 4)
+        grad_down_w = downs.reshape(hidden_width // nb, width).astype(F32)
+        part = width // 16
+        ins = projs[:, :, :3].reshape(2, 4, 3, part, 3, 128).transpose(1, 3, 4, 2, 0, 5)
+        grad_in_w = ins.reshape(slice_rows, 3 * width).astype(F32)
+        outs = projs[:, :, 3].transpose(1, 2, 0, 3)
+        grad_out_w = outs.reshape(slice_rows, width).astype(F32)
+        count = early.shape[1]
+        early = jnp.concatenate(
+            [early[0, :, :6].reshape(count, -1), early[1].reshape(count, -1)[:, : 2 * hidden_width]],
+            axis=1,
+        )
+        gain_sums = late[1, :, :2].reshape(count, 2, heads, head).sum(axis=2)
+        late = jnp.concatenate(
+            [
+                late[0].reshape(count, -1), late[1, :, 2], gain_sums.reshape(count, -1),
+            ],
+            axis=1,
         )
     else:
         feed, grad_hidden, d_down, d_gate, d_bias = feed_call(
@@ -846,46 +1307,23 @@
             down_bias[None],
         )
         gate_bias = d_bias.reshape(blocks, 2, unit).transpose(1, 0, 2)
-    dq, dk0, dk1, dv0, dv1 = attend_back_call(
-        q, k0, k1, v0, v1, grown, grad_mixed, mixed, inverse, head
-    )
-    dk1, dv1 = moves.pair(dk1), moves.pair(dv1)
-    grad_x, d_in, sums_one, in_bias = project_back_call(
-        dq, dk0, dk1, dv0, dv1, raw, hidden_one, x, grad_middle, mod, inproj_weight, qgain, kgain,
-        cosine, sine, head,
-    )
-
-    def give_back(rows_out):
-        parts = rows_out.reshape(4, cells, width)
-        got = [parts[0]] + [moves.plane(parts[k], k) for k in range(1, 4)]
-        return regroup(got, place).reshape(tokens.shape)
-
-    output = give_back(output_rows)
-    grad_tokens = give_back(grad_x)
-
-    slice_rows = width // nb
-    if quick:
-        own = take(totals, z).astype(F32)
-        for d in range(1, nb):
-            own = add(own, moves.flip(take(totals, z ^ d), batch=d))
-        own = own.astype(BF16)
-        own = regroup([own] + [moves.plane(own, k) for k in range(1, 4)], place)
-        own = regroup([own, moves.pair(own)], core)
-        gates = own[:, :, :2].reshape(2, 4, 2, slice_rows, 2, 128).transpose(3, 0, 2, 4, 1, 5)
-        grad_gu_w = gates.reshape(slice_rows, 2 * hidden_width).astype(F32)
-        downs = own[:, :, 2].reshape(2, 4, 3, 64, 256).transpose(1, 0, 3, 2, 4)
-        grad_down_w = downs.reshape(hidden_width // nb, width).astype(F32)
-
-        def by_rows(d, order, first, second):
-            wide = d.shape[2]
-            d = d.reshape(2, nb, 2, 2, slice_rows // 4, wide).transpose(0, 2, 3, 1, 4, 5)
-            d = reduce_pieces(moves, d, core, first, second, order, z)
-            d = d.reshape(2, slice_rows, wide)
-            return jnp.concatenate([d[0], d[1]], axis=1).astype(F32)
-
-        grad_out_w = by_rows(d_out, (1, 2), side, gy)
-        grad_in_w = by_rows(d_in, (2, 1), gy, side)
-    else:
+        dq, dk0, dk1, dv0, dv1 = attend_back_call(
+            q, k0, k1, v0, v1, grown, grad_mixed, mixed, inverse, head
+        )
+        dk1, dv1 = moves.pair(dk1), moves.pair(dv1)
+        grad_x, d_in, sums_one, in_bias = project_back_call(
+            dq, dk0, dk1, dv0, dv1, raw, hidden_one, x, grad_middle, mod, inproj_weight, qgain,
+            kgain, cosine, sine, head,
+        )
+
+        def give_back(rows_out):
+            parts = rows_out.reshape(4, cells, width)
+            got = [parts[0]] + [moves.plane(parts[k], k) for k in range(1, 4)]
+            return regroup(got, place).reshape(tokens.shape)
+
+        output = give_back(output_rows)
+        grad_tokens = give_back(grad_x)
+        slice_rows = width // nb
 
         def scatter(d):
             d = lax.psum_scatter(d.astype(BF16), "batch", scatter_dimension=0, tiled=True)
@@ -900,10 +1338,11 @@
         )
         grad_out_w = scatter(joined(d_out))
         grad_in_w = scatter(joined(d_in))
-
-    gain_sums = sums_one[2:4].reshape(2, heads, head).sum(axis=1)
-    early = jnp.concatenate([sums_two[:6].reshape(-1), gate_bias.reshape(-1)])
-    late = jnp.concatenate([sums_one[:2].reshape(-1), in_bias.reshape(-1), gain_sums.reshape(-1)])
+        gain_sums = sums_one[2:4].reshape(2, heads, head).sum(axis=1)
+        early = jnp.concatenate([sums_two[:6].reshape(-1), gate_bias.reshape(-1)])
+        late = jnp.concatenate(
+            [sums_one[:2].reshape(-1), in_bias.reshape(-1), gain_sums.reshape(-1)]
+        )
 
     def everywhere(vector):
         halves = vector.reshape(2, -1)
@@ -914,8 +1353,8 @@
 
     known = jnp.concatenate([condition, jnp.broadcast_to(label.astype(F32), (128,))])
     known = moves.gather(known)
-    early = everywhere(early)
-    late = everywhere(late)
+    if not quick:
+        early, late = everywhere(early), everywhere(late)
     grad_modulation = jnp.concatenate([late[:, : 2 * width], early[:, : 4 * width]], axis=1)
     conditions = known[:, :width]
     all_labels = known[:, width].astype(jnp.int32)

time: 364 us -> 278 us (0.76); the launches traced: 357 us -> 277 us
  waiting for transfers between devices: 82.2 us -> 6.95 us
  Pallas kernels: 116 us -> 178 us
  starting transfers between devices: 60 us -> 16.6 us
  other arithmetic: 38.4 us -> 11.7 us
    ppermute x59 -> x12, waiting for transfers between devices: 82.2 us -> 6.95 us  [flip(): return lax.ppermute(value, AXES, pairs)]
    pallas_call x2 -> x1, Pallas kernels: 29.3 us -> 92.8 us  [back_call(): pl.pallas_call(functools.partial(back_kernel, head), grid=(7,), in_specs=...]
    ppermute x59 -> x12, starting transfers between devices: 60 us -> 16.6 us  [flip(): return lax.ppermute(value, AXES, pairs)]
    convert_element_type x11 -> x2, other arithmetic: 14.2 us -> 2.19 us  [the longest x1 1.33 us: body(): grad_in_w = ins.reshape(slice_rows, 3 * width).astype(F32)]
    convert_element_type x0 -> x4, local copies, waits for them, and re-layouts: none -> 9.25 us  [the longest x3 8.8 us: body(): grad_in_w = ins.reshape(slice_rows, 3 * width).astype(F32)]
    another operation x10 -> x0, other arithmetic: 8.61 us -> none  [regroup(): stacked = jnp.stack(parts)]
    unnamed x60 -> x52, local copies, waits for them, and re-layouts: 5.59 us -> 7.66 us
  transfers between devices with their start and end apart: 59 -> 12, of which waited for: 23 -> 4; matrix products, arithmetic and copies ran while one was open for 24% -> 5% of each run, Pallas kernels for 12% -> 5%
where the time goes in v3:
time: 278 us; the launch traced here: 277 us
  Pallas kernels  178 us (64%)
  local copies, waits for them, and re-layouts  46.5 us (17%)
  starting transfers between devices  16.6 us (6%)
  matrix products  12.2 us (4%)
  other arithmetic  11.7 us (4%)
  waiting for transfers between devices  6.95 us (2%)
  between operations  4.53 us (2%)
    pallas_call x1, Pallas kernels, back_call(): pl.pallas_call(functools.partial(back_kernel, head), grid=(7,), in_specs=...  92.8 us
    pallas_call x1, Pallas kernels, feed_turn_call(): pl.pallas_call(feed_turn_kernel, grid=(9,), in_specs=[once((rows, width))...  56.2 us
    ppermute x12, starting transfers between devices, flip(): return lax.ppermute(value, AXES, pairs)  16.6 us
    pallas_call x1, Pallas kernels, attend_call(): pl.pallas_call(functools.partial(attend_kernel, head ** (-0.5)), grid=(wi...  11.9 us
    convert_element_type x3, local copies, waits for them, and re-layouts, body(): grad_gu_w = gates.reshape(slice_rows, 2 * hidden_width).astype(F32)  9.74 us
    convert_element_type x3, local copies, waits for them, and re-layouts, body(): grad_in_w = ins.reshape(slice_rows, 3 * width).astype(F32)  8.8 us
    unnamed x52, local copies, waits for them, and re-layouts  7.66 us
    ppermute x12, waiting for transfers between devices, flip(): return lax.ppermute(value, AXES, pairs)  6.95 us
  transfers between devices with their start and end apart: 12, of which 4 were waited for; matrix products, arithmetic and copies ran while one was open for 5% of the time, Pallas kernels for 5%

profile of v3, /device:TPU:0, one launch (start us, length us, event | category | flops | bytes accessed | tf_op | source)
XLA Modules:
  0.0 276.7 jit_solution(11483347275250105636)
XLA Ops:
  0.7 1.3 dynamic-slice_bitcast_fusion.7
  2.0 3.1 %collective-permute-start = (bf16[128,768]{1,0:T(8,128)(2,1)S(1)}, bf16[128,768]{1,0:T(8,128)(2,1)S(1)}, u32[]{:S(2)}, u32[]{:S(2)}) collective-permute-start(bf16[128,768]{1,0:T(8,128)(2,1)S(1)} %get-tuple-element.73), channel_id=1, source_target_pairs={{0,2},{1,3},{2,0},{3,1},{4,6},{5,7},{6,4},{7,5},{8,10},{9,11},{10,... | collective-permute-start | bytes 589832 | tf_op jit(solution)/shard_map/ppermute | solution.py:1170
  5.1 1.5 collective-permute-start.1
  11.9 2.0 collective-permute-start.8
  14.8 1.8 sine_multiply_fusion
  18.1 6.4 %modulation.1 = f32[16,4608]{1,0:T(8,128)} custom-call(bf16[16,768]{1,0:T(8,128)(2,1)} %broadcast_in_dim.67.act_ref, bf16[768,4608]{1,0:T(8,128)(2,1)} %weight_ref.4, bf16[1,4608]{1,0:T(2,128)(2,1)} %broadcast_in_dim.68.bias_ref), custom_call_target="tpu_custom_call" | custom-call | tf_op jit(solution)/shard_map/modulation/pallas_call | solution.py:49
  24.5 1.5 slice.68.mod_ref
  28.0 1.6 collective-permute-start.9
  30.5 6.5 %project.1 = (bf16[512,768]{1,0:T(8,128)(2,1)}, bf16[512,768]{1,0:T(8,128)(2,1)}, bf16[512,768]{1,0:T(8,128)(2,1)}, bf16[512,768]{1,0:T(8,128)(2,1)}, bf16[512,1536]{1,0:T(8,128)(2,1)}) custom-call(bf16[512,768]{1,0:T(8,128)(2,1)} %pad_maximum_fusion.x_ref.x_hbm, f32[1,4608]{1,0:T(1,128)} %slice.68.mod_ref, bf16[768,2304]{1,0:T(8,128)(2,1)} %weight_hbm.1, ...), custom_call_target="tpu_custom_call" | custom-call | tf_op jit(solution)/shard_map/project/pallas_call | solution.py:114
  37.6 1.6 collective-permute-start.10
  39.3 2.1 collective-permute-done.10
  41.5 2.6 collective-permute-start.11
  47.1 2.4 collective-permute-start.7
  52.1 3.0 %collective-permute-done.7 = bf16[128,768]{1,0:T(8,128)(2,1)S(1)} collective-permute-done((bf16[128,768]{1,0:T(8,128)(2,1)S(1)}, bf16[128,768]{1,0:T(8,128)(2,1)S(1)}, u32[]{:S(2)}, u32[]{:S(2)}) %collective-permute-start.7) | collective-permute-done | bytes 196640 | tf_op jit(solution)/shard_map/ppermute | solution.py:1170
  57.2 11.9 %attend.1 = (bf16[512,768]{1,0:T(8,128)(2,1)}, bf16[12,512,1024]{2,1,0:T(8,128)(2,1)}, f32[512,768]{1,0:T(8,128)}) custom-call(bf16[512,768]{1,0:T(8,128)(2,1)} %get-tuple-element.41.q_ref, bf16[512,768]{1,0:T(8,128)(2,1)} %get-tuple-element.42.k0_ref, bf16[512,768]{1,0:T(8,128)(2,1)} %copy-done.1, bf16[512,768]{1,0:T(8,128)(2,1)} %get-tuple-element.43.v0_ref, ...), custom_call_target="tpu_custom_call" | custom-call | tf_op jit(solution)/shard_map/attend/pallas_call | solution.py:155
  69.2 4.4 %middle.1 = (bf16[512,768]{1,0:T(8,128)(2,1)}, f32[512,768]{1,0:T(8,128)}, bf16[512,768]{1,0:T(8,128)(2,1)}, bf16[768,512]{1,0:T(8,128)(2,1)}, bf16[512,768]{1,0:T(8,128)(2,1)}) custom-call(bf16[512,768]{1,0:T(8,128)(2,1)} %get-tuple-element.44.mix_ref, bf16[512,768]{1,0:T(8,128)(2,1)} %pad_maximum_fusion.x_ref.x_hbm, ...), custom_call_target="tpu_custom_call" | custom-call | tf_op jit(solution)/shard_map/middle/pallas_call | solution.py:239
  73.6 56.2 %feed_turn.1 = (bf16[512,768]{1,0:T(8,128)(2,1)}, f32[512,768]{1,0:T(8,128)}, bf16[512,768]{1,0:T(8,128)(2,1)}, bf16[2,768,384]{2,1,0:T(8,128)(2,1)}, f32[2,8,76...) custom-call(bf16[512,768]{1,0:T(8,128)(2,1)} %get-tuple-element.45.h2_ref, bf16[768,512]{1,0:T(8,128)(2,1)} %get-tuple-element.46.h2t_ref, ...), custom_call_target="tpu_custom_call" | custom-call | tf_op jit(solution)/shard_map/feed_turn/pallas_call | solution.py:665
  129.8 92.8 %back.1 = (bf16[4,128,768]{2,1,0:T(8,128)(2,1)}, bf16[4,128,768]{2,1,0:T(8,128)(2,1)}, bf16[2,4,3,192,256]{4,3,2,1,0:T(8,128)(2,1)}, bf16[2,4,4,48,384]{4,3,2,1,...) custom-call(bf16[512,768]{1,0:T(8,128)(2,1)} %get-tuple-element.41.q_ref, ...), custom_call_target="tpu_custom_call" | custom-call | tf_op jit(solution)/shard_map/back/pallas_call | solution.py:1112
  227.0 5.7 %add_multiply_fusion = f32[16,768]{1,0:T(8,128)} fusion(bf16[768,4608]{1,0:T(8,128)(2,1)} %weight_ref.4, f32[16,3072]{1,0:T(8,128)S(1)} %slice.70, f32[16,1536]{1,0:T(8,128)S(1)} %slice.69, f32[16,896]{1,0:T(8,128)S(1)} %concatenate.64), kind=kOutput, calls=%fused_computation.25 | convolution fusion | flops 113639424 | bytes 7471104 | tf_op jit(solution)/shard_map/dot_general | solution.py:23
  234.6 1.3 slice_convert_fusion.1
  240.3 3.0 %reshape.188 = f32[2,4,2,192,2,128]{5,4,3,2,1,0:T(2,128)} reshape(f32[2,4,2,192,256]{4,3,2,1,0:T(8,128)S(1)} %slice_convert_fusion) | data formatting | bytes 6291456 | tf_op jit(solution)/shard_map/convert_element_type | solution.py:1280
  243.3 3.9 %copy.54 = f32[192,2,2,2,4,128]{5,4,3,2,1,0:T(4,128)S(1)} copy(f32[192,2,2,2,4,128]{5,3,0,2,4,1:T(2,128)} %bitcast.60) | data formatting | bytes 6291456 | tf_op jit(solution)/shard_map/convert_element_type | solution.py:1280
  247.2 2.8 %reshape.184 = f32[192,4096]{1,0:T(8,128)} reshape(f32[192,2,2,2,4,128]{5,4,3,2,1,0:T(4,128)S(1)} %copy.54) | data formatting | bytes 6291456 | tf_op jit(solution)/shard_map/convert_element_type | solution.py:1280
  250.0 2.7 reshape.186
  252.7 2.6 copy.50
  255.3 3.6 %reshape.182 = f32[192,2304]{1,0:T(8,128)} reshape(f32[4,48,3,3,2,128]{5,4,3,2,1,0:T(2,128)} %copy.50) | data formatting | bytes 3538944 | tf_op jit(solution)/shard_map/convert_element_type | solution.py:1285
  258.9 3.1 %fusion.3 = f32[1001,768]{1,0:T(8,128)} fusion(f32[16,768]{1,0:T(8,128)S(1)} %copy-done.12, s32[16]{0:T(128)S(1)} %fusion.12), kind=kOutput, calls=%fused_computation.23 | convolution fusion | flops 147619472 | bytes 3124288 | tf_op jit(solution)/shard_map/dot_general | solution.py:1374
  262.7 1.5 copy.61
  265.6 1.4 dynamic_slice.94
  266.9 1.4 fusion.27
  269.6 1.4 dynamic_slice.89
  271.0 3.3 %fusion.5 = f32[192,4608]{1,0:T(8,128)} fusion(f32[16,3072]{1,0:T(8,128)S(1)} %slice.70, f32[16,1536]{1,0:T(8,128)S(1)} %slice.69, f32[16,768]{1,0:T(8,128)} %get-tuple-element.75, s32[]{:T(128)S(6)} %select_n.199, f32[16,768]{1,0:T(8,128)} %get-tuple-element.74), kind=kOutput, calls=%fused_computation.29 | convolution fusion | flops 28612608 | bytes 3866628 | tf_op jit(solution)/shard_map/dot_general | solution.py:27
  (132 shorter events, 31.5 us)
Async XLA Ops:
  0.6 6.0 %copy-start.20 = (s32[4]{0:T(128)S(1)}, s32[4]{0:T(128)}, u32[]{:S(2)}) copy-start(s32[4]{0:T(128)} %param.19) | copy-start | bytes 52
  0.7 8.5 %copy-start.21 = (s32[4]{0:T(128)S(1)}, s32[4]{0:T(128)}, u32[]{:S(2)}) copy-start(s32[4]{0:T(128)} %param.18) | copy-start | bytes 52
  0.7 13.5 %copy-start.13 = (bf16[4608]{0:T(1024)(128)(2,1)S(1)}, bf16[4608]{0:T(1024)(128)(2,1)}, u32[]{:S(2)}) copy-start(bf16[4608]{0:T(1024)(128)(2,1)} %param.22) | copy-start | bytes 27652
  2.0 27.5 %collective-permute-start = (bf16[128,768]{1,0:T(8,128)(2,1)S(1)}, bf16[128,768]{1,0:T(8,128)(2,1)S(1)}, u32[]{:S(2)}, u32[]{:S(2)}) collective-permute-start(bf16[128,768]{1,0:T(8,128)(2,1)S(1)} %get-tuple-element.73), channel_id=1, source_target_pairs={{0,2},{1,3},{2,0},{3,1},{4,6},{5,7},{6,4},{7,5},{8,10},{9,11},{10,... | collective-permute-start | bytes 589832 | tf_op jit(solution)/shard_map/ppermute | solution.py:1170
  5.1 24.5 %collective-permute-start.1 = (bf16[128,768]{1,0:T(8,128)(2,1)S(1)}, bf16[128,768]{1,0:T(8,128)(2,1)S(1)}, u32[]{:S(2)}, u32[]{:S(2)}) collective-permute-start(bf16[128,768]{1,0:T(8,128)(2,1)S(1)} %get-tuple-element.72), channel_id=1, source_target_pairs={{0,4},{1,5},{2,6},{3,7},{4,0},{5,1},{6,2},{7,3},{8,12},{9,13},{10,... | collective-permute-start | bytes 589832 | tf_op jit(solution)/shard_map/ppermute | solution.py:1170
  6.6 23.0 %collective-permute-start.2 = (bf16[128,768]{1,0:T(8,128)(2,1)S(1)}, bf16[128,768]{1,0:T(8,128)(2,1)S(1)}, u32[]{:S(2)}, u32[]{:S(2)}) collective-permute-start(bf16[128,768]{1,0:T(8,128)(2,1)S(1)} %get-tuple-element.71), channel_id=1, source_target_pairs={{0,6},{1,7},{2,4},{3,5},{4,2},{5,3},{6,0},{7,1},{8,14},{9,15},{10,... | collective-permute-start | bytes 589832 | tf_op jit(solution)/shard_map/ppermute | solution.py:1170
  11.9 16.1 %collective-permute-start.8 = (f32[1,896]{1,0:T(1,128)S(1)}, f32[1,896]{1,0:T(1,128)S(1)}, u32[]{:S(2)}, u32[]{:S(2)}) collective-permute-start(f32[1,896]{1,0:T(1,128)S(1)} %broadcast_in_dim.78), channel_id=1, source_target_pairs={{0,2},{1,3},{2,0},{3,1},{4,6},{5,7},{6,4},{7,5},{8,10},{9,11},{10,... | collective-permute-start | bytes 10760 | tf_op jit(solution)/shard_map/ppermute | solution.py:1170
  18.1 8.0 %copy-start.18 = (bf16[64]{0:T(256)(128)(2,1)S(1)}, bf16[64]{0:T(256)(128)(2,1)}, u32[]{:S(2)}) copy-start(bf16[64]{0:T(256)(128)(2,1)} %param.25) | copy-start | bytes 388
  18.1 8.6 %copy-start.19 = (bf16[64]{0:T(256)(128)(2,1)S(1)}, bf16[64]{0:T(256)(128)(2,1)}, u32[]{:S(2)}) copy-start(bf16[64]{0:T(256)(128)(2,1)} %param.26) | copy-start | bytes 388
  18.1 9.3 %copy-start.15 = (bf16[2304]{0:T(1024)(128)(2,1)S(1)}, bf16[2304]{0:T(1024)(128)(2,1)}, u32[]{:S(2)}) copy-start(bf16[2304]{0:T(1024)(128)(2,1)} %param.24) | copy-start | bytes 13828
  28.0 9.7 %collective-permute-start.9 = (f32[2,896]{1,0:T(2,128)S(1)}, f32[2,896]{1,0:T(2,128)S(1)}, u32[]{:S(2)}, u32[]{:S(2)}) collective-permute-start(f32[2,896]{1,0:T(2,128)S(1)} %pad_maximum_fusion.6), channel_id=1, source_target_pairs={{0,4},{1,5},{2,6},{3,7},{4,0},{5,1},{6,2},{7,3},{8,12},{9,13},{10,... | collective-permute-start | bytes 21512 | tf_op jit(solution)/shard_map/ppermute | solution.py:1170
  30.5 13.6 %copy-start.8 = (bf16[4,16,8,768]{3,2,1,0:T(8,128)(2,1)S(1)}, bf16[4,16,8,768]{3,2,1,0:T(8,128)(2,1)}, u32[]{:S(2)}) copy-start(bf16[4,16,8,768]{3,2,1,0:T(8,128)(2,1)} %param.33) | copy-start | bytes 2359300
  37.0 8.3 %copy-start.16 = (bf16[768]{0:T(1024)(128)(2,1)S(1)}, bf16[768]{0:T(1024)(128)(2,1)}, u32[]{:S(2)}) copy-start(bf16[768]{0:T(1024)(128)(2,1)} %param.28) | copy-start | bytes 4612
  37.0 8.8 %copy-start.14 = (bf16[4096]{0:T(1024)(128)(2,1)S(1)}, bf16[4096]{0:T(1024)(128)(2,1)}, u32[]{:S(2)}) copy-start(bf16[4096]{0:T(1024)(128)(2,1)} %param.30) | copy-start | bytes 24580
  37.0 9.4 %copy-start.17 = (bf16[768]{0:T(1024)(128)(2,1)S(1)}, bf16[768]{0:T(1024)(128)(2,1)}, u32[]{:S(2)}) copy-start(bf16[768]{0:T(1024)(128)(2,1)} %param.32) | copy-start | bytes 4612
  37.1 19.0 %collective-permute-start.3 = (bf16[512,768]{1,0:T(8,128)(2,1)}, bf16[512,768]{1,0:T(8,128)(2,1)S(1)}, u32[]{:S(2)}, u32[]{:S(2)}) collective-permute-start(bf16[512,768]{1,0:T(8,128)(2,1)} %get-tuple-element.42.k0_ref), channel_id=1, source_target_pairs={{0,1},{1,0},{2,3},{3,2},{4,5},{5,4},{6,7},{7,6},{8,9},{9,8},{10,11... | collective-permute-start | bytes 2359304 | tf_op jit(solution)/shard_map/ppermute | solution.py:1170
  37.1 18.9 %collective-permute-start.4 = (bf16[512,768]{1,0:T(8,128)(2,1)}, bf16[512,768]{1,0:T(8,128)(2,1)S(1)}, u32[]{:S(2)}, u32[]{:S(2)}) collective-permute-start(bf16[512,768]{1,0:T(8,128)(2,1)} %get-tuple-element.43.v0_ref), channel_id=1, source_target_pairs={{0,1},{1,0},{2,3},{3,2},{4,5},{5,4},{6,7},{7,6},{8,9},{9,8},{10,11... | collective-permute-start | bytes 2359304 | tf_op jit(solution)/shard_map/ppermute | solution.py:1170
  37.6 3.8 %collective-permute-start.10 = (f32[4,896]{1,0:T(4,128)S(1)}, f32[4,896]{1,0:T(4,128)S(1)}, u32[]{:S(2)}, u32[]{:S(2)}) collective-permute-start(f32[4,896]{1,0:T(4,128)S(1)} %pad_maximum_fusion.4), channel_id=1, source_target_pairs={{0,8},{1,9},{2,10},{3,11},{4,12},{5,13},{6,14},{7,15},{8,0},{9,1},... | collective-permute-start | bytes 43016 | tf_op jit(solution)/shard_map/ppermute | solution.py:1170
  41.5 5.6 %collective-permute-start.11 = (f32[8,896]{1,0:T(8,128)S(1)}, f32[8,896]{1,0:T(8,128)S(1)}, u32[]{:S(2)}, u32[]{:S(2)}) collective-permute-start(f32[8,896]{1,0:T(8,128)S(1)} %pad_maximum_fusion.3), channel_id=1, source_target_pairs={{0,16},{1,17},{2,18},{3,19},{4,20},{5,21},{6,22},{7,23},{8,24},{9,... | collective-permute-start | bytes 86024 | tf_op jit(solution)/shard_map/ppermute | solution.py:1170
  44.2 7.4 %collective-permute-start.5 = (bf16[128,768]{1,0:T(8,128)(2,1)S(1)}, bf16[128,768]{1,0:T(8,128)(2,1)S(1)}, u32[]{:S(2)}, u32[]{:S(2)}) collective-permute-start(bf16[128,768]{1,0:T(8,128)(2,1)S(1)} %get-tuple-element.69), channel_id=1, source_target_pairs={{0,2},{1,3},{2,0},{3,1},{4,6},{5,7},{6,4},{7,5},{8,10},{9,11},{10,... | collective-permute-start | bytes 589832 | tf_op jit(solution)/shard_map/ppermute | solution.py:1170
  44.7 7.4 %collective-permute-start.6 = (bf16[128,768]{1,0:T(8,128)(2,1)S(1)}, bf16[128,768]{1,0:T(8,128)(2,1)S(1)}, u32[]{:S(2)}, u32[]{:S(2)}) collective-permute-start(bf16[128,768]{1,0:T(8,128)(2,1)S(1)} %get-tuple-element.68), channel_id=1, source_target_pairs={{0,4},{1,5},{2,6},{3,7},{4,0},{5,1},{6,2},{7,3},{8,12},{9,13},{10,... | collective-permute-start | bytes 589832 | tf_op jit(solution)/shard_map/ppermute | solution.py:1170
  47.1 8.0 %collective-permute-start.7 = (bf16[128,768]{1,0:T(8,128)(2,1)S(1)}, bf16[128,768]{1,0:T(8,128)(2,1)S(1)}, u32[]{:S(2)}, u32[]{:S(2)}) collective-permute-start(bf16[128,768]{1,0:T(8,128)(2,1)S(1)} %get-tuple-element.67), channel_id=1, source_target_pairs={{0,6},{1,7},{2,4},{3,5},{4,2},{5,3},{6,0},{7,1},{8,14},{9,15},{10,... | collective-permute-start | bytes 589832 | tf_op jit(solution)/shard_map/ppermute | solution.py:1170
  222.6 2.1 copy-start.11
  227.0 5.7 %copy-start.3 = (bf16[2,4,3,192,256]{4,3,2,1,0:T(8,128)(2,1)S(1)}, bf16[2,4,3,192,256]{4,3,2,1,0:T(8,128)(2,1)}, u32[]{:S(2)}) copy-start(bf16[2,4,3,192,256]{4,3,2,1,0:T(8,128)(2,1)} %get-tuple-element.65) | copy-start | bytes 7077892
  233.0 1.6 copy-start.7
  255.3 3.6 %copy-start.12 = (f32[16,768]{1,0:T(8,128)S(1)}, f32[16,768]{1,0:T(8,128)}, u32[]{:S(2)}) copy-start(f32[16,768]{1,0:T(8,128)} %add_multiply_fusion) | copy-start | bytes 147460
  258.9 3.1 %copy-start = (bf16[2,4,1,192,256]{4,3,2,1,0:T(8,128)(2,1)S(1)}, bf16[2,4,1,192,256]{4,3,2,1,0:T(8,128)(2,1)}, u32[]{:S(2)}) copy-start(bf16[2,4,1,192,256]{4,3,2,1,0:T(8,128)(2,1)} %slice.67) | copy-start | bytes 2359300
  262.7 1.5 slice-start
  262.7 1.5 copy-start.4
  264.2 4.1 %copy-start.6 = (f32[2,8,4,768]{3,1,2,0:T(8,128)S(1)}, f32[2,8,4,768]{3,1,2,0:T(8,128)}, u32[]{:S(2)}) copy-start(f32[2,8,4,768]{3,1,2,0:T(8,128)} %copy-done.5) | copy-start | bytes 589828
  271.0 4.0 %copy-start.10 = (bf16[4,128,768]{2,1,0:T(8,128)(2,1)S(1)}, bf16[4,128,768]{2,1,0:T(8,128)(2,1)}, u32[]{:S(2)}) copy-start(bf16[4,128,768]{2,1,0:T(8,128)(2,1)} %get-tuple-element.60) | copy-start | bytes 2359300
  274.4 1.5 copy-start.9
  (3 other events, 2.7 us)

commit v4 on v3

--- a/solution.py
+++ b/solution.py
@@ -487,7 +487,7 @@
 
 def feed_turn_kernel(
     h2_ref, h2t_ref, gf_ref, wg0, wg1, wu0, wu1, bg0, bg1, bu0, bu1, wd0, wd1,
-    mid_ref, att_ref, dy_ref, mix_ref, mod_ref, weight_ref, dbias_ref,
+    mid_ref, att_ref, dy_ref, mix_ref, mod_ref, weight_ref, dbias_ref, known_ref,
     out_ref, gmid_ref, gmix_ref, dw_ref, sums_ref, total_ref,
     feed_ref, gh_ref, bias_ref, made, paired, near, pair_send, pair_recv, near_send, near_recv,
 ):
@@ -610,7 +610,7 @@
         sums_ref[0, 3:4, :] = col_sum(dy * feed)
         sums_ref[0, 4:5, :] = col_sum(grad_attended.astype(F32))
         sums_ref[0, 5:6, :] = col_sum(gf_ref[...].astype(F32))
-        sums_ref[0, 6:8, :] = jnp.zeros((2, width), F32)
+        sums_ref[0, 6:8, :] = known_ref[...]
         for row in range(32):
             col = (row % 6) * unit
             sums_ref[1, row // 6 : row // 6 + 1, col : col + unit] = bias_ref[row : row + 1, :]
@@ -647,7 +647,7 @@
 
 def feed_turn_call(
     hidden, hidden_t, grad_feed, gate_up, gate_up_bias, down, middle, attended, dy, mixed, mod,
-    weight, down_bias,
+    weight, down_bias, known,
 ):
     rows, width = hidden.shape
     low = jax.ShapeDtypeStruct((rows, width), BF16)
@@ -670,7 +670,7 @@
         + [bias(0, 0), bias(1, 0), bias(0, 1), bias(1, 1)]
         + [deep(0), deep(1)]
         + [once((rows, width))] * 4
-        + [once(mod.shape), once(weight.shape), once(down_bias.shape)],
+        + [once(each.shape) for each in (mod, weight, down_bias, known)],
         out_specs=[full(shape.shape) for shape in out_shape],
         out_shape=out_shape,
         scratch_shapes=[
@@ -692,7 +692,7 @@
     )(
         hidden, hidden_t, grad_feed, gate_up, gate_up, gate_up, gate_up, gate_up_bias,
         gate_up_bias, gate_up_bias, gate_up_bias, down, down, middle, attended, dy, mixed, mod,
-        weight, down_bias,
+        weight, down_bias, known,
     )
 
 
@@ -1146,6 +1146,152 @@
     )
 
 
+def finish_kernel(
+    head, feeds_ref, projs_ref, early_ref, late_ref, modw_hbm,
+    cond_ref, table_hbm, gmodw_hbm, gmodb_ref, ginw_hbm, ginb_ref, gqg_ref, gkg_ref, goutw_hbm,
+    goutb_ref, gguw_hbm, ggub_ref, gdownw_hbm, gdownb_ref,
+    modw_ref, table_ref, gmodw_ref, ginw_ref, goutw_ref, gguw_ref, gdownw_ref, acts_ref, load_sem,
+    store_sem,
+):
+    place = Place()
+    width = early_ref.shape[3]
+    part = projs_ref.shape[3]
+    load = pltpu.make_async_copy(modw_hbm, modw_ref, load_sem)
+    load.start()
+    stores = [
+        pltpu.make_async_copy(source, target, store_sem.at[i])
+        for i, (source, target) in enumerate(
+            (
+                (gguw_ref, gguw_hbm), (gdownw_ref, gdownw_hbm), (ginw_ref, ginw_hbm),
+                (goutw_ref, goutw_hbm), (gmodw_ref, gmodw_hbm), (table_ref, table_hbm),
+            )
+        )
+    ]
+    for c in range(2):
+        for chip in range(4):
+            for f in range(2):
+                for i in range(2):
+                    col = (((c * 2 + f) * 2 + i) * 4 + chip) * 128
+                    gguw_ref[:, col : col + 128] = feeds_ref[
+                        c, chip, f, :, i * 128 : (i + 1) * 128
+                    ].astype(F32)
+    stores[0].start()
+    for c in range(2):
+        for chip in range(4):
+            row = chip * 128 + c * 64
+            for b in range(3):
+                gdownw_ref[row : row + 64, b * 256 : (b + 1) * 256] = feeds_ref[
+                    c, chip, 2, b * 64 : (b + 1) * 64, :
+                ].astype(F32)
+    stores[1].start()
+    for c in range(2):
+        for chip in range(4):
+            row = chip * part
+            for g in range(3):
+                for q in range(3):
+                    col = q * width + g * 256 + c * 128
+                    ginw_ref[row : row + part, col : col + 128] = projs_ref[
+                        c, chip, g, :, q * 128 : (q + 1) * 128
+                    ].astype(F32)
+            half = width // 2
+            goutw_ref[row : row + part, c * half : (c + 1) * half] = projs_ref[c, chip, 3].astype(F32)
+    stores[2].start()
+    stores[3].start()
+
+    vectors = [late_ref[0, :, 0, :], late_ref[0, :, 1, :]]
+    vectors += [early_ref[0, :, j, :] for j in range(4)]
+    lows = [vector.astype(BF16) for vector in vectors]
+    conditions = early_ref[0, :, 6, :]
+    labels = early_ref[0, :, 7, :]
+    sig = 1.0 / (1.0 + jnp.exp(-conditions))
+    acts = (conditions * sig).astype(BF16)
+    size = acts_ref.shape[1]
+    for z in range(4):
+
+        @pl.when(place.z == z)
+        def _(z=z):
+            acts_ref[...] = acts[:, z * size : (z + 1) * size]
+
+    mine = acts_ref[...]
+    for j, low in enumerate(lows):
+        gmodw_ref[:, j * width : (j + 1) * width] = mm_tn(mine, low)
+    stores[4].start()
+    early_sum = jnp.sum(early_ref[0], axis=0)
+    gate_sum = jnp.sum(early_ref[1], axis=0)
+    late_sum = jnp.sum(late_ref[0], axis=0)
+    gain_sum = jnp.sum(late_ref[1], axis=0)
+    mod_b = jnp.concatenate(
+        [late_sum[0:1], late_sum[1:2]] + [early_sum[j : j + 1] for j in range(4)], axis=1
+    )
+    in_b = jnp.concatenate([late_sum[2:3], late_sum[3:4], gain_sum[2:3]], axis=1)
+    gate_b = jnp.concatenate(
+        [gate_sum[n // 6 : n // 6 + 1, (n % 6) * 128 : (n % 6) * 128 + 128] for n in range(32)],
+        axis=1,
+    )
+    gains = sum(gain_sum[0:2, i : i + 128] for i in range(0, width, 128))
+    gains = gains[:, :head] + gains[:, head:]
+    pieces = (
+        (gmodb_ref, mod_b), (ginb_ref, in_b), (gqg_ref, gains[0:1]), (gkg_ref, gains[1:2]),
+        (goutb_ref, early_sum[4:5]), (ggub_ref, gate_b), (gdownb_ref, early_sum[5:6]),
+    )
+    for z in range(4):
+
+        @pl.when(place.z == z)
+        def _(z=z):
+            for ref, row in pieces:
+                size = row.shape[1] // 4
+                ref[...] = row[:, z * size : (z + 1) * size]
+
+    load.wait()
+    grad = sum(mm_nt(low, modw_ref[:, j * width : (j + 1) * width]) for j, low in enumerate(lows))
+    grad = grad * sig * (1.0 + conditions * (1.0 - sig))
+    for k in range(4):
+        cond_ref[pl.ds(place.flipped(k), 1), :] = grad[k : k + 1]
+    classes = table_ref.shape[0]
+    wide = -(-classes // 128) * 128
+    column = lax.broadcasted_iota(jnp.int32, (1, wide), 1).astype(F32)
+    onehot = jnp.where(labels[:, 0:1] == column, 1.0, 0.0).astype(BF16)
+    high = grad.astype(BF16)
+    rest = grad - high.astype(F32)
+    middle = rest.astype(BF16)
+    last = (rest - middle.astype(F32)).astype(BF16)
+    table = mm_tn(
+        jnp.concatenate([onehot] * 3, axis=0), jnp.concatenate([high, middle, last], axis=0)
+    )
+    table_ref[...] = table[:classes]
+    stores[5].start()
+    for store in stores:
+        store.wait()
+
+
+def finish_call(feeds, projs, early, late, weight, head, classes, hidden_width):
+    width = weight.shape[0]
+    rows = width // 4
+    whole = lambda *shape: jax.ShapeDtypeStruct(shape, F32)
+    anywhere = pl.BlockSpec(memory_space=pl.ANY)
+    out_shape = [
+        whole(4, width), whole(classes, width), whole(rows, 6 * width), whole(1, 6 * width // 4),
+        whole(rows, 3 * width), whole(1, 3 * width // 4), whole(1, head // 4), whole(1, head // 4),
+        whole(rows, width), whole(1, rows), whole(rows, 2 * hidden_width),
+        whole(1, 2 * hidden_width // 4), whole(hidden_width // 4, width), whole(1, rows),
+    ]
+    big = (1, 2, 4, 8, 10, 12)
+    return pl.pallas_call(
+        functools.partial(finish_kernel, head),
+        in_specs=[pl.BlockSpec(memory_space=pltpu.VMEM)] * 4 + [anywhere],
+        out_specs=[
+            anywhere if i in big else pl.BlockSpec(memory_space=pltpu.VMEM)
+            for i in range(len(out_shape))
+        ],
+        out_shape=out_shape,
+        scratch_shapes=[pltpu.VMEM(weight.shape, BF16)]
+        + [pltpu.VMEM(out_shape[i].shape, F32) for i in big]
+        + [pltpu.VMEM((16, rows), BF16), pltpu.SemaphoreType.DMA, pltpu.SemaphoreType.DMA((6,))],
+        compiler_params=params(),
+        name="finish",
+    )(feeds, projs, early, late, weight)
+
+
 def take(array_in, index, axis=0):
     return lax.dynamic_index_in_dim(array_in, index, axis, keepdims=False)
 
@@ -1264,38 +1410,28 @@
     blocks = hidden_width // unit
     quick = nb == 4 and hidden_width == 16 * 128
     if quick:
+        known = jnp.stack([condition, jnp.broadcast_to(label.astype(F32), (width,))])
+        known = jnp.where(core == 0, known, 0.0)
         output_rows, grad_middle, grad_mixed, d_out, sums_two, totals = feed_turn_call(
             hidden_two, hidden_two_t, grad_feed, gate_up_weight, gate_up_bias[None], down_weight,
-            middle, attended, dy, mixed, mod, outproj_weight, down_bias[None],
+            middle, attended, dy, mixed, mod, outproj_weight, down_bias[None], known,
         )
         output, grad_tokens, feeds, projs, early, late = back_call(
             q, k0, k1, v0, v1, grad_mixed, mixed, inverse, grown, mod, qgain, kgain, cosine, sine,
             d_out, totals, sums_two, raw, hidden_one, x, grad_middle, inproj_weight, output_rows,
             head,
         )
-        output = output.reshape(tokens.shape)
-        grad_tokens = grad_tokens.reshape(tokens.shape)
-        slice_rows = width // nb
-        gates = feeds[:, :, :2].reshape(2, 4, 2, slice_rows, 2, 128).transpose(3, 0, 2, 4, 1, 5)
-        grad_gu_w = gates.reshape(slice_rows, 2 * hidden_width).astype(F32)
-        downs = feeds[:, :, 2].reshape(2, 4, 3, 64, 256).transpose(1, 0, 3, 2, 4)
-        grad_down_w = downs.reshape(hidden_width // nb, width).astype(F32)
-        part = width // 16
-        ins = projs[:, :, :3].reshape(2, 4, 3, part, 3, 128).transpose(1, 3, 4, 2, 0, 5)
-        grad_in_w = ins.reshape(slice_rows, 3 * width).astype(F32)
-        outs = projs[:, :, 3].transpose(1, 2, 0, 3)
-        grad_out_w = outs.reshape(slice_rows, width).astype(F32)
-        count = early.shape[1]
-        early = jnp.concatenate(
-            [early[0, :, :6].reshape(count, -1), early[1].reshape(count, -1)[:, : 2 * hidden_width]],
-            axis=1,
-        )
-        gain_sums = late[1, :, :2].reshape(count, 2, heads, head).sum(axis=2)
-        late = jnp.concatenate(
-            [
-                late[0].reshape(count, -1), late[1, :, 2], gain_sums.reshape(count, -1),
-            ],
-            axis=1,
+        (
+            grad_condition, grad_table, grad_mod_w, grad_mod_b, grad_in_w, grad_in_b, grad_q_gain,
+            grad_k_gain, grad_out_w, grad_out_b, grad_gu_w, grad_gu_b, grad_down_w, grad_down_b,
+        ) = finish_call(
+            feeds, projs, early, late, modulate_weight, head, class_count, hidden_width
+        )
+        return (
+            output.reshape(tokens.shape), grad_tokens.reshape(tokens.shape), grad_condition,
+            grad_table, grad_mod_w, grad_mod_b[0], grad_in_w, grad_in_b[0], grad_q_gain[0],
+            grad_k_gain[0], grad_out_w, grad_out_b[0], grad_gu_w, grad_gu_b[0], grad_down_w,
+            grad_down_b[0],
         )
     else:
         feed, grad_hidden, d_down, d_gate, d_bias = feed_call(
@@ -1353,8 +1489,7 @@
 
     known = jnp.concatenate([condition, jnp.broadcast_to(label.astype(F32), (128,))])
     known = moves.gather(known)
-    if not quick:
-        early, late = everywhere(early), everywhere(late)
+    early, late = everywhere(early), everywhere(late)
     grad_modulation = jnp.concatenate([late[:, : 2 * width], early[:, : 4 * width]], axis=1)
     conditions = known[:, :width]
     all_labels = known[:, width].astype(jnp.int32)

time: 278 us -> 233 us (0.84)
  local copies, waits for them, and re-layouts: 46.5 us -> 12 us
  Pallas kernels: 178 us -> 194 us
  matrix products: 12.2 us -> 0 us
  starting transfers between devices: 16.6 us -> 8.75 us
  other arithmetic: 11.7 us -> 7.89 us
    convert_element_type x8 -> x0, local copies, waits for them, and re-layouts: 19.7 us -> none  [the longest x3 9.74 us: body(): grad_gu_w = gates.reshape(slice_rows, 2 * hidden_width).astype(F32)]
    pallas_call x0 -> x1, Pallas kernels: none -> 15.2 us  [finish_call(): pl.pallas_call(functools.partial(finish_kernel, head), in_specs=[pl.Block...]
    dot_general x3 -> x0, matrix products: 12.2 us -> none  [the longest x1 5.71 us: mm_nt(): lax.dot_general(left, right, (((1,), (1,)), ((), ())), preferred_element_...]
    ppermute x12 -> x8, starting transfers between devices: 16.6 us -> 8.75 us  [flip(): return lax.ppermute(value, AXES, pairs)]
    dynamic_slice x5 -> x0, local copies, waits for them, and re-layouts: 5.41 us -> none  [the longest x4 4.03 us: part(): lax.dynamic_slice_in_dim(vector, start + z * (size // nb), size // nb, ax...]
    unnamed x52 -> x30, local copies, waits for them, and re-layouts: 7.66 us -> 2.99 us
    slice x12 -> x0, local copies, waits for them, and re-layouts: 3.81 us -> none  [the longest x2 1.09 us: body(): early[1].reshape(count, -1)[:, :2 * hidden_width]]
    convert_element_type x5 -> x0, other arithmetic: 3.35 us -> none  [the longest x1 1.33 us: body(): grad_in_w = ins.reshape(slice_rows, 3 * width).astype(F32)]
  transfers between devices with their start and end apart: 12 -> 8, of which waited for: 4 -> 2; matrix products, arithmetic and copies ran while one was open for 5% -> 5% of each run, Pallas kernels for 5% -> 3%
where the time goes in v4:
time: 233 us
  Pallas kernels  194 us (83%)
  local copies, waits for them, and re-layouts  12 us (5%)
  starting transfers between devices  8.75 us (4%)
  other arithmetic  7.89 us (3%)
  waiting for transfers between devices  5.97 us (3%)
  between operations  4.36 us (2%)
    pallas_call x1, Pallas kernels, back_call(): pl.pallas_call(functools.partial(back_kernel, head), grid=(7,), in_specs=...  92.3 us
    pallas_call x1, Pallas kernels, feed_turn_call(): pl.pallas_call(feed_turn_kernel, grid=(9,), in_specs=[once((rows, width))...  57 us
    pallas_call x1, Pallas kernels, finish_call(): pl.pallas_call(functools.partial(finish_kernel, head), in_specs=[pl.Block...  15.2 us
    pallas_call x1, Pallas kernels, attend_call(): pl.pallas_call(functools.partial(attend_kernel, head ** (-0.5)), grid=(wi...  12 us
    ppermute x8, starting transfers between devices, flip(): return lax.ppermute(value, AXES, pairs)  8.75 us
    pallas_call x1, Pallas kernels, project_call(): pl.pallas_call(functools.partial(project_kernel, head), grid=(2,), in_spe...  6.53 us
    pallas_call x1, Pallas kernels, modulation_call(): pl.pallas_call(modulation_kernel, grid=(wide // width,), in_specs=[full((...  6.42 us
    ppermute x8, waiting for transfers between devices, flip(): return lax.ppermute(value, AXES, pairs)  5.97 us
  transfers between devices with their start and end apart: 8, of which 2 were waited for; matrix products, arithmetic and copies ran while one was open for 5% of the time, Pallas kernels for 3%

profile of v4, /device:TPU:0, one launch (start us, length us, event | category | flops | bytes accessed | tf_op | source)
XLA Modules:
  0.0 232.7 jit_solution(11376355696377457618)
XLA Ops:
  0.8 1.3 dynamic-slice_bitcast_fusion.7
  2.0 4.0 %collective-permute-start.2 = (bf16[128,768]{1,0:T(8,128)(2,1)S(1)}, bf16[128,768]{1,0:T(8,128)(2,1)S(1)}, u32[]{:S(2)}, u32[]{:S(2)}) collective-permute-start(bf16[128,768]{1,0:T(8,128)(2,1)S(1)} %get-tuple-element.101), channel_id=1, source_target_pairs={{0,6},{1,7},{2,4},{3,5},{4,2},{5,3},{6,0},{7,1},{8,14},{9,15},{10,... | collective-permute-start | bytes 589832 | tf_op jit(solution)/shard_map/ppermute | solution.py:1316
  6.9 0.6 dynamic_slice.41
  8.8 0.6 dynamic_slice.40
  10.2 0.7 broadcast_in_dim_tile.6.qgain_ref
  10.8 0.7 broadcast_in_dim_tile.7.kgain_ref
  11.5 0.6 broadcast_in_dim.67.bias_ref
  12.1 0.6 broadcast_in_dim.66.bias_ref
  13.4 0.7 convert_reduce_fusion
  14.1 0.6 broadcast_in_dim.65.act_ref
  14.7 6.4 %modulation.1 = f32[16,4608]{1,0:T(8,128)} custom-call(bf16[16,768]{1,0:T(8,128)(2,1)} %broadcast_in_dim.65.act_ref, bf16[768,4608]{1,0:T(8,128)(2,1)} %modw_hbm.1, bf16[1,4608]{1,0:T(2,128)(2,1)} %broadcast_in_dim.66.bias_ref), custom_call_target="tpu_custom_call" | custom-call | tf_op jit(solution)/shard_map/modulation/pallas_call | solution.py:49
  21.2 1.5 slice.4.mod_ref
  22.7 1.8 sine_multiply_fusion
  24.5 0.9 pad_maximum_fusion.x_ref.x_hbm
  25.5 6.5 %project.1 = (bf16[512,768]{1,0:T(8,128)(2,1)}, bf16[512,768]{1,0:T(8,128)(2,1)}, bf16[512,768]{1,0:T(8,128)(2,1)}, bf16[512,768]{1,0:T(8,128)(2,1)}, bf16[512,1536]{1,0:T(8,128)(2,1)}) custom-call(bf16[512,768]{1,0:T(8,128)(2,1)} %pad_maximum_fusion.x_ref.x_hbm, f32[1,4608]{1,0:T(1,128)} %slice.4.mod_ref, bf16[768,2304]{1,0:T(8,128)(2,1)} %weight_hbm.1, ...), custom_call_target="tpu_custom_call" | custom-call | tf_op jit(solution)/shard_map/project/pallas_call | solution.py:114
  32.7 2.9 %collective-permute-start.7 = (bf16[128,768]{1,0:T(8,128)(2,1)S(1)}, bf16[128,768]{1,0:T(8,128)(2,1)S(1)}, u32[]{:S(2)}, u32[]{:S(2)}) collective-permute-start(bf16[128,768]{1,0:T(8,128)(2,1)S(1)} %get-tuple-element.97), channel_id=1, source_target_pairs={{0,6},{1,7},{2,4},{3,5},{4,2},{5,3},{6,0},{7,1},{8,14},{9,15},{10,... | collective-permute-start | bytes 589832 | tf_op jit(solution)/shard_map/ppermute | solution.py:1316
  37.5 0.6 broadcast_in_dim.75.dbias_ref
  38.1 0.6 broadcast_in_dim.74.bg0.bg1.bu0.bu1
  38.7 0.6 pad_select_fusion.known_ref
  39.3 2.2 collective-permute-done.7
  41.5 3.8 %collective-permute-done.6 = bf16[128,768]{1,0:T(8,128)(2,1)S(1)} collective-permute-done((bf16[128,768]{1,0:T(8,128)(2,1)S(1)}, bf16[128,768]{1,0:T(8,128)(2,1)S(1)}, u32[]{:S(2)}, u32[]{:S(2)}) %collective-permute-start.6) | collective-permute-done | bytes 196640 | tf_op jit(solution)/shard_map/ppermute | solution.py:1316
  45.2 1.0 pad_maximum_fusion.1.dy_ref
  46.2 0.9 copy-done
  47.4 12.0 %attend.1 = (bf16[512,768]{1,0:T(8,128)(2,1)}, bf16[12,512,1024]{2,1,0:T(8,128)(2,1)}, f32[512,768]{1,0:T(8,128)}) custom-call(bf16[512,768]{1,0:T(8,128)(2,1)} %get-tuple-element.55.q_ref, bf16[512,768]{1,0:T(8,128)(2,1)} %get-tuple-element.56.k0_ref, bf16[512,768]{1,0:T(8,128)(2,1)} %copy-done, bf16[512,768]{1,0:T(8,128)(2,1)} %get-tuple-element.57.v0_ref, ...), custom_call_target="tpu_custom_call" | custom-call | tf_op jit(solution)/shard_map/attend/pallas_call | solution.py:155
  59.4 4.4 %middle.1 = (bf16[512,768]{1,0:T(8,128)(2,1)}, f32[512,768]{1,0:T(8,128)}, bf16[512,768]{1,0:T(8,128)(2,1)}, bf16[768,512]{1,0:T(8,128)(2,1)}, bf16[512,768]{1,0:T(8,128)(2,1)}) custom-call(bf16[512,768]{1,0:T(8,128)(2,1)} %get-tuple-element.58.mix_ref, bf16[512,768]{1,0:T(8,128)(2,1)} %pad_maximum_fusion.x_ref.x_hbm, ...), custom_call_target="tpu_custom_call" | custom-call | tf_op jit(solution)/shard_map/middle/pallas_call | solution.py:239
  63.8 57.0 %feed_turn.1 = (bf16[512,768]{1,0:T(8,128)(2,1)}, f32[512,768]{1,0:T(8,128)}, bf16[512,768]{1,0:T(8,128)(2,1)}, bf16[2,768,384]{2,1,0:T(8,128)(2,1)}, f32[2,8,76...) custom-call(bf16[512,768]{1,0:T(8,128)(2,1)} %get-tuple-element.59.h2_ref, bf16[768,512]{1,0:T(8,128)(2,1)} %get-tuple-element.60.h2t_ref, ...), custom_call_target="tpu_custom_call" | custom-call | tf_op jit(solution)/shard_map/feed_turn/pallas_call | solution.py:665
  120.8 92.3 %back.1 = (bf16[4,128,768]{2,1,0:T(8,128)(2,1)}, bf16[4,128,768]{2,1,0:T(8,128)(2,1)}, bf16[2,4,3,192,256]{4,3,2,1,0:T(8,128)(2,1)}, bf16[2,4,4,48,384]{4,3,2,1,...) custom-call(bf16[512,768]{1,0:T(8,128)(2,1)} %get-tuple-element.55.q_ref, ...), custom_call_target="tpu_custom_call" | custom-call | tf_op jit(solution)/shard_map/back/pallas_call | solution.py:1112
  213.0 15.2 %finish.1 = (f32[4,768]{1,0:T(4,128)}, f32[1001,768]{1,0:T(8,128)}, f32[192,4608]{1,0:T(8,128)}, f32[1,1152]{1,0:T(1,128)}, f32[192,2304]{1,0:T(8,128)}, /*index...) custom-call(bf16[2,4,3,192,256]{4,3,2,1,0:T(8,128)(2,1)} %get-tuple-, ...), custom_call_target="tpu_custom_call" | custom-call | tf_op jit(solution)/shard_map/finish/pallas_call | solution.py:1279
  228.3 1.4 reduce.2
  229.6 1.3 reduce.1
  230.9 0.9 copy.35
  231.8 0.9 copy.36
  (55 shorter events, 3.0 us)
Async XLA Ops:
  0.6 6.3 %copy-start.12 = (s32[4]{0:T(128)S(1)}, s32[4]{0:T(128)}, u32[]{:S(2)}) copy-start(s32[4]{0:T(128)} %param.19) | copy-start | bytes 52
  0.7 8.2 %copy-start.13 = (s32[4]{0:T(128)S(1)}, s32[4]{0:T(128)}, u32[]{:S(2)}) copy-start(s32[4]{0:T(128)} %param.18) | copy-start | bytes 52
  0.7 9.5 %copy-start.10 = (bf16[64]{0:T(256)(128)(2,1)S(1)}, bf16[64]{0:T(256)(128)(2,1)}, u32[]{:S(2)}) copy-start(bf16[64]{0:T(256)(128)(2,1)} %param.25) | copy-start | bytes 388
  0.7 10.2 %copy-start.11 = (bf16[64]{0:T(256)(128)(2,1)S(1)}, bf16[64]{0:T(256)(128)(2,1)}, u32[]{:S(2)}) copy-start(bf16[64]{0:T(256)(128)(2,1)} %param.26) | copy-start | bytes 388
  0.7 10.8 %copy-start.7 = (bf16[2304]{0:T(1024)(128)(2,1)S(1)}, bf16[2304]{0:T(1024)(128)(2,1)}, u32[]{:S(2)}) copy-start(bf16[2304]{0:T(1024)(128)(2,1)} %param.24) | copy-start | bytes 13828
  0.7 11.4 %copy-start.5 = (bf16[4608]{0:T(1024)(128)(2,1)S(1)}, bf16[4608]{0:T(1024)(128)(2,1)}, u32[]{:S(2)}) copy-start(bf16[4608]{0:T(1024)(128)(2,1)} %param.22) | copy-start | bytes 27652
  2.0 22.5 %collective-permute-start.2 = (bf16[128,768]{1,0:T(8,128)(2,1)S(1)}, bf16[128,768]{1,0:T(8,128)(2,1)S(1)}, u32[]{:S(2)}, u32[]{:S(2)}) collective-permute-start(bf16[128,768]{1,0:T(8,128)(2,1)S(1)} %get-tuple-element.101), channel_id=1, source_target_pairs={{0,6},{1,7},{2,4},{3,5},{4,2},{5,3},{6,0},{7,1},{8,14},{9,15},{10,... | collective-permute-start | bytes 589832 | tf_op jit(solution)/shard_map/ppermute | solution.py:1316
  6.0 18.5 %collective-permute-start.1 = (bf16[128,768]{1,0:T(8,128)(2,1)S(1)}, bf16[128,768]{1,0:T(8,128)(2,1)S(1)}, u32[]{:S(2)}, u32[]{:S(2)}) collective-permute-start(bf16[128,768]{1,0:T(8,128)(2,1)S(1)} %get-tuple-element.102), channel_id=1, source_target_pairs={{0,4},{1,5},{2,6},{3,7},{4,0},{5,1},{6,2},{7,3},{8,12},{9,13},{10,... | collective-permute-start | bytes 589832 | tf_op jit(solution)/shard_map/ppermute | solution.py:1316
  6.6 18.0 %collective-permute-start = (bf16[128,768]{1,0:T(8,128)(2,1)S(1)}, bf16[128,768]{1,0:T(8,128)(2,1)S(1)}, u32[]{:S(2)}, u32[]{:S(2)}) collective-permute-start(bf16[128,768]{1,0:T(8,128)(2,1)S(1)} %get-tuple-element.103), channel_id=1, source_target_pairs={{0,2},{1,3},{2,0},{3,1},{4,6},{5,7},{6,4},{7,5},{8,10},{9,11},{10,... | collective-permute-start | bytes 589832 | tf_op jit(solution)/shard_map/ppermute | solution.py:1316
  25.5 7.1 %copy-start.2 = (bf16[4,16,8,768]{3,2,1,0:T(8,128)(2,1)S(1)}, bf16[4,16,8,768]{3,2,1,0:T(8,128)(2,1)}, u32[]{:S(2)}) copy-start(bf16[4,16,8,768]{3,2,1,0:T(8,128)(2,1)} %param.33) | copy-start | bytes 2359300
  32.0 4.9 %copy-start.8 = (bf16[768]{0:T(1024)(128)(2,1)S(1)}, bf16[768]{0:T(1024)(128)(2,1)}, u32[]{:S(2)}) copy-start(bf16[768]{0:T(1024)(128)(2,1)} %param.28) | copy-start | bytes 4612
  32.0 5.5 %copy-start.9 = (bf16[768]{0:T(1024)(128)(2,1)S(1)}, bf16[768]{0:T(1024)(128)(2,1)}, u32[]{:S(2)}) copy-start(bf16[768]{0:T(1024)(128)(2,1)} %param.32) | copy-start | bytes 4612
  32.0 6.0 %copy-start.6 = (bf16[4096]{0:T(1024)(128)(2,1)S(1)}, bf16[4096]{0:T(1024)(128)(2,1)}, u32[]{:S(2)}) copy-start(bf16[4096]{0:T(1024)(128)(2,1)} %param.30) | copy-start | bytes 24580
  32.0 14.2 %collective-permute-start.3 = (bf16[512,768]{1,0:T(8,128)(2,1)}, bf16[512,768]{1,0:T(8,128)(2,1)S(1)}, u32[]{:S(2)}, u32[]{:S(2)}) collective-permute-start(bf16[512,768]{1,0:T(8,128)(2,1)} %get-tuple-element.56.k0_ref), channel_id=1, source_target_pairs={{0,1},{1,0},{2,3},{3,2},{4,5},{5,4},{6,7},{7,6},{8,9},{9,8},{10,11... | collective-permute-start | bytes 2359304 | tf_op jit(solution)/shard_map/ppermute | solution.py:1316
  32.1 14.1 %collective-permute-start.4 = (bf16[512,768]{1,0:T(8,128)(2,1)}, bf16[512,768]{1,0:T(8,128)(2,1)S(1)}, u32[]{:S(2)}, u32[]{:S(2)}) collective-permute-start(bf16[512,768]{1,0:T(8,128)(2,1)} %get-tuple-element.57.v0_ref), channel_id=1, source_target_pairs={{0,1},{1,0},{2,3},{3,2},{4,5},{5,4},{6,7},{7,6},{8,9},{9,8},{10,11... | collective-permute-start | bytes 2359304 | tf_op jit(solution)/shard_map/ppermute | solution.py:1316
  32.7 8.8 %collective-permute-start.7 = (bf16[128,768]{1,0:T(8,128)(2,1)S(1)}, bf16[128,768]{1,0:T(8,128)(2,1)S(1)}, u32[]{:S(2)}, u32[]{:S(2)}) collective-permute-start(bf16[128,768]{1,0:T(8,128)(2,1)S(1)} %get-tuple-element.97), channel_id=1, source_target_pairs={{0,6},{1,7},{2,4},{3,5},{4,2},{5,3},{6,0},{7,1},{8,14},{9,15},{10,... | collective-permute-start | bytes 589832 | tf_op jit(solution)/shard_map/ppermute | solution.py:1316
  35.6 9.6 %collective-permute-start.6 = (bf16[128,768]{1,0:T(8,128)(2,1)S(1)}, bf16[128,768]{1,0:T(8,128)(2,1)S(1)}, u32[]{:S(2)}, u32[]{:S(2)}) collective-permute-start(bf16[128,768]{1,0:T(8,128)(2,1)S(1)} %get-tuple-element.98), channel_id=1, source_target_pairs={{0,4},{1,5},{2,6},{3,7},{4,0},{5,1},{6,2},{7,3},{8,12},{9,13},{10,... | collective-permute-start | bytes 589832 | tf_op jit(solution)/shard_map/ppermute | solution.py:1316
  36.1 9.1 %collective-permute-start.5 = (bf16[128,768]{1,0:T(8,128)(2,1)S(1)}, bf16[128,768]{1,0:T(8,128)(2,1)S(1)}, u32[]{:S(2)}, u32[]{:S(2)}) collective-permute-start(bf16[128,768]{1,0:T(8,128)(2,1)S(1)} %get-tuple-element.99), channel_id=1, source_target_pairs={{0,2},{1,3},{2,0},{3,1},{4,6},{5,7},{6,4},{7,5},{8,10},{9,11},{10,... | collective-permute-start | bytes 589832 | tf_op jit(solution)/shard_map/ppermute | solution.py:1316
  46.2 0.9 copy-start
  46.2 1.2 copy-start.1
  213.0 17.9 %copy-start.4 = (bf16[4,128,768]{2,1,0:T(8,128)(2,1)S(1)}, bf16[4,128,768]{2,1,0:T(8,128)(2,1)}, u32[]{:S(2)}) copy-start(bf16[4,128,768]{2,1,0:T(8,128)(2,1)} %get-tuple-element.74) | copy-start | bytes 2359300
  228.3 3.6 %copy-start.3 = (bf16[4,128,768]{2,1,0:T(8,128)(2,1)S(1)}, bf16[4,128,768]{2,1,0:T(8,128)(2,1)}, u32[]{:S(2)}) copy-start(bf16[4,128,768]{2,1,0:T(8,128)(2,1)} %get-tuple-element.75) | copy-start | bytes 2359300

commit v5 on v4

--- a/solution.py
+++ b/solution.py
@@ -231,7 +231,7 @@
     gf_ref[...] = (mod_ref[:, 5 * width :] * dy_ref[...].astype(F32)).astype(BF16)
 
 
-def middle_call(mixed, x, dy, mod, weight, bias):
+def middle_call(mixed, x, dy, mod, weight, bias, bias_at=0):
     rows, width = x.shape
     block = rows // 2
     by_row = pl.BlockSpec((block, width), lambda i: (i, 0))
@@ -239,7 +239,8 @@
     return pl.pallas_call(
         middle_kernel,
         grid=(2,),
-        in_specs=[by_row] * 3 + [full(mod.shape), full(weight.shape), full(bias.shape)],
+        in_specs=[by_row] * 3
+        + [full(mod.shape), full(weight.shape), pl.BlockSpec((1, width), lambda i: (0, bias_at))],
         out_specs=[by_row] * 3 + [pl.BlockSpec((width, block), lambda i: (0, i)), by_row],
         out_shape=[low, jax.ShapeDtypeStruct((rows, width), F32), low]
         + [jax.ShapeDtypeStruct((width, rows), BF16), low],
@@ -646,14 +647,16 @@
 
 
 def feed_turn_call(
-    hidden, hidden_t, grad_feed, gate_up, gate_up_bias, down, middle, attended, dy, mixed, mod,
-    weight, down_bias, known,
+    hidden, hidden_t, grad_feed, gate_up, down, middle, attended, dy, mixed, mod, weight, small,
+    known,
 ):
     rows, width = hidden.shape
     low = jax.ShapeDtypeStruct((rows, width), BF16)
     wide = jax.ShapeDtypeStruct((rows, width), F32)
     cols = lambda i, e: pl.BlockSpec((width, 128), lambda s: (0, 16 * e + feed_block(s, i)))
-    bias = lambda i, e: pl.BlockSpec((1, 128), lambda s: (0, 16 * e + feed_block(s, i)))
+    first = GATE_BIAS * width // 128
+    bias = lambda i, e: pl.BlockSpec((1, 128), lambda s: (0, first + 16 * e + feed_block(s, i)))
+    down_bias = pl.BlockSpec((1, width), lambda s: (0, DOWN_BIAS), pipeline_mode=pl.Buffered(1))
     deep = lambda i: pl.BlockSpec((128, width), lambda s: (feed_block(s, i), 0))
     piece = (width + 384, 256)
     out_shape = [
@@ -670,7 +673,7 @@
         + [bias(0, 0), bias(1, 0), bias(0, 1), bias(1, 1)]
         + [deep(0), deep(1)]
         + [once((rows, width))] * 4
-        + [once(each.shape) for each in (mod, weight, down_bias, known)],
+        + [once(mod.shape), once(weight.shape), down_bias, once(known.shape)],
         out_specs=[full(shape.shape) for shape in out_shape],
         out_shape=out_shape,
         scratch_shapes=[
@@ -690,10 +693,160 @@
         ),
         name="feed_turn",
     )(
-        hidden, hidden_t, grad_feed, gate_up, gate_up, gate_up, gate_up, gate_up_bias,
-        gate_up_bias, gate_up_bias, gate_up_bias, down, down, middle, attended, dy, mixed, mod,
-        weight, down_bias, known,
-    )
+        hidden, hidden_t, grad_feed, gate_up, gate_up, gate_up, gate_up, small, small, small,
+        small, down, down, middle, attended, dy, mixed, mod, weight, small, known,
+    )
+
+
+IN_BIAS, Q_GAIN, K_GAIN, OUT_BIAS, DOWN_BIAS, GATE_BIAS = 6, 9, 10, 11, 12, 13
+
+
+def small_row(width, head, modulate, inproj, qgain, kgain, outproj, down, gate_up):
+    heads = width // head
+    return jnp.concatenate(
+        [modulate, inproj, jnp.tile(qgain, heads), jnp.tile(kgain, heads), outproj, down, gate_up]
+    )[None]
+
+
+def front_kernel(
+    head, tile_cols, tok_hbm, grad_hbm, act_ref, small_ref, modw_hbm, inw_hbm,
+    x_hbm, dy_hbm, hid_hbm, q_hbm, k0_hbm, v0_hbm, k1_hbm, v1_hbm, raw_hbm, mod_ref, cos_ref,
+    sin_ref,
+    x_ref, own_ref, hid_ref, q_ref, k_ref, v_ref, raw_ref, modw_ref, inw_ref,
+    load_sem, store_sem, tok_send, tok_recv, kv_send, kv_recv,
+):
+    place = Place()
+    core, chip = place.core, place.chip
+    rows, width = x_ref.shape
+    cells = rows // 4
+    loads = [
+        pltpu.make_async_copy(source, target, load_sem.at[i])
+        for i, (source, target) in enumerate(
+            (
+                (tok_hbm.at[chip], x_ref.at[pl.ds(0, cells)]), (modw_hbm, modw_ref),
+                (inw_hbm, inw_ref), (grad_hbm.at[chip], own_ref),
+            )
+        )
+    ]
+    stores = [
+        pltpu.make_async_copy(source, target, store_sem.at[i])
+        for i, (source, target) in enumerate(
+            (
+                (own_ref, dy_hbm.at[pl.ds(0, cells)]), (x_ref, x_hbm), (hid_ref, hid_hbm),
+                (k_ref, k0_hbm), (v_ref, v0_hbm), (q_ref, q_hbm), (raw_ref, raw_hbm),
+            )
+        )
+    ]
+
+    def token_copy(which, k):
+        source, target = ((tok_hbm, x_ref), (grad_hbm, dy_hbm))[which]
+        return send(
+            source.at[place.flipped(k)], target.at[pl.ds(k * cells, cells)],
+            tok_send.at[which, k - 1], tok_recv.at[which, k - 1], place.plane(k),
+        )
+
+    def kv_copy(which, chunk):
+        source, target = ((k_ref, k1_hbm), (v_ref, v1_hbm))[which]
+        span = pl.ds(chunk * cells, cells if chunk == 0 else rows - cells)
+        return send(
+            source.at[span], target.at[span], kv_send.at[which, chunk], kv_recv.at[which, chunk],
+            place.pair(),
+        )
+
+    def vector(start, count=1):
+        return small_ref[:, start * width : (start + count) * width].astype(F32)
+
+    def project(start, size, chunk):
+        span = slice(start, start + size)
+        x = x_ref[span, :].astype(F32)
+        normed = x * lax.rsqrt(jnp.mean(x * x, axis=-1, keepdims=True) + NORM_EPSILON)
+        hidden = normed * (1.0 + mod_ref[:, width : 2 * width]) + mod_ref[:, :width]
+        hidden = hidden.astype(BF16)
+        hid_ref[span, :] = hidden
+        for part in (1, 2, 0):
+            raw = mm(hidden, inw_ref[:, part * width : (part + 1) * width]) + vector(IN_BIAS + part)
+            if part == 2:
+                v_ref[span, :] = raw.astype(BF16)
+                for which in (0, 1):
+                    kv_copy(which, chunk).start()
+                continue
+            raw_ref[span, part * width : (part + 1) * width] = raw.astype(BF16)
+            factor = lax.rsqrt(head_sum(raw * raw, head) * (1.0 / head) + NORM_EPSILON)
+            scaled = raw * factor * vector((Q_GAIN, K_GAIN)[part])
+            turned = turn(scaled, cos_ref[span, :], sin_ref[span, :], head).astype(BF16)
+            (q_ref, k_ref)[part][span, :] = turned
+
+    for load in loads:
+        load.start()
+    meet([place.pair()] + [place.plane(k) for k in (1, 2, 3)])
+    for k in (3, 1, 2):
+        token_copy(0, k).start()
+
+    quarter = head // 4
+    lane = lax.broadcasted_iota(jnp.int32, (1, 128), 1)
+    rate = jnp.exp(-math.log(10000.0) / quarter * lax.rem(lane, quarter).astype(F32))
+    by_row = lax.rem(lane, head) < head // 2
+    sign = jnp.where(lax.rem(lane, 2 * quarter) < quarter, -1.0, 1.0)
+    cell = lax.broadcasted_iota(jnp.int32, (cells, 128), 0)
+    row, col = cell // tile_cols, lax.rem(cell, tile_cols)
+    for k in range(4):
+        there = place.flipped(k)
+        down = (there // 2) * (cells // tile_cols) + row
+        across = (2 * lax.rem(there, 2) + core) * tile_cols + col
+        angle = jnp.where(by_row, down, across).astype(F32) * rate
+        cos_ref[k * cells : (k + 1) * cells, :] = jnp.cos(angle)
+        sin_ref[k * cells : (k + 1) * cells, :] = sign * jnp.sin(angle)
+    loads[1].wait()
+    mod_ref[...] = mm(act_ref[...], modw_ref[...])[:1] + vector(0, 6)
+    loads[0].wait()
+    loads[2].wait()
+    project(0, cells, 0)
+    loads[3].wait()
+    stores[0].start()
+    for k in (1, 2, 3):
+        token_copy(0, k).wait()
+    for k in (3, 1, 2):
+        token_copy(1, k).start()
+    stores[1].start()
+    project(cells, rows - cells, 1)
+    for store in stores[2:]:
+        store.start()
+    for which in (0, 1):
+        for chunk in (0, 1):
+            kv_copy(which, chunk).wait()
+    for k in (1, 2, 3):
+        token_copy(1, k).wait()
+    for store in stores:
+        store.wait()
+
+
+def front_call(tokens, grads, act, small, modw, inw, head, tile_cols):
+    images, cells, width = tokens.shape
+    rows = images * cells
+    low = lambda *shape: jax.ShapeDtypeStruct(shape, BF16)
+    vmem = lambda *shape: pltpu.VMEM(shape, BF16)
+    anywhere = pl.BlockSpec(memory_space=pl.ANY)
+    inside = pl.BlockSpec(memory_space=pltpu.VMEM)
+    sems = lambda *shape: pltpu.SemaphoreType.DMA(shape)
+    return pl.pallas_call(
+        functools.partial(front_kernel, head, tile_cols),
+        in_specs=[anywhere] * 2 + [inside] * 2 + [anywhere] * 2,
+        out_specs=[anywhere] * 9 + [inside] * 3,
+        out_shape=[low(rows, width)] * 8
+        + [
+            low(rows, 2 * width), jax.ShapeDtypeStruct((1, 6 * width), F32),
+            jax.ShapeDtypeStruct((rows, 128), F32), jax.ShapeDtypeStruct((rows, 128), F32),
+        ],
+        scratch_shapes=[
+            vmem(rows, width), vmem(cells, width), vmem(rows, width), vmem(rows, width),
+            vmem(rows, width), vmem(rows, width), vmem(rows, 2 * width), vmem(*modw.shape),
+            vmem(*inw.shape), sems(4), sems(7), sems(2, 3), sems(2, 3), sems(2, 2), sems(2, 2),
+        ],
+        compiler_params=pltpu.CompilerParams(
+            vmem_limit_bytes=VMEM_LIMIT, collective_id=3, has_side_effects=True
+        ),
+        name="front",
+    )(tokens, grads, act, small, modw, inw)
 
 
 Z_FIRST = (False, False, False, False)
@@ -990,7 +1143,7 @@
                 grad = both(dv0_s) + both(dv_in)
             else:
                 grad = both(dq_s) if part == 0 else both(dk0_s) + both(dk_in)
-                gain = (qgain_ref, kgain_ref)[part][:, :256]
+                gain = (qgain_ref, kgain_ref)[part][:, :256].astype(F32)
                 raw = raw_ref[:, span].astype(F32)
                 factor = lax.rsqrt(head_sum(raw * raw, head) * (1.0 / head) + NORM_EPSILON)
                 normed = raw * factor
@@ -1093,7 +1246,7 @@
 
 
 def back_call(
-    q, k0, k1, v0, v1, grad_mixed, mixed, inverse, grown, mod, qgain, kgain, cosine, sine, d_out,
+    q, k0, k1, v0, v1, grad_mixed, mixed, inverse, grown, mod, small_vectors, cosine, sine, d_out,
     totals, early, raw, hidden, x, grad_middle, weight, output_rows, head,
 ):
     rows, width = q.shape
@@ -1101,7 +1254,8 @@
     low = lambda *shape: jax.ShapeDtypeStruct(shape, BF16)
     pair = pl.BlockSpec((rows, 128), lambda s: (0, jnp.minimum(s, 5)))
     anywhere = pl.BlockSpec(memory_space=pl.ANY)
-    small = [mod, qgain, kgain, cosine, sine, d_out, totals, early]
+    small = [mod, small_vectors, small_vectors, cosine, sine, d_out, totals, early]
+    gain = lambda at: pl.BlockSpec((1, width), lambda s: (0, at), pipeline_mode=pl.Buffered(1))
     out_shape = [
         low(4, rows // 4, width), low(4, rows // 4, width),
         low(2, 4, 3, width // 4, 256), low(2, 4, GROUPS, part, half),
@@ -1114,7 +1268,8 @@
         grid=(7,),
         in_specs=[pair] * 8
         + [pl.BlockSpec((2, rows, 2 * rows), lambda s: (jnp.minimum(s, 5), 0, 0))]
-        + [once(each.shape) for each in small]
+        + [once(mod.shape), gain(Q_GAIN), gain(K_GAIN)]
+        + [once(each.shape) for each in small[3:]]
         + [anywhere] * 6,
         out_specs=[anywhere] * 6,
         out_shape=out_shape,
@@ -1361,13 +1516,6 @@
     tiles = tokens.reshape(image_count, cells, width)
     grads = cotangent.reshape(image_count, cells, width)
 
-    def exchange(blocks):
-        return [take(blocks, place)] + [
-            moves.plane(take(blocks, place ^ k), k) for k in range(1, 4)
-        ]
-
-    x = jnp.concatenate(exchange(tiles), axis=0)
-
     half_width = width // 2
     step = take(timesteps, place).astype(F32)
     label = take(labels, place)
@@ -1375,6 +1523,49 @@
     features = jnp.concatenate([jnp.cos(step * rates), jnp.sin(step * rates)])
     condition = features + take(class_table, label).astype(F32)
     cond_act = jax.nn.silu(condition).astype(BF16)
+    if nb == 4 and hidden_width == 16 * 128:
+        act = jnp.broadcast_to(cond_act[None], (16, width))
+        small = small_row(
+            width, head, modulate_bias, inproj_bias, query_gain, key_gain, outproj_bias, down_bias,
+            gate_up_bias,
+        )
+        known = jnp.stack([condition, jnp.broadcast_to(label.astype(F32), (width,))])
+        known = jnp.where(core == 0, known, 0.0)
+        x, dy, hidden_one, q, k0, v0, k1, v1, raw, mod, cosine, sine = front_call(
+            tiles, grads, act, small, modulate_weight, inproj_weight, head, tile_cols
+        )
+        mixed, grown, inverse = attend_call(q, k0, k1, v0, v1, head)
+        attended, middle, hidden_two, hidden_two_t, grad_feed = middle_call(
+            mixed, x, dy, mod, outproj_weight, small, OUT_BIAS
+        )
+        output_rows, grad_middle, grad_mixed, d_out, sums_two, totals = feed_turn_call(
+            hidden_two, hidden_two_t, grad_feed, gate_up_weight, down_weight, middle, attended, dy,
+            mixed, mod, outproj_weight, small, known,
+        )
+        output, grad_tokens, feeds, projs, early, late = back_call(
+            q, k0, k1, v0, v1, grad_mixed, mixed, inverse, grown, mod, small, cosine, sine, d_out,
+            totals, sums_two, raw, hidden_one, x, grad_middle, inproj_weight, output_rows, head,
+        )
+        (
+            grad_condition, grad_table, grad_mod_w, grad_mod_b, grad_in_w, grad_in_b, grad_q_gain,
+            grad_k_gain, grad_out_w, grad_out_b, grad_gu_w, grad_gu_b, grad_down_w, grad_down_b,
+        ) = finish_call(
+            feeds, projs, early, late, modulate_weight, head, class_count, hidden_width
+        )
+        return (
+            output.reshape(tokens.shape), grad_tokens.reshape(tokens.shape), grad_condition,
+            grad_table, grad_mod_w, grad_mod_b[0], grad_in_w, grad_in_b[0], grad_q_gain[0],
+            grad_k_gain[0], grad_out_w, grad_out_b[0], grad_gu_w, grad_gu_b[0], grad_down_w,
+            grad_down_b[0],
+        )
+
+    def exchange(blocks):
+        return [take(blocks, place)] + [
+            moves.plane(take(blocks, place ^ k), k) for k in range(1, 4)
+        ]
+
+    x = jnp.concatenate(exchange(tiles), axis=0)
+
     mod = modulation_call(
         jnp.broadcast_to(cond_act[None], (16, width)), modulate_weight, modulate_bias[None]
     )[:1]
@@ -1408,77 +1599,51 @@
 
     unit = 256
     blocks = hidden_width // unit
-    quick = nb == 4 and hidden_width == 16 * 128
-    if quick:
-        known = jnp.stack([condition, jnp.broadcast_to(label.astype(F32), (width,))])
-        known = jnp.where(core == 0, known, 0.0)
-        output_rows, grad_middle, grad_mixed, d_out, sums_two, totals = feed_turn_call(
-            hidden_two, hidden_two_t, grad_feed, gate_up_weight, gate_up_bias[None], down_weight,
-            middle, attended, dy, mixed, mod, outproj_weight, down_bias[None], known,
-        )
-        output, grad_tokens, feeds, projs, early, late = back_call(
-            q, k0, k1, v0, v1, grad_mixed, mixed, inverse, grown, mod, qgain, kgain, cosine, sine,
-            d_out, totals, sums_two, raw, hidden_one, x, grad_middle, inproj_weight, output_rows,
-            head,
-        )
-        (
-            grad_condition, grad_table, grad_mod_w, grad_mod_b, grad_in_w, grad_in_b, grad_q_gain,
-            grad_k_gain, grad_out_w, grad_out_b, grad_gu_w, grad_gu_b, grad_down_w, grad_down_b,
-        ) = finish_call(
-            feeds, projs, early, late, modulate_weight, head, class_count, hidden_width
-        )
-        return (
-            output.reshape(tokens.shape), grad_tokens.reshape(tokens.shape), grad_condition,
-            grad_table, grad_mod_w, grad_mod_b[0], grad_in_w, grad_in_b[0], grad_q_gain[0],
-            grad_k_gain[0], grad_out_w, grad_out_b[0], grad_gu_w, grad_gu_b[0], grad_down_w,
-            grad_down_b[0],
-        )
-    else:
-        feed, grad_hidden, d_down, d_gate, d_bias = feed_call(
-            hidden_two, hidden_two_t, grad_feed, gate_up_weight, gate_up_bias[None], down_weight,
-            jnp.zeros((rows, width), F32), jnp.zeros((rows, width), F32), 0, 1, unit,
-        )
-        output_rows, grad_middle, grad_mixed, d_out, sums_two = turn_call(
-            feed, grad_hidden, middle, attended, dy, grad_feed, mixed, mod, outproj_weight,
-            down_bias[None],
-        )
-        gate_bias = d_bias.reshape(blocks, 2, unit).transpose(1, 0, 2)
-        dq, dk0, dk1, dv0, dv1 = attend_back_call(
-            q, k0, k1, v0, v1, grown, grad_mixed, mixed, inverse, head
-        )
-        dk1, dv1 = moves.pair(dk1), moves.pair(dv1)
-        grad_x, d_in, sums_one, in_bias = project_back_call(
-            dq, dk0, dk1, dv0, dv1, raw, hidden_one, x, grad_middle, mod, inproj_weight, qgain,
-            kgain, cosine, sine, head,
-        )
-
-        def give_back(rows_out):
-            parts = rows_out.reshape(4, cells, width)
-            got = [parts[0]] + [moves.plane(parts[k], k) for k in range(1, 4)]
-            return regroup(got, place).reshape(tokens.shape)
-
-        output = give_back(output_rows)
-        grad_tokens = give_back(grad_x)
-        slice_rows = width // nb
-
-        def scatter(d):
-            d = lax.psum_scatter(d.astype(BF16), "batch", scatter_dimension=0, tiled=True)
-            return lax.psum(d, ("gy", "gx")).astype(F32)
-
-        def joined(d):
-            return jnp.concatenate([d[0], d[1]], axis=1)
-
-        grad_down_w = scatter(d_down.reshape(hidden_width, width))
-        grad_gu_w = scatter(
-            d_gate.transpose(2, 1, 0, 3).reshape(width, 2 * hidden_width)
-        )
-        grad_out_w = scatter(joined(d_out))
-        grad_in_w = scatter(joined(d_in))
-        gain_sums = sums_one[2:4].reshape(2, heads, head).sum(axis=1)
-        early = jnp.concatenate([sums_two[:6].reshape(-1), gate_bias.reshape(-1)])
-        late = jnp.concatenate(
-            [sums_one[:2].reshape(-1), in_bias.reshape(-1), gain_sums.reshape(-1)]
-        )
+    feed, grad_hidden, d_down, d_gate, d_bias = feed_call(
+        hidden_two, hidden_two_t, grad_feed, gate_up_weight, gate_up_bias[None], down_weight,
+        jnp.zeros((rows, width), F32), jnp.zeros((rows, width), F32), 0, 1, unit,
+    )
+    output_rows, grad_middle, grad_mixed, d_out, sums_two = turn_call(
+        feed, grad_hidden, middle, attended, dy, grad_feed, mixed, mod, outproj_weight,
+        down_bias[None],
+    )
+    gate_bias = d_bias.reshape(blocks, 2, unit).transpose(1, 0, 2)
+    dq, dk0, dk1, dv0, dv1 = attend_back_call(
+        q, k0, k1, v0, v1, grown, grad_mixed, mixed, inverse, head
+    )
+    dk1, dv1 = moves.pair(dk1), moves.pair(dv1)
+    grad_x, d_in, sums_one, in_bias = project_back_call(
+        dq, dk0, dk1, dv0, dv1, raw, hidden_one, x, grad_middle, mod, inproj_weight, qgain,
+        kgain, cosine, sine, head,
+    )
+
+    def give_back(rows_out):
+        parts = rows_out.reshape(4, cells, width)
+        got = [parts[0]] + [moves.plane(parts[k], k) for k in range(1, 4)]
+        return regroup(got, place).reshape(tokens.shape)
+
+    output = give_back(output_rows)
+    grad_tokens = give_back(grad_x)
+    slice_rows = width // nb
+
+    def scatter(d):
+        d = lax.psum_scatter(d.astype(BF16), "batch", scatter_dimension=0, tiled=True)
+        return lax.psum(d, ("gy", "gx")).astype(F32)
+
+    def joined(d):
+        return jnp.concatenate([d[0], d[1]], axis=1)
+
+    grad_down_w = scatter(d_down.reshape(hidden_width, width))
+    grad_gu_w = scatter(
+        d_gate.transpose(2, 1, 0, 3).reshape(width, 2 * hidden_width)
+    )
+    grad_out_w = scatter(joined(d_out))
+    grad_in_w = scatter(joined(d_in))
+    gain_sums = sums_one[2:4].reshape(2, heads, head).sum(axis=1)
+    early = jnp.concatenate([sums_two[:6].reshape(-1), gate_bias.reshape(-1)])
+    late = jnp.concatenate(
+        [sums_one[:2].reshape(-1), in_bias.reshape(-1), gain_sums.reshape(-1)]
+    )
 
     def everywhere(vector):
         halves = vector.reshape(2, -1)

time: 233 us -> 228 us (0.979)
  Pallas kernels: 194 us -> 207 us
  starting transfers between devices: 8.75 us -> 0 us
  waiting for transfers between devices: 5.97 us -> 0 us
  other arithmetic: 7.89 us -> 4.08 us
    pallas_call x2 -> x1, Pallas kernels: 12.9 us -> 25.7 us  [front_call(): pl.pallas_call(functools.partial(front_kernel, head, tile_cols), in_specs...]
    ppermute x8 -> x0, starting transfers between devices: 8.75 us -> none  [flip(): return lax.ppermute(value, AXES, pairs)]
    ppermute x8 -> x0, waiting for transfers between devices: 5.97 us -> none  [flip(): return lax.ppermute(value, AXES, pairs)]
    unnamed x30 -> x12, local copies, waits for them, and re-layouts: 2.99 us -> 5.73 us
    broadcast_in_dim x6 -> x2, local copies, waits for them, and re-layouts: 3.62 us -> 1.27 us  [the longest x1 0.65 us: small_row(): jnp.concatenate([modulate, inproj, jnp.tile(qgain, heads), jnp.tile(kgain...]
  transfers between devices with their start and end apart: 8 -> 0, of which waited for: 2 -> 0; matrix products, arithmetic and copies ran while one was open for 5% -> 0% of each run, Pallas kernels for 3% -> 0%
where the time goes in v5:
time: 228 us; the launch traced here: 227 us
  Pallas kernels  207 us (91%)
  local copies, waits for them, and re-layouts  11.8 us (5%)
  other arithmetic  4.08 us (2%)
  between operations  3.99 us (2%)
    pallas_call x1, Pallas kernels, back_call(): pl.pallas_call(functools.partial(back_kernel, head), grid=(7,), in_specs=...  93.1 us
    pallas_call x1, Pallas kernels, feed_turn_call(): pl.pallas_call(feed_turn_kernel, grid=(9,), in_specs=[once((rows, width))...  57.1 us
    pallas_call x1, Pallas kernels, front_call(): pl.pallas_call(functools.partial(front_kernel, head, tile_cols), in_specs...  25.7 us
    pallas_call x1, Pallas kernels, finish_call(): pl.pallas_call(functools.partial(finish_kernel, head), in_specs=[pl.Block...  15.2 us
    pallas_call x1, Pallas kernels, attend_call(): pl.pallas_call(functools.partial(attend_kernel, head ** (-0.5)), grid=(wi...  11.9 us
    unnamed x12, local copies, waits for them, and re-layouts  5.73 us

profile of v5, /device:TPU:0, one launch (start us, length us, event | category | flops | bytes accessed | tf_op | source)
XLA Modules:
  0.0 227.3 jit_solution(10381971565742240666)
XLA Ops:
  0.7 1.2 dynamic_slice.12
  4.5 1.2 dynamic_slice.11
  6.4 0.1 fusion
  6.5 0.7 convert_reduce_fusion
  7.2 0.7 tile.8
  7.9 0.1 tile.9
  8.0 0.7 tile.20
  8.6 0.1 tile.21
  8.7 0.6 pad_select_fusion.known_ref
  9.3 0.6 broadcast_in_dim.16.act_ref
  9.9 0.9 dynamic-update-slice
  10.9 0.9 dynamic-update-slice.1
  11.8 0.2 dynamic-update-slice.2
  12.0 0.2 dynamic-update-slice.3
  12.2 0.9 dynamic-update-slice.4
  13.0 0.9 dynamic-update-slice.5
  13.9 0.9 dynamic-update-slice.6
  14.8 0.7 broadcast_in_dim.17.small_ref.bias_ref.bg0.bg1.bu0.bu1.dbias_ref.qgain_ref.kgain_ref
  15.4 25.7 %front.1 = (bf16[512,768]{1,0:T(8,128)(2,1)}, bf16[512,768]{1,0:T(8,128)(2,1)}, bf16[512,768]{1,0:T(8,128)(2,1)}, bf16[512,768]{1,0:T(8,128)(2,1)}, bf16[512,768...) custom-call(bf16[4,128,768]{2,1,0:T(8,128)(2,1)} %bitcast.11, ...), custom_call_target="tpu_custom_call" | custom-call | tf_op jit(solution)/shard_map/front/pallas_call | solution.py:831
  41.1 11.9 %attend.1 = (bf16[512,768]{1,0:T(8,128)(2,1)}, bf16[12,512,1024]{2,1,0:T(8,128)(2,1)}, f32[512,768]{1,0:T(8,128)}) custom-call(bf16[512,768]{1,0:T(8,128)(2,1)} %get-tuple-element.62.q_ref, bf16[512,768]{1,0:T(8,128)(2,1)} %get-tuple-element.63.k0_ref, bf16[512,768]{1,0:T(8,128)(2,1)} %get-tuple-element.64.k1_ref, ...), custom_call_target="tpu_custom_call" | custom-call | tf_op jit(solution)/shard_map/attend/pallas_call | solution.py:155
  53.1 4.4 %middle.1 = (bf16[512,768]{1,0:T(8,128)(2,1)}, f32[512,768]{1,0:T(8,128)}, bf16[512,768]{1,0:T(8,128)(2,1)}, bf16[768,512]{1,0:T(8,128)(2,1)}, bf16[512,768]{1,0:T(8,128)(2,1)}) custom-call(bf16[512,768]{1,0:T(8,128)(2,1)} %get-tuple-element.67.mix_ref, bf16[512,768]{1,0:T(8,128)(2,1)} %get-tuple-element.68.x_ref.x_hbm, ...), custom_call_target="tpu_custom_call" | custom-call | tf_op jit(solution)/shard_map/middle/pallas_call | solution.py:239
  57.5 57.1 %feed_turn.1 = (bf16[512,768]{1,0:T(8,128)(2,1)}, f32[512,768]{1,0:T(8,128)}, bf16[512,768]{1,0:T(8,128)(2,1)}, bf16[2,768,384]{2,1,0:T(8,128)(2,1)}, f32[2,8,76...) custom-call(bf16[512,768]{1,0:T(8,128)(2,1)} %get-tuple-element.71.h2_ref, bf16[768,512]{1,0:T(8,128)(2,1)} %get-tuple-element.72.h2t_ref, ...), custom_call_target="tpu_custom_call" | custom-call | tf_op jit(solution)/shard_map/feed_turn/pallas_call | solution.py:668
  114.6 93.1 %back.1 = (bf16[4,128,768]{2,1,0:T(8,128)(2,1)}, bf16[4,128,768]{2,1,0:T(8,128)(2,1)}, bf16[2,4,3,192,256]{4,3,2,1,0:T(8,128)(2,1)}, bf16[2,4,4,48,384]{4,3,2,1,...) custom-call(bf16[512,768]{1,0:T(8,128)(2,1)} %get-tuple-element.62.q_ref, ...), custom_call_target="tpu_custom_call" | custom-call | tf_op jit(solution)/shard_map/back/pallas_call | solution.py:1266
  207.7 0.0 copy-start.1
  207.7 15.2 %finish.1 = (f32[4,768]{1,0:T(4,128)}, f32[1001,768]{1,0:T(8,128)}, f32[192,4608]{1,0:T(8,128)}, f32[1,1152]{1,0:T(1,128)}, f32[192,2304]{1,0:T(8,128)}, /*index...) custom-call(bf16[2,4,3,192,256]{4,3,2,1,0:T(8,128)(2,1)} %get-tuple-, ...), custom_call_target="tpu_custom_call" | custom-call | tf_op jit(solution)/shard_map/finish/pallas_call | solution.py:1434
  222.9 0.0 copy-start
  222.9 1.4 reduce.2
  224.2 1.3 reduce.1
  225.5 0.0 copy-done.1
  225.5 0.9 copy.42
  226.4 0.0 copy-done
  226.4 0.9 copy.43
  (1 shorter events, 0.0 us)
Async XLA Ops:
  207.7 17.9 %copy-start.1 = (bf16[4,128,768]{2,1,0:T(8,128)(2,1)S(1)}, bf16[4,128,768]{2,1,0:T(8,128)(2,1)}, u32[]{:S(2)}) copy-start(bf16[4,128,768]{2,1,0:T(8,128)(2,1)} %get-tuple-element.88) | copy-start | bytes 2359300
  222.9 3.6 %copy-start = (bf16[4,128,768]{2,1,0:T(8,128)(2,1)S(1)}, bf16[4,128,768]{2,1,0:T(8,128)(2,1)}, u32[]{:S(2)}) copy-start(bf16[4,128,768]{2,1,0:T(8,128)(2,1)} %get-tuple-element.89) | copy-start | bytes 2359300

commit v6 on v5

--- a/solution.py
+++ b/solution.py
@@ -849,7 +849,7 @@
     )(tokens, grads, act, small, modw, inw)
 
 
-Z_FIRST = (False, False, False, False)
+Z_FIRST = (False, False, True, False)
 GROUPS = 4
 
 
@@ -953,7 +953,6 @@
         return send(here, here, proj_send.at[3], proj_recv.at[3], place.pair())
 
     smalls = ((early_ref, early_in, early_all, 8), (late_ref, late_in, late_all, 4))
-    hops = [place.plane(1), place.plane(2), place.depth(1), place.depth(2)]
 
     def small_pair(which):
         source, target, _, count = smalls[which]
@@ -962,29 +961,45 @@
             place.pair(),
         )
 
-    def small_hop(which, i):
-        _, _, full_ref, _ = smalls[which]
-        have = 1 << i
+    def small_plane(which, k):
+        full_ref = smalls[which][2]
+        return send(
+            full_ref.at[core, pl.ds(0, 1)], full_ref.at[core, pl.ds(k, 1)],
+            small_send.at[which, k], small_recv.at[which, k], place.plane(k),
+        )
+
+    def small_depth(which, d):
+        full_ref = smalls[which][2]
+        have = 4 * d
         return send(
             full_ref.at[core, pl.ds(0, have)], full_ref.at[core, pl.ds(have, have)],
-            small_send.at[which, 1 + i], small_recv.at[which, 1 + i], hops[i],
+            small_send.at[which, 3 + d], small_recv.at[which, 3 + d], place.depth(d),
         )
 
     def small_last(which):
         here = smalls[which][2].at[core]
         return send(
-            here, here, small_send.at[which, 5], small_recv.at[which, 5], place.pair()
+            here, here, small_send.at[which, 6], small_recv.at[which, 6], place.pair()
         )
 
     def small_begin(which):
         source, target, full_ref, _ = smalls[which]
         small_pair(which).wait_recv()
         full_ref[core, 0] = source[core] + target[...]
-        small_hop(which, 0).start()
+        for k in (1, 2, 3):
+            small_plane(which, k).start()
 
     def small_next(which, i):
-        small_hop(which, i).wait_recv()
-        (small_hop(which, i + 1) if i < 3 else small_last(which)).start()
+        if i == 0:
+            for k in (1, 2, 3):
+                small_plane(which, k).wait_recv()
+            small_depth(which, 1).start()
+        elif i == 1:
+            small_depth(which, 1).wait_recv()
+            small_depth(which, 2).start()
+        else:
+            small_depth(which, 2).wait_recv()
+            small_last(which).start()
 
     def start_group(g):
         pair_copy(g).wait_recv()
@@ -1095,9 +1110,9 @@
         start_group(3)
         small_begin(0)
 
-    for i in range(4):
-
-        @pl.when(step == 2 + i)
+    for i in range(3):
+
+        @pl.when(step == 3 + i)
         def _(i=i):
             small_next(0, i)
 
@@ -1121,8 +1136,6 @@
                 + z_in[1, i].astype(F32)
                 + z_in[2, i].astype(F32)
             ).astype(BF16)
-        for k in (1, 2, 3):
-            feed_copy(k).start()
 
     @pl.when((step >= 2) & (lax.rem(step, 2) == 0))
     def _():
@@ -1178,44 +1191,45 @@
     @pl.when(step == 6)
     def _():
         pair_copy(2).start()
-        go_on(0)
-        go_on(1)
+        grad_hidden = gh_ref[...]
         loads[3].wait()
         loads[4].wait()
-        grad_hidden = gh_ref[...]
         x = x_ref[...].astype(F32)
         factor = lax.rsqrt(jnp.mean(x * x, axis=-1, keepdims=True) + NORM_EPSILON)
         normed = x * factor
         late_ref[0, 0:1, :] = col_sum(grad_hidden)
         late_ref[0, 1:2, :] = col_sum(grad_hidden * normed)
         late_ref[1, 3:4, :] = jnp.zeros((1, width), F32)
+        small_pair(1).start()
+        go_on(0)
+        go_on(1)
+        small_begin(1)
+        start_group(2)
         grad_normed = grad_hidden * (1.0 + mod_ref[:, width : 2 * width])
         back = factor * (
             grad_normed - normed * jnp.mean(grad_normed * normed, axis=-1, keepdims=True)
         )
-        small_pair(1).start()
-        start_group(2)
         gx_ref[...] = (gmid_ref[...] + back).astype(BF16)
-        small_begin(1)
         for k in (1, 2, 3):
             token_copy(1, k).start()
         own_tokens(1).start()
+        for k in (1, 2, 3):
+            feed_copy(k).start()
+        small_next(1, 0)
         finish(3)
-        small_next(1, 0)
         finish(0)
+        small_next(1, 1)
         finish(1)
-        small_next(1, 1)
+        small_next(1, 2)
         go_on(2)
-        small_next(1, 2)
+        finish(2)
+        for k in (1, 2, 3):
+            proj_copy(k).start()
         for k in (1, 2, 3):
             feed_copy(k).wait_recv()
         for k in (1, 2, 3):
             feed_copy(k).wait_send()
         feed_pair().start()
-        finish(2)
-        for k in (1, 2, 3):
-            proj_copy(k).start()
-        small_next(1, 3)
         for k in (1, 2, 3):
             proj_copy(k).wait()
         proj_pair().start()
@@ -1224,8 +1238,10 @@
             for k in (1, 2, 3):
                 token_copy(which, k).wait()
             small_pair(which).wait_send()
-            for i in range(4):
-                small_hop(which, i).wait_send()
+            for k in (1, 2, 3):
+                small_plane(which, k).wait_send()
+            for d in (1, 2):
+                small_depth(which, d).wait_send()
             small_last(which).wait()
             stores[which].start()
             for p in range(6):
@@ -1289,7 +1305,7 @@
             sems(9), sems(2), sems(2, 6), sems(2, 6), sems(GROUPS), sems(GROUPS),
             sems(GROUPS, 3), sems(GROUPS, 3), sems(GROUPS, 3), sems(GROUPS, 3),
             sems(3), sems(3), sems(2, 3), sems(2, 3), sems(4), sems(4), sems(4), sems(4),
-            sems(2, 6), sems(2, 6),
+            sems(2, 7), sems(2, 7),
         ],
         compiler_params=pltpu.CompilerParams(
             vmem_limit_bytes=VMEM_LIMIT, collective_id=2, has_side_effects=True

time: 228 us -> 221 us (0.969)
  Pallas kernels: 207 us -> 200 us
    pallas_call x1, Pallas kernels: 93.1 us -> 85.7 us  [back_call(): pl.pallas_call(functools.partial(back_kernel, head), grid=(7,), in_specs=...]
where the time goes in v6:
time: 221 us; the launch traced here: 220 us
  Pallas kernels  200 us (90%)
  local copies, waits for them, and re-layouts  11.8 us (5%)
  other arithmetic  4.08 us (2%)
  between operations  3.99 us (2%)
    pallas_call x1, Pallas kernels, back_call(): pl.pallas_call(functools.partial(back_kernel, head), grid=(7,), in_specs=...  85.7 us
    pallas_call x1, Pallas kernels, feed_turn_call(): pl.pallas_call(feed_turn_kernel, grid=(9,), in_specs=[once((rows, width))...  57.1 us
    pallas_call x1, Pallas kernels, front_call(): pl.pallas_call(functools.partial(front_kernel, head, tile_cols), in_specs...  25.7 us
    pallas_call x1, Pallas kernels, finish_call(): pl.pallas_call(functools.partial(finish_kernel, head), in_specs=[pl.Block...  15.2 us
    pallas_call x1, Pallas kernels, attend_call(): pl.pallas_call(functools.partial(attend_kernel, head ** (-0.5)), grid=(wi...  11.9 us
    unnamed x12, local copies, waits for them, and re-layouts  5.73 us

profile of v6, /device:TPU:0, one launch (start us, length us, event | category | flops | bytes accessed | tf_op | source)
XLA Modules:
  0.0 219.9 jit_solution(13453581026428250075)
XLA Ops:
  0.7 1.2 dynamic_slice.12
  4.5 1.2 dynamic_slice.11
  6.4 0.1 fusion
  6.5 0.7 convert_reduce_fusion
  7.2 0.7 tile.8
  7.9 0.1 tile.9
  8.0 0.7 tile.20
  8.6 0.1 tile.21
  8.7 0.6 pad_select_fusion.known_ref
  9.3 0.6 broadcast_in_dim.16.act_ref
  9.9 0.9 dynamic-update-slice
  10.9 0.9 dynamic-update-slice.1
  11.8 0.2 dynamic-update-slice.2
  12.0 0.2 dynamic-update-slice.3
  12.2 0.9 dynamic-update-slice.4
  13.0 0.9 dynamic-update-slice.5
  13.9 0.9 dynamic-update-slice.6
  14.8 0.7 broadcast_in_dim.17.small_ref.bias_ref.bg0.bg1.bu0.bu1.dbias_ref.qgain_ref.kgain_ref
  15.4 25.7 %front.1 = (bf16[512,768]{1,0:T(8,128)(2,1)}, bf16[512,768]{1,0:T(8,128)(2,1)}, bf16[512,768]{1,0:T(8,128)(2,1)}, bf16[512,768]{1,0:T(8,128)(2,1)}, bf16[512,768...) custom-call(bf16[4,128,768]{2,1,0:T(8,128)(2,1)} %bitcast.11, ...), custom_call_target="tpu_custom_call" | custom-call | tf_op jit(solution)/shard_map/front/pallas_call | solution.py:831
  41.1 11.9 %attend.1 = (bf16[512,768]{1,0:T(8,128)(2,1)}, bf16[12,512,1024]{2,1,0:T(8,128)(2,1)}, f32[512,768]{1,0:T(8,128)}) custom-call(bf16[512,768]{1,0:T(8,128)(2,1)} %get-tuple-element.62.q_ref, bf16[512,768]{1,0:T(8,128)(2,1)} %get-tuple-element.63.k0_ref, bf16[512,768]{1,0:T(8,128)(2,1)} %get-tuple-element.64.k1_ref, ...), custom_call_target="tpu_custom_call" | custom-call | tf_op jit(solution)/shard_map/attend/pallas_call | solution.py:155
  53.1 4.4 %middle.1 = (bf16[512,768]{1,0:T(8,128)(2,1)}, f32[512,768]{1,0:T(8,128)}, bf16[512,768]{1,0:T(8,128)(2,1)}, bf16[768,512]{1,0:T(8,128)(2,1)}, bf16[512,768]{1,0:T(8,128)(2,1)}) custom-call(bf16[512,768]{1,0:T(8,128)(2,1)} %get-tuple-element.67.mix_ref, bf16[512,768]{1,0:T(8,128)(2,1)} %get-tuple-element.68.x_ref.x_hbm, ...), custom_call_target="tpu_custom_call" | custom-call | tf_op jit(solution)/shard_map/middle/pallas_call | solution.py:239
  57.5 57.1 %feed_turn.1 = (bf16[512,768]{1,0:T(8,128)(2,1)}, f32[512,768]{1,0:T(8,128)}, bf16[512,768]{1,0:T(8,128)(2,1)}, bf16[2,768,384]{2,1,0:T(8,128)(2,1)}, f32[2,8,76...) custom-call(bf16[512,768]{1,0:T(8,128)(2,1)} %get-tuple-element.71.h2_ref, bf16[768,512]{1,0:T(8,128)(2,1)} %get-tuple-element.72.h2t_ref, ...), custom_call_target="tpu_custom_call" | custom-call | tf_op jit(solution)/shard_map/feed_turn/pallas_call | solution.py:668
  114.6 85.7 %back.1 = (bf16[4,128,768]{2,1,0:T(8,128)(2,1)}, bf16[4,128,768]{2,1,0:T(8,128)(2,1)}, bf16[2,4,3,192,256]{4,3,2,1,0:T(8,128)(2,1)}, bf16[2,4,4,48,384]{4,3,2,1,...) custom-call(bf16[512,768]{1,0:T(8,128)(2,1)} %get-tuple-element.62.q_ref, ...), custom_call_target="tpu_custom_call" | custom-call | tf_op jit(solution)/shard_map/back/pallas_call | solution.py:1282
  200.3 0.0 copy-start.1
  200.3 15.2 %finish.1 = (f32[4,768]{1,0:T(4,128)}, f32[1001,768]{1,0:T(8,128)}, f32[192,4608]{1,0:T(8,128)}, f32[1,1152]{1,0:T(1,128)}, f32[192,2304]{1,0:T(8,128)}, /*index...) custom-call(bf16[2,4,3,192,256]{4,3,2,1,0:T(8,128)(2,1)} %get-tuple-, ...), custom_call_target="tpu_custom_call" | custom-call | tf_op jit(solution)/shard_map/finish/pallas_call | solution.py:1450
  215.5 0.0 copy-start
  215.5 1.4 reduce.2
  216.9 1.3 reduce.1
  218.2 0.0 copy-done.1
  218.2 0.9 copy.42
  219.0 0.0 copy-done
  219.0 0.9 copy.43
  (1 shorter events, 0.0 us)
Async XLA Ops:
  200.3 17.9 %copy-start.1 = (bf16[4,128,768]{2,1,0:T(8,128)(2,1)S(1)}, bf16[4,128,768]{2,1,0:T(8,128)(2,1)}, u32[]{:S(2)}) copy-start(bf16[4,128,768]{2,1,0:T(8,128)(2,1)} %get-tuple-element.88) | copy-start | bytes 2359300
  215.5 3.6 %copy-start = (bf16[4,128,768]{2,1,0:T(8,128)(2,1)S(1)}, bf16[4,128,768]{2,1,0:T(8,128)(2,1)}, u32[]{:S(2)}) copy-start(bf16[4,128,768]{2,1,0:T(8,128)(2,1)} %get-tuple-element.89) | copy-start | bytes 2359300

commit v7 on v6

--- a/solution.py
+++ b/solution.py
@@ -489,7 +489,7 @@
 def feed_turn_kernel(
     h2_ref, h2t_ref, gf_ref, wg0, wg1, wu0, wu1, bg0, bg1, bu0, bu1, wd0, wd1,
     mid_ref, att_ref, dy_ref, mix_ref, mod_ref, weight_ref, dbias_ref, known_ref,
-    out_ref, gmid_ref, gmix_ref, dw_ref, sums_ref, total_ref,
+    out_ref, gmid_ref, gmix_ref, dw_ref, sums_ref, total_ref, passed_ref,
     feed_ref, gh_ref, bias_ref, made, paired, near, pair_send, pair_recv, near_send, near_recv,
 ):
     place = Place()
@@ -564,26 +564,13 @@
         of = step - 1
         copy = pair_copy(of)
         copy.wait_recv()
-        late = (of == 4) | (of == 5)
-
-        @pl.when(jnp.logical_not(late))
-        def _():
-            paired[of] = (made[1 - slot, core].astype(F32) + paired[of].astype(F32)).astype(BF16)
-
-        @pl.when(late)
-        def _():
-            near_copy(of - 4, 1).wait_recv()
-            paired[of] = (
-                made[1 - slot, core].astype(F32)
-                + paired[of].astype(F32)
-                + near[of - 4].astype(F32)
-            ).astype(BF16)
-
-        @pl.when((of == 0) | (of == 2) | (of == 5))
+        paired[of] = (made[1 - slot, core].astype(F32) + paired[of].astype(F32)).astype(BF16)
+
+        @pl.when((of == 0) | (of == 2))
         def _():
             near_copy(of, 2).start()
 
-        @pl.when((of == 1) | (of == 3) | (of == 4))
+        @pl.when((of == 1) | (of == 3))
         def _():
             near_copy(of, 1).start()
 
@@ -621,25 +608,22 @@
         dw_ref[1] = mm(mixed_t, grad_attended[:, half:]).astype(BF16)
         for of in (6, 7):
             pair_copy(of).wait_send()
-        for of in (2, 3, 4, 5):
-            near_copy(of, 1).wait_recv()
-        for of in range(6):
-            near_copy(of, 1).wait_send()
+        for of in range(4):
+            near_copy(of, 1).wait()
         rows = width // 4
-        for f in range(2):
-            for z in range(4):
-                span = slice(z * rows, (z + 1) * rows)
-                total_ref[z, f] = sum(
-                    part.astype(F32)
-                    for part in (paired[6 + f, span], near[2 + f, span], near[4 + f, span])
-                ).astype(BF16)
-            for i in range(2):
-                for b in range(3):
-                    span = slice(g_rows + b * 128 + i * 64, g_rows + b * 128 + i * 64 + 64)
-                    total_ref[2 * f + i, 2, b * 64 : b * 64 + 64] = sum(
-                        part.astype(F32)
-                        for part in (paired[6 + f, span], near[2 + f, span], near[4 + f, span])
-                    ).astype(BF16)
+        for target, mine, there in ((total_ref, 6, 2), (passed_ref, 4, 0)):
+            for f in range(2):
+
+                def added(span, f=f, mine=mine, there=there):
+                    both = paired[mine + f, span].astype(F32) + near[there + f, span].astype(F32)
+                    return both.astype(BF16)
+
+                for z in range(4):
+                    target[z, f] = added(slice(z * rows, (z + 1) * rows))
+                for i in range(2):
+                    for b in range(3):
+                        start = g_rows + b * 128 + i * 64
+                        target[2 * f + i, 2, b * 64 : b * 64 + 64] = added(slice(start, start + 64))
 
 
 def once(shape):
@@ -663,6 +647,7 @@
         low, wide, low,
         jax.ShapeDtypeStruct((2, width, width // 2), BF16),
         jax.ShapeDtypeStruct((2, 8, width), F32),
+        jax.ShapeDtypeStruct((4, 3, width // 4, 256), BF16),
         jax.ShapeDtypeStruct((4, 3, width // 4, 256), BF16),
     ]
     return pl.pallas_call(
@@ -682,11 +667,11 @@
             pltpu.VMEM((32, 128), F32),
             pltpu.VMEM((2, 2) + piece, BF16),
             pltpu.VMEM((8,) + piece, BF16),
-            pltpu.VMEM((6,) + piece, BF16),
+            pltpu.VMEM((4,) + piece, BF16),
             pltpu.SemaphoreType.DMA((2,)),
             pltpu.SemaphoreType.DMA((8,)),
-            pltpu.SemaphoreType.DMA((6,)),
-            pltpu.SemaphoreType.DMA((6,)),
+            pltpu.SemaphoreType.DMA((4,)),
+            pltpu.SemaphoreType.DMA((4,)),
         ],
         compiler_params=pltpu.CompilerParams(
             vmem_limit_bytes=VMEM_LIMIT, collective_id=1, has_side_effects=True
@@ -698,21 +683,15 @@
     )
 
 
-IN_BIAS, Q_GAIN, K_GAIN, OUT_BIAS, DOWN_BIAS, GATE_BIAS = 6, 9, 10, 11, 12, 13
-
-
-def small_row(width, head, modulate, inproj, qgain, kgain, outproj, down, gate_up):
-    heads = width // head
-    return jnp.concatenate(
-        [modulate, inproj, jnp.tile(qgain, heads), jnp.tile(kgain, heads), outproj, down, gate_up]
-    )[None]
+Q_GAIN, K_GAIN, OUT_BIAS, DOWN_BIAS, GATE_BIAS = 0, 1, 2, 3, 4
 
 
 def front_kernel(
-    head, tile_cols, tok_hbm, grad_hbm, act_ref, small_ref, modw_hbm, inw_hbm,
+    head, tile_cols, tok_hbm, grad_hbm, time_ref, label_ref, modb_ref, inb_ref, qgain_ref,
+    kgain_ref, outb_ref, downb_ref, gateb_ref, table_hbm, modw_hbm, inw_hbm,
     x_hbm, dy_hbm, hid_hbm, q_hbm, k0_hbm, v0_hbm, k1_hbm, v1_hbm, raw_hbm, mod_ref, cos_ref,
-    sin_ref,
-    x_ref, own_ref, hid_ref, q_ref, k_ref, v_ref, raw_ref, modw_ref, inw_ref,
+    sin_ref, small_ref, known_ref,
+    x_ref, own_ref, hid_ref, q_ref, k_ref, v_ref, raw_ref, table_ref, modw_ref, inw_ref,
     load_sem, store_sem, tok_send, tok_recv, kv_send, kv_recv,
 ):
     place = Place()
@@ -724,7 +703,7 @@
         for i, (source, target) in enumerate(
             (
                 (tok_hbm.at[chip], x_ref.at[pl.ds(0, cells)]), (modw_hbm, modw_ref),
-                (inw_hbm, inw_ref), (grad_hbm.at[chip], own_ref),
+                (inw_hbm, inw_ref), (grad_hbm.at[chip], own_ref), (table_hbm, table_ref),
             )
         )
     ]
@@ -753,8 +732,10 @@
             place.pair(),
         )
 
-    def vector(start, count=1):
-        return small_ref[:, start * width : (start + count) * width].astype(F32)
+    def line(ref):
+        return ref[...].astype(F32)[None, :]
+
+    in_bias = line(inb_ref)
 
     def project(start, size, chunk):
         span = slice(start, start + size)
@@ -764,7 +745,8 @@
         hidden = hidden.astype(BF16)
         hid_ref[span, :] = hidden
         for part in (1, 2, 0):
-            raw = mm(hidden, inw_ref[:, part * width : (part + 1) * width]) + vector(IN_BIAS + part)
+            raw = mm(hidden, inw_ref[:, part * width : (part + 1) * width])
+            raw = raw + in_bias[:, part * width : (part + 1) * width]
             if part == 2:
                 v_ref[span, :] = raw.astype(BF16)
                 for which in (0, 1):
@@ -772,15 +754,35 @@
                 continue
             raw_ref[span, part * width : (part + 1) * width] = raw.astype(BF16)
             factor = lax.rsqrt(head_sum(raw * raw, head) * (1.0 / head) + NORM_EPSILON)
-            scaled = raw * factor * vector((Q_GAIN, K_GAIN)[part])
+            scaled = raw * factor * small_ref[:, part * width : (part + 1) * width]
             turned = turn(scaled, cos_ref[span, :], sin_ref[span, :], head).astype(BF16)
             (q_ref, k_ref)[part][span, :] = turned
 
-    for load in loads:
-        load.start()
+    for i in (0, 4, 1, 2, 3):
+        loads[i].start()
     meet([place.pair()] + [place.plane(k) for k in (1, 2, 3)])
     for k in (3, 1, 2):
         token_copy(0, k).start()
+
+    for start, row in (
+        (Q_GAIN, jnp.concatenate([line(qgain_ref)] * (width // head), axis=1)),
+        (K_GAIN, jnp.concatenate([line(kgain_ref)] * (width // head), axis=1)),
+        (OUT_BIAS, line(outb_ref)), (DOWN_BIAS, line(downb_ref)), (GATE_BIAS, line(gateb_ref)),
+    ):
+        small_ref[:, start * width : start * width + row.shape[1]] = row
+    half = width // 2
+    index = lax.broadcasted_iota(jnp.int32, (1, half), 1).astype(F32)
+    phase = time_ref[chip].astype(F32) * jnp.exp(-math.log(10000.0) * index / half)
+    features = jnp.concatenate([jnp.cos(phase), jnp.sin(phase)], axis=1)
+    label = label_ref[chip]
+    classes = lax.broadcasted_iota(jnp.int32, (16, table_ref.shape[0]), 1)
+    loads[4].wait()
+    chosen = mm(jnp.where(classes == label, 1.0, 0.0).astype(BF16), table_ref[...])
+    condition = features + chosen[:1]
+    known_ref[0:1, :] = jnp.where(core == 0, condition, 0.0)
+    known_ref[1:2, :] = jnp.where(core == 0, jnp.zeros((1, width), F32) + label.astype(F32), 0.0)
+    act = condition * (1.0 / (1.0 + jnp.exp(-condition)))
+    act = jnp.broadcast_to(act, (16, width)).astype(BF16)
 
     quarter = head // 4
     lane = lax.broadcasted_iota(jnp.int32, (1, 128), 1)
@@ -797,7 +799,7 @@
         cos_ref[k * cells : (k + 1) * cells, :] = jnp.cos(angle)
         sin_ref[k * cells : (k + 1) * cells, :] = sign * jnp.sin(angle)
     loads[1].wait()
-    mod_ref[...] = mm(act_ref[...], modw_ref[...])[:1] + vector(0, 6)
+    mod_ref[...] = mm(act, modw_ref[...])[:1] + line(modb_ref)
     loads[0].wait()
     loads[2].wait()
     project(0, cells, 0)
@@ -820,7 +822,9 @@
         store.wait()
 
 
-def front_call(tokens, grads, act, small, modw, inw, head, tile_cols):
+def front_call(
+    tokens, grads, timesteps, labels, vectors, class_table, modw, inw, head, tile_cols
+):
     images, cells, width = tokens.shape
     rows = images * cells
     low = lambda *shape: jax.ShapeDtypeStruct(shape, BF16)
@@ -830,39 +834,46 @@
     sems = lambda *shape: pltpu.SemaphoreType.DMA(shape)
     return pl.pallas_call(
         functools.partial(front_kernel, head, tile_cols),
-        in_specs=[anywhere] * 2 + [inside] * 2 + [anywhere] * 2,
-        out_specs=[anywhere] * 9 + [inside] * 3,
+        in_specs=[anywhere] * 2
+        + [pl.BlockSpec(memory_space=pltpu.SMEM)] * 2
+        + [inside] * len(vectors)
+        + [anywhere] * 3,
+        out_specs=[anywhere] * 9 + [inside] * 5,
         out_shape=[low(rows, width)] * 8
         + [
             low(rows, 2 * width), jax.ShapeDtypeStruct((1, 6 * width), F32),
             jax.ShapeDtypeStruct((rows, 128), F32), jax.ShapeDtypeStruct((rows, 128), F32),
+            jax.ShapeDtypeStruct((1, GATE_BIAS * width + vectors[-1].shape[0]), F32),
+            jax.ShapeDtypeStruct((2, width), F32),
         ],
         scratch_shapes=[
             vmem(rows, width), vmem(cells, width), vmem(rows, width), vmem(rows, width),
-            vmem(rows, width), vmem(rows, width), vmem(rows, 2 * width), vmem(*modw.shape),
-            vmem(*inw.shape), sems(4), sems(7), sems(2, 3), sems(2, 3), sems(2, 2), sems(2, 2),
+            vmem(rows, width), vmem(rows, width), vmem(rows, 2 * width), vmem(*class_table.shape),
+            vmem(*modw.shape), vmem(*inw.shape), sems(5), sems(7), sems(2, 3), sems(2, 3), sems(2, 2), sems(2, 2),
         ],
         compiler_params=pltpu.CompilerParams(
             vmem_limit_bytes=VMEM_LIMIT, collective_id=3, has_side_effects=True
         ),
         name="front",
-    )(tokens, grads, act, small, modw, inw)
-
-
-Z_FIRST = (False, False, True, False)
+    )(tokens, grads, timesteps, labels, *vectors, class_table, modw, inw)
+
+
+Z_FIRST = (False, False, False, False)
 GROUPS = 4
+TOKEN_STEP = 3
+PASS_STEP = 4
 
 
 def back_kernel(
     head, q_ref, k0_ref, k1_ref, v0_ref, v1_ref, gm_ref, mix_ref, rl_ref, e_ref,
-    mod_ref, qgain_ref, kgain_ref, cos_ref, sin_ref, dout_ref, totals_ref, early_ref,
+    mod_ref, qgain_ref, kgain_ref, cos_ref, sin_ref, dout_ref, totals_ref, passed_ref, early_ref,
     raw_hbm, hid_hbm, x_hbm, gmid_hbm, weight_hbm, rows_hbm,
     output_ref, gtok_ref, feeds_hbm, projs_hbm, early_hbm, late_hbm,
     feeds_ref, projs_ref, early_all, late_all, raw_ref, hid_ref, x_ref, gmid_ref, weight_ref, hidt_ref, gh_ref, gx_ref, late_ref,
     dq_s, dk0_s, dv0_s, dk1_s, dv1_s, dk_in, dv_in,
-    made, paired, first_out, first_in, second_out, second_in, z_in, early_in, late_in,
+    made, paired, first_out, first_in, second_out, second_in, landed, z_in, early_in, late_in,
     load_sem, own_sem, kv_send, kv_recv, pair_send, pair_recv, first_send, first_recv,
-    second_send, second_recv, z_send, z_recv, tok_send, tok_recv, feed_send, feed_recv,
+    second_send, second_recv, pass_send, pass_recv, z_send, z_recv, tok_send, tok_recv, feed_send, feed_recv,
     proj_send, proj_recv, small_send, small_recv,
 ):
     place = Place()
@@ -893,9 +904,16 @@
         )
     ]
 
+    def pass_copy(f, i):
+        part = (slice(None), f) if i == 0 else (pl.ds(2 * f, 2), 2)
+        return send(
+            passed_ref.at[part], landed.at[part], pass_send.at[f, i], pass_recv.at[f, i],
+            place.plane(f + 1),
+        )
+
     def z_copy(d):
         return send(
-            totals_ref.at[place.flipped_z(d)], z_in.at[d - 1], z_send.at[d - 1], z_recv.at[d - 1],
+            landed.at[place.flipped_z(d)], z_in.at[d - 1], z_send.at[d - 1], z_recv.at[d - 1],
             place.depth(d),
         )
 
@@ -1049,13 +1067,11 @@
             + [place.plane(k) for k in (1, 2, 3)]
             + [place.depth(d) for d in (1, 2, 3)]
         )
+        for f in (0, 1):
+            for i in (0, 1):
+                pass_copy(f, i).start()
         pair_copy(3).start()
         small_pair(0).start()
-        for d in (1, 2, 3):
-            z_copy(d).start()
-        for k in (1, 2, 3):
-            token_copy(0, k).start()
-        own_tokens(0).start()
         gh_ref[...] = jnp.zeros_like(gh_ref)
 
     @pl.when(step >= 1)
@@ -1125,17 +1141,20 @@
         start_group(1)
         go_on(3)
 
-    @pl.when(step == 6)
-    def _():
+    @pl.when(step == TOKEN_STEP)
+    def _():
+        for k in (1, 2, 3):
+            token_copy(0, k).start()
+        own_tokens(0).start()
+
+    @pl.when(step == PASS_STEP)
+    def _():
+        for f in (0, 1):
+            for i in (0, 1):
+                pass_copy(f, i).wait_recv()
+        landed[...] = (landed[...].astype(F32) + totals_ref[...].astype(F32)).astype(BF16)
         for d in (1, 2, 3):
-            z_copy(d).wait_recv()
-        for i in range(3):
-            feeds_ref[core, chip, i] = (
-                totals_ref[z, i].astype(F32)
-                + z_in[0, i].astype(F32)
-                + z_in[1, i].astype(F32)
-                + z_in[2, i].astype(F32)
-            ).astype(BF16)
+            z_copy(d).start()
 
     @pl.when((step >= 2) & (lax.rem(step, 2) == 0))
     def _():
@@ -1213,18 +1232,27 @@
         for k in (1, 2, 3):
             token_copy(1, k).start()
         own_tokens(1).start()
+        for d in (1, 2, 3):
+            z_copy(d).wait_recv()
+        for i in range(3):
+            feeds_ref[core, chip, i] = (
+                landed[z, i].astype(F32)
+                + z_in[0, i].astype(F32)
+                + z_in[1, i].astype(F32)
+                + z_in[2, i].astype(F32)
+            ).astype(BF16)
         for k in (1, 2, 3):
             feed_copy(k).start()
-        small_next(1, 0)
         finish(3)
         finish(0)
-        small_next(1, 1)
         finish(1)
-        small_next(1, 2)
         go_on(2)
+        small_next(1, 0)
         finish(2)
         for k in (1, 2, 3):
             proj_copy(k).start()
+        small_next(1, 1)
+        small_next(1, 2)
         for k in (1, 2, 3):
             feed_copy(k).wait_recv()
         for k in (1, 2, 3):
@@ -1246,6 +1274,9 @@
             stores[which].start()
             for p in range(6):
                 kv_copy(which, p).wait_send()
+        for f in (0, 1):
+            for i in (0, 1):
+                pass_copy(f, i).wait_send()
         for k in (1, 2, 3):
             z_copy(k).wait_send()
             for g in range(4):
@@ -1263,14 +1294,14 @@
 
 def back_call(
     q, k0, k1, v0, v1, grad_mixed, mixed, inverse, grown, mod, small_vectors, cosine, sine, d_out,
-    totals, early, raw, hidden, x, grad_middle, weight, output_rows, head,
+    totals, passed, early, raw, hidden, x, grad_middle, weight, output_rows, head,
 ):
     rows, width = q.shape
     half, part = width // 2, width // 16
     low = lambda *shape: jax.ShapeDtypeStruct(shape, BF16)
     pair = pl.BlockSpec((rows, 128), lambda s: (0, jnp.minimum(s, 5)))
     anywhere = pl.BlockSpec(memory_space=pl.ANY)
-    small = [mod, small_vectors, small_vectors, cosine, sine, d_out, totals, early]
+    small = [mod, small_vectors, small_vectors, cosine, sine, d_out, totals, passed, early]
     gain = lambda at: pl.BlockSpec((1, width), lambda s: (0, at), pipeline_mode=pl.Buffered(1))
     out_shape = [
         low(4, rows // 4, width), low(4, rows // 4, width),
@@ -1300,11 +1331,12 @@
             vmem(2, 2, width, half), vmem(GROUPS, width, half),
             vmem(GROUPS, 4, 4, part, half), vmem(GROUPS, 3, 4, part, half),
             vmem(GROUPS, 4, part, half), vmem(GROUPS, 3, part, half),
-            vmem(3, 3, width // 4, 256),
+            vmem(*totals.shape), vmem(3, 3, width // 4, 256),
             pltpu.VMEM((8, width), F32), pltpu.VMEM((4, width), F32),
             sems(9), sems(2), sems(2, 6), sems(2, 6), sems(GROUPS), sems(GROUPS),
             sems(GROUPS, 3), sems(GROUPS, 3), sems(GROUPS, 3), sems(GROUPS, 3),
-            sems(3), sems(3), sems(2, 3), sems(2, 3), sems(4), sems(4), sems(4), sems(4),
+            sems(2, 2), sems(2, 2), sems(3), sems(3), sems(2, 3), sems(2, 3), sems(4), sems(4),
+            sems(4), sems(4),
             sems(2, 7), sems(2, 7),
         ],
         compiler_params=pltpu.CompilerParams(
@@ -1411,10 +1443,10 @@
         def _(z=z):
             for ref, row in pieces:
                 size = row.shape[1] // 4
-                ref[...] = row[:, z * size : (z + 1) * size]
+                ref[...] = row[0, z * size : (z + 1) * size]
 
     load.wait()
-    grad = sum(mm_nt(low, modw_ref[:, j * width : (j + 1) * width]) for j, low in enumerate(lows))
+    grad = sum(mm_nt(modw_ref[:, j * width : (j + 1) * width], low) for j, low in enumerate(lows)).T
     grad = grad * sig * (1.0 + conditions * (1.0 - sig))
     for k in range(4):
         cond_ref[pl.ds(place.flipped(k), 1), :] = grad[k : k + 1]
@@ -1441,10 +1473,10 @@
     whole = lambda *shape: jax.ShapeDtypeStruct(shape, F32)
     anywhere = pl.BlockSpec(memory_space=pl.ANY)
     out_shape = [
-        whole(4, width), whole(classes, width), whole(rows, 6 * width), whole(1, 6 * width // 4),
-        whole(rows, 3 * width), whole(1, 3 * width // 4), whole(1, head // 4), whole(1, head // 4),
-        whole(rows, width), whole(1, rows), whole(rows, 2 * hidden_width),
-        whole(1, 2 * hidden_width // 4), whole(hidden_width // 4, width), whole(1, rows),
+        whole(4, width), whole(classes, width), whole(rows, 6 * width), whole(6 * width // 4),
+        whole(rows, 3 * width), whole(3 * width // 4), whole(head // 4), whole(head // 4),
+        whole(rows, width), whole(rows), whole(rows, 2 * hidden_width),
+        whole(2 * hidden_width // 4), whole(hidden_width // 4, width), whole(rows),
     ]
     big = (1, 2, 4, 8, 10, 12)
     return pl.pallas_call(
@@ -1532,6 +1564,45 @@
     tiles = tokens.reshape(image_count, cells, width)
     grads = cotangent.reshape(image_count, cells, width)
 
+    if nb == 4 and hidden_width == 16 * 128:
+        vectors = (
+            modulate_bias, inproj_bias, query_gain, key_gain, outproj_bias, down_bias, gate_up_bias
+        )
+        x, dy, hidden_one, q, k0, v0, k1, v1, raw, mod, cosine, sine, small, known = front_call(
+            tiles, grads, timesteps, labels, vectors, class_table, modulate_weight, inproj_weight,
+            head, tile_cols,
+        )
+        mixed, grown, inverse = attend_call(q, k0, k1, v0, v1, head)
+        attended, middle, hidden_two, hidden_two_t, grad_feed = middle_call(
+            mixed, x, dy, mod, outproj_weight, small, OUT_BIAS
+        )
+        output_rows, grad_middle, grad_mixed, d_out, sums_two, totals, passed = feed_turn_call(
+            hidden_two, hidden_two_t, grad_feed, gate_up_weight, down_weight, middle, attended, dy,
+            mixed, mod, outproj_weight, small, known,
+        )
+        output, grad_tokens, feeds, projs, early, late = back_call(
+            q, k0, k1, v0, v1, grad_mixed, mixed, inverse, grown, mod, small, cosine, sine, d_out,
+            totals, passed, sums_two, raw, hidden_one, x, grad_middle, inproj_weight, output_rows, head,
+        )
+        (
+            grad_condition, grad_table, grad_mod_w, grad_mod_b, grad_in_w, grad_in_b, grad_q_gain,
+            grad_k_gain, grad_out_w, grad_out_b, grad_gu_w, grad_gu_b, grad_down_w, grad_down_b,
+        ) = finish_call(
+            feeds, projs, early, late, modulate_weight, head, class_count, hidden_width
+        )
+        return (
+            output.reshape(tokens.shape), grad_tokens.reshape(tokens.shape), grad_condition,
+            grad_table, grad_mod_w, grad_mod_b, grad_in_w, grad_in_b, grad_q_gain, grad_k_gain,
+            grad_out_w, grad_out_b, grad_gu_w, grad_gu_b, grad_down_w, grad_down_b,
+        )
+
+    def exchange(blocks):
+        return [take(blocks, place)] + [
+            moves.plane(take(blocks, place ^ k), k) for k in range(1, 4)
+        ]
+
+    x = jnp.concatenate(exchange(tiles), axis=0)
+
     half_width = width // 2
     step = take(timesteps, place).astype(F32)
     label = take(labels, place)
@@ -1539,49 +1610,6 @@
     features = jnp.concatenate([jnp.cos(step * rates), jnp.sin(step * rates)])
     condition = features + take(class_table, label).astype(F32)
     cond_act = jax.nn.silu(condition).astype(BF16)
-    if nb == 4 and hidden_width == 16 * 128:
-        act = jnp.broadcast_to(cond_act[None], (16, width))
-        small = small_row(
-            width, head, modulate_bias, inproj_bias, query_gain, key_gain, outproj_bias, down_bias,
-            gate_up_bias,
-        )
-        known = jnp.stack([condition, jnp.broadcast_to(label.astype(F32), (width,))])
-        known = jnp.where(core == 0, known, 0.0)
-        x, dy, hidden_one, q, k0, v0, k1, v1, raw, mod, cosine, sine = front_call(
-            tiles, grads, act, small, modulate_weight, inproj_weight, head, tile_cols
-        )
-        mixed, grown, inverse = attend_call(q, k0, k1, v0, v1, head)
-        attended, middle, hidden_two, hidden_two_t, grad_feed = middle_call(
-            mixed, x, dy, mod, outproj_weight, small, OUT_BIAS
-        )
-        output_rows, grad_middle, grad_mixed, d_out, sums_two, totals = feed_turn_call(
-            hidden_two, hidden_two_t, grad_feed, gate_up_weight, down_weight, middle, attended, dy,
-            mixed, mod, outproj_weight, small, known,
-        )
-        output, grad_tokens, feeds, projs, early, late = back_call(
-            q, k0, k1, v0, v1, grad_mixed, mixed, inverse, grown, mod, small, cosine, sine, d_out,
-            totals, sums_two, raw, hidden_one, x, grad_middle, inproj_weight, output_rows, head,
-        )
-        (
-            grad_condition, grad_table, grad_mod_w, grad_mod_b, grad_in_w, grad_in_b, grad_q_gain,
-            grad_k_gain, grad_out_w, grad_out_b, grad_gu_w, grad_gu_b, grad_down_w, grad_down_b,
-        ) = finish_call(
-            feeds, projs, early, late, modulate_weight, head, class_count, hidden_width
-        )
-        return (
-            output.reshape(tokens.shape), grad_tokens.reshape(tokens.shape), grad_condition,
-            grad_table, grad_mod_w, grad_mod_b[0], grad_in_w, grad_in_b[0], grad_q_gain[0],
-            grad_k_gain[0], grad_out_w, grad_out_b[0], grad_gu_w, grad_gu_b[0], grad_down_w,
-            grad_down_b[0],
-        )
-
-    def exchange(blocks):
-        return [take(blocks, place)] + [
-            moves.plane(take(blocks, place ^ k), k) for k in range(1, 4)
-        ]
-
-    x = jnp.concatenate(exchange(tiles), axis=0)
-
     mod = modulation_call(
         jnp.broadcast_to(cond_act[None], (16, width)), modulate_weight, modulate_bias[None]
     )[:1]

time: 221 us -> 199 us (0.900)
  local copies, waits for them, and re-layouts: 11.8 us -> 2.28 us
  Pallas kernels: 200 us -> 193 us
  other arithmetic: 4.08 us -> 0 us
  between operations: 3.99 us -> 0.71 us
    pallas_call x1, Pallas kernels: 57.1 us -> 44.6 us  [feed_turn_call(): pl.pallas_call(feed_turn_kernel, grid=(9,), in_specs=[once((rows, width))...]
    pallas_call x1, Pallas kernels: 85.7 us -> 90.9 us  [back_call(): pl.pallas_call(functools.partial(back_kernel, head), grid=(7,), in_specs=...]
    unnamed x12 -> x6, local copies, waits for them, and re-layouts: 5.73 us -> 2.28 us
    pallas_call x2 -> x0, other arithmetic: 2.66 us -> none  [finish_call(): pl.pallas_call(functools.partial(finish_kernel, head), in_specs=[pl.Block...]
    dynamic_slice x2 -> x0, local copies, waits for them, and re-layouts: 2.49 us -> none  [take(): return lax.dynamic_index_in_dim(array_in, index, axis, keepdims=False)]
where the time goes in v7:
time: 199 us; the launch traced here: 196 us
  Pallas kernels  193 us (97%)
  local copies, waits for them, and re-layouts  2.28 us (1%)
    pallas_call x1, Pallas kernels, back_call(): pl.pallas_call(functools.partial(back_kernel, head), grid=(7,), in_specs=...  90.9 us
    pallas_call x1, Pallas kernels, feed_turn_call(): pl.pallas_call(feed_turn_kernel, grid=(9,), in_specs=[once((rows, width))...  44.6 us
    pallas_call x1, Pallas kernels, front_call(): pl.pallas_call(functools.partial(front_kernel, head, tile_cols), in_specs...  25.7 us
    pallas_call x1, Pallas kernels, finish_call(): pl.pallas_call(functools.partial(finish_kernel, head), in_specs=[pl.Block...  15.3 us
    pallas_call x1, Pallas kernels, attend_call(): pl.pallas_call(functools.partial(attend_kernel, head ** (-0.5)), grid=(wi...  12.1 us
    pallas_call x1, Pallas kernels, middle_call(): pl.pallas_call(middle_kernel, grid=(2,), in_specs=[by_row] * 3 + [full(mo...  4.41 us

profile of v7, /device:TPU:0, one launch (start us, length us, event | category | flops | bytes accessed | tf_op | source)
XLA Modules:
  0.0 196.1 jit_solution(8783612465533642118)
XLA Ops:
  0.7 25.7 %front.1 = (bf16[512,768]{1,0:T(8,128)(2,1)}, bf16[512,768]{1,0:T(8,128)(2,1)}, bf16[512,768]{1,0:T(8,128)(2,1)}, bf16[512,768]{1,0:T(8,128)(2,1)}, bf16[512,768...) custom-call(bf16[4,128,768]{2,1,0:T(8,128)(2,1)} %bitcast.6, ...), custom_call_target="tpu_custom_call" | custom-call | tf_op jit(solution)/shard_map/front/pallas_call | solution.py:835
  26.4 12.1 %attend.1 = (bf16[512,768]{1,0:T(8,128)(2,1)}, bf16[12,512,1024]{2,1,0:T(8,128)(2,1)}, f32[512,768]{1,0:T(8,128)}) custom-call(bf16[512,768]{1,0:T(8,128)(2,1)} %get-tuple-element.65.q_ref, bf16[512,768]{1,0:T(8,128)(2,1)} %get-tuple-element.66.k0_ref, bf16[512,768]{1,0:T(8,128)(2,1)} %get-tuple-element.67.k1_ref, ...), custom_call_target="tpu_custom_call" | custom-call | tf_op jit(solution)/shard_map/attend/pallas_call | solution.py:155
  38.5 4.4 %middle.1 = (bf16[512,768]{1,0:T(8,128)(2,1)}, f32[512,768]{1,0:T(8,128)}, bf16[512,768]{1,0:T(8,128)(2,1)}, bf16[768,512]{1,0:T(8,128)(2,1)}, bf16[512,768]{1,0:T(8,128)(2,1)}) custom-call(bf16[512,768]{1,0:T(8,128)(2,1)} %get-tuple-element.70.mix_ref, bf16[512,768]{1,0:T(8,128)(2,1)} %get-tuple-element.71.x_ref.x_hbm, ...), custom_call_target="tpu_custom_call" | custom-call | tf_op jit(solution)/shard_map/middle/pallas_call | solution.py:239
  42.9 44.6 %feed_turn.1 = (bf16[512,768]{1,0:T(8,128)(2,1)}, f32[512,768]{1,0:T(8,128)}, bf16[512,768]{1,0:T(8,128)(2,1)}, bf16[2,768,384]{2,1,0:T(8,128)(2,1)}, f32[2,8,76...) custom-call(bf16[512,768]{1,0:T(8,128)(2,1)} %get-tuple-element.75.h2_ref, ...), custom_call_target="tpu_custom_call" | custom-call | tf_op jit(solution)/shard_map/feed_turn/pallas_call | solution.py:653
  87.6 90.9 %back.1 = (bf16[4,128,768]{2,1,0:T(8,128)(2,1)}, bf16[4,128,768]{2,1,0:T(8,128)(2,1)}, bf16[2,4,3,192,256]{4,3,2,1,0:T(8,128)(2,1)}, bf16[2,4,4,48,384]{4,3,2,1,...) custom-call(bf16[512,768]{1,0:T(8,128)(2,1)} %get-tuple-element.65.q_ref, ...), custom_call_target="tpu_custom_call" | custom-call | tf_op jit(solution)/shard_map/back/pallas_call | solution.py:1313
  178.4 0.0 copy-start.1
  178.4 15.3 %finish.1 = (f32[4,768]{1,0:T(4,128)}, f32[1001,768]{1,0:T(8,128)}, f32[192,4608]{1,0:T(8,128)}, f32[1152]{0:T(1024)}, f32[192,2304]{1,0:T(8,128)}, /*index=5*/f...) custom-call(bf16[2,4,3,192,256]{4,3,2,1,0:T(8,128)(2,1)} %get-tuple-, ...), custom_call_target="tpu_custom_call" | custom-call | tf_op jit(solution)/shard_map/finish/pallas_call | solution.py:1482
  193.8 0.0 copy-start
  193.8 0.0 copy-done.1
  193.8 0.9 copy.35
  194.7 0.5 copy-done
  195.2 0.9 copy.36
Async XLA Ops:
  178.4 15.4 %copy-start.1 = (bf16[4,128,768]{2,1,0:T(8,128)(2,1)S(1)}, bf16[4,128,768]{2,1,0:T(8,128)(2,1)}, u32[]{:S(2)}) copy-start(bf16[4,128,768]{2,1,0:T(8,128)(2,1)} %get-tuple-element.94) | copy-start | bytes 2359300
  193.8 1.4 copy-start

commit v8 on v7

--- a/solution.py
+++ b/solution.py
@@ -520,6 +520,19 @@
     def _():
         pair_copy(step - 1).start()
 
+    def join_pair(of):
+        copy = pair_copy(of)
+        copy.wait_recv()
+        paired[of] = (made[1 - slot, core].astype(F32) + paired[of].astype(F32)).astype(BF16)
+
+        @pl.when((of == 0) | (of == 2))
+        def _():
+            near_copy(of, 2).start()
+
+        @pl.when((of == 1) | (of == 3))
+        def _():
+            near_copy(of, 1).start()
+
     @pl.when(step < 8)
     def _():
         owner, half = feed_order(step)
@@ -544,6 +557,10 @@
                 row = 16 * e + (2 * half + i) * 4 + place.flipped(owner)
                 bias_ref[pl.ds(row, 1), :] = total[:, i * unit : (i + 1) * unit]
 
+        @pl.when(step >= 1)
+        def _():
+            join_pair(step - 1)
+
         @pl.when(step >= 2)
         def _():
             pair_copy(step - 2).wait_send()
@@ -559,23 +576,9 @@
                         i * 128 + c * 64 : i * 128 + c * 64 + 64
                     ]
 
-    @pl.when(step >= 1)
-    def _():
-        of = step - 1
-        copy = pair_copy(of)
-        copy.wait_recv()
-        paired[of] = (made[1 - slot, core].astype(F32) + paired[of].astype(F32)).astype(BF16)
-
-        @pl.when((of == 0) | (of == 2))
-        def _():
-            near_copy(of, 2).start()
-
-        @pl.when((of == 1) | (of == 3))
-        def _():
-            near_copy(of, 1).start()
-
     @pl.when(step == 8)
     def _():
+        join_pair(7)
         half = width // 2
         dy = dy_ref[...].astype(F32)
         feed = feed_ref[...] + dbias_ref[...].astype(F32)
@@ -683,15 +686,78 @@
     )
 
 
+def attend_tiles_kernel(
+    scale, q_ref, k0_ref, k1_ref, v0_ref, v1_ref, grad_hbm, mix_ref, e_ref, rl_ref, dy_hbm,
+    own_ref, own_sem, tok_send, tok_recv,
+):
+    place = Place()
+    cells = own_ref.shape[0]
+    step = pl.program_id(0)
+    load = pltpu.make_async_copy(grad_hbm.at[place.chip], own_ref, own_sem.at[0])
+    store = pltpu.make_async_copy(own_ref, dy_hbm.at[pl.ds(0, cells)], own_sem.at[1])
+
+    def token_copy(k):
+        return send(
+            grad_hbm.at[place.flipped(k)], dy_hbm.at[pl.ds(k * cells, cells)], tok_send.at[k - 1],
+            tok_recv.at[k - 1], place.plane(k),
+        )
+
+    @pl.when(step == 0)
+    def _():
+        load.start()
+        meet([place.plane(k) for k in (1, 2, 3)])
+        for k in (3, 1, 2):
+            token_copy(k).start()
+
+    attend_kernel(scale, q_ref, k0_ref, k1_ref, v0_ref, v1_ref, mix_ref, e_ref, rl_ref)
+
+    @pl.when(step == 1)
+    def _():
+        load.wait()
+        store.start()
+
+    @pl.when(step == pl.num_programs(0) - 1)
+    def _():
+        store.wait()
+        for k in (1, 2, 3):
+            token_copy(k).wait()
+
+
+def attend_tiles_call(q, k0, k1, v0, v1, grads, head):
+    rows, width = q.shape
+    pair = pl.BlockSpec((rows, 128), lambda p: (0, p))
+    anywhere = pl.BlockSpec(memory_space=pl.ANY)
+    return pl.pallas_call(
+        functools.partial(attend_tiles_kernel, head**-0.5),
+        grid=(width // 128,),
+        in_specs=[pair] * 5 + [anywhere],
+        out_specs=[pair, pl.BlockSpec((2, rows, 2 * rows), lambda p: (p, 0, 0)), pair, anywhere],
+        out_shape=[
+            jax.ShapeDtypeStruct((rows, width), BF16),
+            jax.ShapeDtypeStruct((width // head, rows, 2 * rows), BF16),
+            jax.ShapeDtypeStruct((rows, width), F32),
+            jax.ShapeDtypeStruct((rows, width), BF16),
+        ],
+        scratch_shapes=[
+            pltpu.VMEM((rows // 4, width), BF16), pltpu.SemaphoreType.DMA((2,)),
+            pltpu.SemaphoreType.DMA((3,)), pltpu.SemaphoreType.DMA((3,)),
+        ],
+        compiler_params=pltpu.CompilerParams(
+            vmem_limit_bytes=VMEM_LIMIT, collective_id=4, has_side_effects=True
+        ),
+        name="attend_tiles",
+    )(q, k0, k1, v0, v1, grads)
+
+
 Q_GAIN, K_GAIN, OUT_BIAS, DOWN_BIAS, GATE_BIAS = 0, 1, 2, 3, 4
 
 
 def front_kernel(
-    head, tile_cols, tok_hbm, grad_hbm, time_ref, label_ref, modb_ref, inb_ref, qgain_ref,
+    head, tile_cols, tok_hbm, time_ref, label_ref, modb_ref, inb_ref, qgain_ref,
     kgain_ref, outb_ref, downb_ref, gateb_ref, table_hbm, modw_hbm, inw_hbm,
-    x_hbm, dy_hbm, hid_hbm, q_hbm, k0_hbm, v0_hbm, k1_hbm, v1_hbm, raw_hbm, mod_ref, cos_ref,
+    x_hbm, hid_hbm, q_hbm, k0_hbm, v0_hbm, k1_hbm, v1_hbm, raw_hbm, mod_ref, cos_ref,
     sin_ref, small_ref, known_ref,
-    x_ref, own_ref, hid_ref, q_ref, k_ref, v_ref, raw_ref, table_ref, modw_ref, inw_ref,
+    x_ref, hid_ref, q_ref, k_ref, v_ref, raw_ref, table_ref, modw_ref, inw_ref,
     load_sem, store_sem, tok_send, tok_recv, kv_send, kv_recv,
 ):
     place = Place()
@@ -703,7 +769,7 @@
         for i, (source, target) in enumerate(
             (
                 (tok_hbm.at[chip], x_ref.at[pl.ds(0, cells)]), (modw_hbm, modw_ref),
-                (inw_hbm, inw_ref), (grad_hbm.at[chip], own_ref), (table_hbm, table_ref),
+                (inw_hbm, inw_ref), (table_hbm, table_ref),
             )
         )
     ]
@@ -711,17 +777,16 @@
         pltpu.make_async_copy(source, target, store_sem.at[i])
         for i, (source, target) in enumerate(
             (
-                (own_ref, dy_hbm.at[pl.ds(0, cells)]), (x_ref, x_hbm), (hid_ref, hid_hbm),
-                (k_ref, k0_hbm), (v_ref, v0_hbm), (q_ref, q_hbm), (raw_ref, raw_hbm),
+                (x_ref, x_hbm), (hid_ref, hid_hbm), (k_ref, k0_hbm),
+                (v_ref, v0_hbm), (q_ref, q_hbm), (raw_ref, raw_hbm),
             )
         )
     ]
 
-    def token_copy(which, k):
-        source, target = ((tok_hbm, x_ref), (grad_hbm, dy_hbm))[which]
+    def token_copy(k):
         return send(
-            source.at[place.flipped(k)], target.at[pl.ds(k * cells, cells)],
-            tok_send.at[which, k - 1], tok_recv.at[which, k - 1], place.plane(k),
+            tok_hbm.at[place.flipped(k)], x_ref.at[pl.ds(k * cells, cells)], tok_send.at[k - 1],
+            tok_recv.at[k - 1], place.plane(k),
         )
 
     def kv_copy(which, chunk):
@@ -758,11 +823,11 @@
             turned = turn(scaled, cos_ref[span, :], sin_ref[span, :], head).astype(BF16)
             (q_ref, k_ref)[part][span, :] = turned
 
-    for i in (0, 4, 1, 2, 3):
+    for i in (0, 3, 1, 2):
         loads[i].start()
     meet([place.pair()] + [place.plane(k) for k in (1, 2, 3)])
     for k in (3, 1, 2):
-        token_copy(0, k).start()
+        token_copy(k).start()
 
     for start, row in (
         (Q_GAIN, jnp.concatenate([line(qgain_ref)] * (width // head), axis=1)),
@@ -776,7 +841,7 @@
     features = jnp.concatenate([jnp.cos(phase), jnp.sin(phase)], axis=1)
     label = label_ref[chip]
     classes = lax.broadcasted_iota(jnp.int32, (16, table_ref.shape[0]), 1)
-    loads[4].wait()
+    loads[3].wait()
     chosen = mm(jnp.where(classes == label, 1.0, 0.0).astype(BF16), table_ref[...])
     condition = features + chosen[:1]
     known_ref[0:1, :] = jnp.where(core == 0, condition, 0.0)
@@ -803,27 +868,21 @@
     loads[0].wait()
     loads[2].wait()
     project(0, cells, 0)
-    loads[3].wait()
+    for k in (1, 2, 3):
+        token_copy(k).wait()
     stores[0].start()
-    for k in (1, 2, 3):
-        token_copy(0, k).wait()
-    for k in (3, 1, 2):
-        token_copy(1, k).start()
-    stores[1].start()
     project(cells, rows - cells, 1)
-    for store in stores[2:]:
+    for store in stores[1:]:
         store.start()
     for which in (0, 1):
         for chunk in (0, 1):
             kv_copy(which, chunk).wait()
-    for k in (1, 2, 3):
-        token_copy(1, k).wait()
     for store in stores:
         store.wait()
 
 
 def front_call(
-    tokens, grads, timesteps, labels, vectors, class_table, modw, inw, head, tile_cols
+    tokens, timesteps, labels, vectors, class_table, modw, inw, head, tile_cols
 ):
     images, cells, width = tokens.shape
     rows = images * cells
@@ -834,12 +893,12 @@
     sems = lambda *shape: pltpu.SemaphoreType.DMA(shape)
     return pl.pallas_call(
         functools.partial(front_kernel, head, tile_cols),
-        in_specs=[anywhere] * 2
+        in_specs=[anywhere]
         + [pl.BlockSpec(memory_space=pltpu.SMEM)] * 2
         + [inside] * len(vectors)
         + [anywhere] * 3,
-        out_specs=[anywhere] * 9 + [inside] * 5,
-        out_shape=[low(rows, width)] * 8
+        out_specs=[anywhere] * 8 + [inside] * 5,
+        out_shape=[low(rows, width)] * 7
         + [
             low(rows, 2 * width), jax.ShapeDtypeStruct((1, 6 * width), F32),
             jax.ShapeDtypeStruct((rows, 128), F32), jax.ShapeDtypeStruct((rows, 128), F32),
@@ -847,20 +906,20 @@
             jax.ShapeDtypeStruct((2, width), F32),
         ],
         scratch_shapes=[
-            vmem(rows, width), vmem(cells, width), vmem(rows, width), vmem(rows, width),
-            vmem(rows, width), vmem(rows, width), vmem(rows, 2 * width), vmem(*class_table.shape),
-            vmem(*modw.shape), vmem(*inw.shape), sems(5), sems(7), sems(2, 3), sems(2, 3), sems(2, 2), sems(2, 2),
+            vmem(rows, width), vmem(rows, width), vmem(rows, width), vmem(rows, width),
+            vmem(rows, width), vmem(rows, 2 * width), vmem(*class_table.shape),
+            vmem(*modw.shape), vmem(*inw.shape), sems(4), sems(6), sems(3), sems(3), sems(2, 2), sems(2, 2),
         ],
         compiler_params=pltpu.CompilerParams(
             vmem_limit_bytes=VMEM_LIMIT, collective_id=3, has_side_effects=True
         ),
         name="front",
-    )(tokens, grads, timesteps, labels, *vectors, class_table, modw, inw)
-
-
-Z_FIRST = (False, False, False, False)
+    )(tokens, timesteps, labels, *vectors, class_table, modw, inw)
+
+
+Z_FIRST = (False, False, False, True)
 GROUPS = 4
-TOKEN_STEP = 3
+TOKEN_STEP = 5
 PASS_STEP = 4
 
 
@@ -954,22 +1013,28 @@
             second_recv.at[g, k - 1], device,
         )
 
-    def feed_copy(k):
-        here = feeds_ref.at[core, chip]
-        return send(here, here, feed_send.at[k - 1], feed_recv.at[k - 1], place.plane(k))
-
-    def feed_pair():
-        here = feeds_ref.at[core]
-        return send(here, here, feed_send.at[3], feed_recv.at[3], place.pair())
-
-    def proj_copy(k):
-        here = projs_ref.at[core, chip]
-        return send(here, here, proj_send.at[k - 1], proj_recv.at[k - 1], place.plane(k))
-
-    def proj_pair():
-        here = projs_ref.at[core]
-        return send(here, here, proj_send.at[3], proj_recv.at[3], place.pair())
-
+    def gather_copy(which, k):
+        full_ref, sends, recvs = gathers[which]
+        here = full_ref.at[core, chip]
+        return send(here, here, sends.at[k - 1], recvs.at[k - 1], place.plane(k))
+
+    def pass_on(which, k):
+        full_ref, sends, recvs = gathers[which]
+        here = full_ref.at[core, place.flipped(k)]
+        if which == 0:
+            half = here.shape[1] // 2
+            here = here.at[:, pl.ds((k - 1) * half, half)]
+        else:
+            half = here.shape[0] // 2
+            here = here.at[pl.ds((k - 1) * half, half)]
+        return send(here, here, sends.at[1 + k], recvs.at[1 + k], place.plane(3 - k))
+
+    def gather_pair(which):
+        full_ref, sends, recvs = gathers[which]
+        here = full_ref.at[core]
+        return send(here, here, sends.at[4], recvs.at[4], place.pair())
+
+    gathers = ((feeds_ref, feed_send, feed_recv), (projs_ref, proj_send, proj_recv))
     smalls = ((early_ref, early_in, early_all, 8), (late_ref, late_in, late_all, 4))
 
     def small_pair(which):
@@ -1220,10 +1285,10 @@
         late_ref[0, 1:2, :] = col_sum(grad_hidden * normed)
         late_ref[1, 3:4, :] = jnp.zeros((1, width), F32)
         small_pair(1).start()
+        small_begin(1)
+        start_group(2)
         go_on(0)
         go_on(1)
-        small_begin(1)
-        start_group(2)
         grad_normed = grad_hidden * (1.0 + mod_ref[:, width : 2 * width])
         back = factor * (
             grad_normed - normed * jnp.mean(grad_normed * normed, axis=-1, keepdims=True)
@@ -1241,26 +1306,29 @@
                 + z_in[1, i].astype(F32)
                 + z_in[2, i].astype(F32)
             ).astype(BF16)
-        for k in (1, 2, 3):
-            feed_copy(k).start()
+        for k in (1, 2):
+            gather_copy(0, k).start()
         finish(3)
         finish(0)
         finish(1)
         go_on(2)
         small_next(1, 0)
         finish(2)
-        for k in (1, 2, 3):
-            proj_copy(k).start()
+        for k in (1, 2):
+            gather_copy(1, k).start()
         small_next(1, 1)
+        for k in (1, 2):
+            gather_copy(0, k).wait_recv()
+            pass_on(0, k).start()
         small_next(1, 2)
-        for k in (1, 2, 3):
-            feed_copy(k).wait_recv()
-        for k in (1, 2, 3):
-            feed_copy(k).wait_send()
-        feed_pair().start()
-        for k in (1, 2, 3):
-            proj_copy(k).wait()
-        proj_pair().start()
+        for k in (1, 2):
+            gather_copy(1, k).wait_recv()
+            pass_on(1, k).start()
+        for which in (0, 1):
+            for k in (1, 2):
+                gather_copy(which, k).wait_send()
+                pass_on(which, k).wait()
+            gather_pair(which).start()
         for which in (0, 1):
             own_tokens(which).wait()
             for k in (1, 2, 3):
@@ -1284,10 +1352,9 @@
                 second_copy(g, k).wait_send()
         for g in (1, 2, 3):
             pair_copy(g).wait_send()
-        feed_pair().wait()
-        stores[2].start()
-        proj_pair().wait()
-        stores[3].start()
+        for which in (0, 1):
+            gather_pair(which).wait()
+            stores[2 + which].start()
         for store in stores:
             store.wait()
 
@@ -1335,8 +1402,8 @@
             pltpu.VMEM((8, width), F32), pltpu.VMEM((4, width), F32),
             sems(9), sems(2), sems(2, 6), sems(2, 6), sems(GROUPS), sems(GROUPS),
             sems(GROUPS, 3), sems(GROUPS, 3), sems(GROUPS, 3), sems(GROUPS, 3),
-            sems(2, 2), sems(2, 2), sems(3), sems(3), sems(2, 3), sems(2, 3), sems(4), sems(4),
-            sems(4), sems(4),
+            sems(2, 2), sems(2, 2), sems(3), sems(3), sems(2, 3), sems(2, 3), sems(5), sems(5),
+            sems(5), sems(5),
             sems(2, 7), sems(2, 7),
         ],
         compiler_params=pltpu.CompilerParams(
@@ -1568,11 +1635,11 @@
         vectors = (
             modulate_bias, inproj_bias, query_gain, key_gain, outproj_bias, down_bias, gate_up_bias
         )
-        x, dy, hidden_one, q, k0, v0, k1, v1, raw, mod, cosine, sine, small, known = front_call(
-            tiles, grads, timesteps, labels, vectors, class_table, modulate_weight, inproj_weight,
-            head, tile_cols,
-        )
-        mixed, grown, inverse = attend_call(q, k0, k1, v0, v1, head)
+        x, hidden_one, q, k0, v0, k1, v1, raw, mod, cosine, sine, small, known = front_call(
+            tiles, timesteps, labels, vectors, class_table, modulate_weight, inproj_weight, head,
+            tile_cols,
+        )
+        mixed, grown, inverse, dy = attend_tiles_call(q, k0, k1, v0, v1, grads, head)
         attended, middle, hidden_two, hidden_two_t, grad_feed = middle_call(
             mixed, x, dy, mod, outproj_weight, small, OUT_BIAS
         )

time: 199 us -> 190 us (0.955); the launches traced: 196 us -> 190 us
  Pallas kernels: 193 us -> 187 us
    pallas_call x1, Pallas kernels: 25.7 us -> 20.5 us  [front_call(): pl.pallas_call(functools.partial(front_kernel, head, tile_cols), in_specs...]
    pallas_call x1, Pallas kernels: 12.1 us -> 15.2 us  [attend_tiles_call(): pl.pallas_call(functools.partial(attend_tiles_kernel, head ** (-0.5)), gr...]
    pallas_call x1, Pallas kernels: 90.9 us -> 87.9 us  [back_call(): pl.pallas_call(functools.partial(back_kernel, head), grid=(7,), in_specs=...]
where the time goes in v8:
time: 190 us
  Pallas kernels  187 us (98%)
  local copies, waits for them, and re-layouts  2.28 us (1%)
    pallas_call x1, Pallas kernels, back_call(): pl.pallas_call(functools.partial(back_kernel, head), grid=(7,), in_specs=...  87.9 us
    pallas_call x1, Pallas kernels, feed_turn_call(): pl.pallas_call(feed_turn_kernel, grid=(9,), in_specs=[once((rows, width))...  43.8 us
    pallas_call x1, Pallas kernels, front_call(): pl.pallas_call(functools.partial(front_kernel, head, tile_cols), in_specs...  20.5 us
    pallas_call x1, Pallas kernels, finish_call(): pl.pallas_call(functools.partial(finish_kernel, head), in_specs=[pl.Block...  15.3 us
    pallas_call x1, Pallas kernels, attend_tiles_call(): pl.pallas_call(functools.partial(attend_tiles_kernel, head ** (-0.5)), gr...  15.2 us
    pallas_call x1, Pallas kernels, middle_call(): pl.pallas_call(middle_kernel, grid=(2,), in_specs=[by_row] * 3 + [full(mo...  4.42 us

profile of v8, /device:TPU:0, one launch (start us, length us, event | category | flops | bytes accessed | tf_op | source)
XLA Modules:
  0.0 190.1 jit_solution(4870926423611753759)
XLA Ops:
  0.7 20.5 %front.1 = (bf16[512,768]{1,0:T(8,128)(2,1)}, bf16[512,768]{1,0:T(8,128)(2,1)}, bf16[512,768]{1,0:T(8,128)(2,1)}, bf16[512,768]{1,0:T(8,128)(2,1)}, bf16[512,768...) custom-call(bf16[4,128,768]{2,1,0:T(8,128)(2,1)} %bitcast.4, ...), custom_call_target="tpu_custom_call" | custom-call | tf_op jit(solution)/shard_map/front/pallas_call | solution.py:894
  21.1 15.2 %attend_tiles.1 = (bf16[512,768]{1,0:T(8,128)(2,1)}, bf16[12,512,1024]{2,1,0:T(8,128)(2,1)}, f32[512,768]{1,0:T(8,128)}, bf16[512,768]{1,0:T(8,128)(2,1)}) custom-call(bf16[512,768]{1,0:T(8,128)(2,1)} %get-tuple-element.65.q_ref, bf16[512,768]{1,0:T(8,128)(2,1)} %get-tuple-element.66.k0_ref, bf16[512,768]{1,0:T(8,128)(2,1)} %get-tuple-element.67.k1_ref, ...), custom_call_target="tpu_custom_call" | custom-call | tf_op jit(solution)/shard_map/attend_tiles/pallas_call | solution.py:730
  36.3 4.4 %middle.1 = (bf16[512,768]{1,0:T(8,128)(2,1)}, f32[512,768]{1,0:T(8,128)}, bf16[512,768]{1,0:T(8,128)(2,1)}, bf16[768,512]{1,0:T(8,128)(2,1)}, bf16[512,768]{1,0:T(8,128)(2,1)}) custom-call(bf16[512,768]{1,0:T(8,128)(2,1)} %get-tuple-element.70.mix_ref, bf16[512,768]{1,0:T(8,128)(2,1)} %get-tuple-element.71.x_ref.x_hbm, ...), custom_call_target="tpu_custom_call" | custom-call | tf_op jit(solution)/shard_map/middle/pallas_call | solution.py:239
  40.8 43.8 %feed_turn.1 = (bf16[512,768]{1,0:T(8,128)(2,1)}, f32[512,768]{1,0:T(8,128)}, bf16[512,768]{1,0:T(8,128)(2,1)}, bf16[2,768,384]{2,1,0:T(8,128)(2,1)}, f32[2,8,76...) custom-call(bf16[512,768]{1,0:T(8,128)(2,1)} %get-tuple-element.75.h2_ref, ...), custom_call_target="tpu_custom_call" | custom-call | tf_op jit(solution)/shard_map/feed_turn/pallas_call | solution.py:656
  84.5 87.9 %back.1 = (bf16[4,128,768]{2,1,0:T(8,128)(2,1)}, bf16[4,128,768]{2,1,0:T(8,128)(2,1)}, bf16[2,4,3,192,256]{4,3,2,1,0:T(8,128)(2,1)}, bf16[2,4,4,48,384]{4,3,2,1,...) custom-call(bf16[512,768]{1,0:T(8,128)(2,1)} %get-tuple-element.65.q_ref, ...), custom_call_target="tpu_custom_call" | custom-call | tf_op jit(solution)/shard_map/back/pallas_call | solution.py:1380
  172.4 0.0 copy-start.1
  172.4 15.3 %finish.1 = (f32[4,768]{1,0:T(4,128)}, f32[1001,768]{1,0:T(8,128)}, f32[192,4608]{1,0:T(8,128)}, f32[1152]{0:T(1024)}, f32[192,2304]{1,0:T(8,128)}, /*index=5*/f...) custom-call(bf16[2,4,3,192,256]{4,3,2,1,0:T(8,128)(2,1)} %get-tuple-, ...), custom_call_target="tpu_custom_call" | custom-call | tf_op jit(solution)/shard_map/finish/pallas_call | solution.py:1549
  187.8 0.0 copy-start
  187.8 0.0 copy-done.1
  187.8 0.9 copy.35
  188.7 0.5 copy-done
  189.2 0.9 copy.36
Async XLA Ops:
  172.4 15.4 %copy-start.1 = (bf16[4,128,768]{2,1,0:T(8,128)(2,1)S(1)}, bf16[4,128,768]{2,1,0:T(8,128)(2,1)}, u32[]{:S(2)}) copy-start(bf16[4,128,768]{2,1,0:T(8,128)(2,1)} %get-tuple-element.94) | copy-start | bytes 2359300
  187.8 1.4 copy-start

commit v9 on v8

--- a/solution.py
+++ b/solution.py
@@ -957,8 +957,10 @@
         pltpu.make_async_copy(source, target, load_sem.at[5 + i])
         for i, (source, target) in enumerate(
             (
-                (early_all, early_hbm), (late_all, late_hbm), (feeds_ref, feeds_hbm),
-                (projs_ref, projs_hbm),
+                (early_all, early_hbm), (late_all, late_hbm),
+                (feeds_ref.at[core], feeds_hbm.at[core]), (projs_ref.at[core], projs_hbm.at[core]),
+                (feeds_ref.at[1 - core], feeds_hbm.at[1 - core]),
+                (projs_ref.at[1 - core], projs_hbm.at[1 - core]),
             )
         )
     ]
@@ -1029,10 +1031,10 @@
             here = here.at[pl.ds((k - 1) * half, half)]
         return send(here, here, sends.at[1 + k], recvs.at[1 + k], place.plane(3 - k))
 
-    def gather_pair(which):
+    def gather_pair(which, k):
         full_ref, sends, recvs = gathers[which]
-        here = full_ref.at[core]
-        return send(here, here, sends.at[4], recvs.at[4], place.pair())
+        here = full_ref.at[core, place.flipped(k)]
+        return send(here, here, sends.at[4 + k], recvs.at[4 + k], place.pair())
 
     gathers = ((feeds_ref, feed_send, feed_recv), (projs_ref, proj_send, proj_recv))
     smalls = ((early_ref, early_in, early_all, 8), (late_ref, late_in, late_all, 4))
@@ -1308,6 +1310,7 @@
             ).astype(BF16)
         for k in (1, 2):
             gather_copy(0, k).start()
+        gather_pair(0, 0).start()
         finish(3)
         finish(0)
         finish(1)
@@ -1316,19 +1319,23 @@
         finish(2)
         for k in (1, 2):
             gather_copy(1, k).start()
+        gather_pair(1, 0).start()
         small_next(1, 1)
         for k in (1, 2):
             gather_copy(0, k).wait_recv()
             pass_on(0, k).start()
+            gather_pair(0, k).start()
         small_next(1, 2)
         for k in (1, 2):
             gather_copy(1, k).wait_recv()
             pass_on(1, k).start()
+            gather_pair(1, k).start()
         for which in (0, 1):
             for k in (1, 2):
                 gather_copy(which, k).wait_send()
                 pass_on(which, k).wait()
-            gather_pair(which).start()
+            gather_pair(which, 3).start()
+            stores[2 + which].start()
         for which in (0, 1):
             own_tokens(which).wait()
             for k in (1, 2, 3):
@@ -1353,8 +1360,9 @@
         for g in (1, 2, 3):
             pair_copy(g).wait_send()
         for which in (0, 1):
-            gather_pair(which).wait()
-            stores[2 + which].start()
+            for k in range(4):
+                gather_pair(which, k).wait()
+            stores[4 + which].start()
         for store in stores:
             store.wait()
 
@@ -1400,10 +1408,10 @@
             vmem(GROUPS, 4, part, half), vmem(GROUPS, 3, part, half),
             vmem(*totals.shape), vmem(3, 3, width // 4, 256),
             pltpu.VMEM((8, width), F32), pltpu.VMEM((4, width), F32),
-            sems(9), sems(2), sems(2, 6), sems(2, 6), sems(GROUPS), sems(GROUPS),
+            sems(11), sems(2), sems(2, 6), sems(2, 6), sems(GROUPS), sems(GROUPS),
             sems(GROUPS, 3), sems(GROUPS, 3), sems(GROUPS, 3), sems(GROUPS, 3),
-            sems(2, 2), sems(2, 2), sems(3), sems(3), sems(2, 3), sems(2, 3), sems(5), sems(5),
-            sems(5), sems(5),
+            sems(2, 2), sems(2, 2), sems(3), sems(3), sems(2, 3), sems(2, 3), sems(8), sems(8),
+            sems(8), sems(8),
             sems(2, 7), sems(2, 7),
         ],
         compiler_params=pltpu.CompilerParams(

time: 190 us -> 190 us (level)
  no operation moved by 1% of the time
where the time goes in v9:
time: 190 us; the launch traced here: 189 us
  Pallas kernels  186 us (98%)
  local copies, waits for them, and re-layouts  2.28 us (1%)
    pallas_call x1, Pallas kernels, back_call(): pl.pallas_call(functools.partial(back_kernel, head), grid=(7,), in_specs=...  87.2 us
    pallas_call x1, Pallas kernels, feed_turn_call(): pl.pallas_call(feed_turn_kernel, grid=(9,), in_specs=[once((rows, width))...  43.8 us
    pallas_call x1, Pallas kernels, front_call(): pl.pallas_call(functools.partial(front_kernel, head, tile_cols), in_specs...  20.5 us
    pallas_call x1, Pallas kernels, finish_call(): pl.pallas_call(functools.partial(finish_kernel, head), in_specs=[pl.Block...  15.3 us
    pallas_call x1, Pallas kernels, attend_tiles_call(): pl.pallas_call(functools.partial(attend_tiles_kernel, head ** (-0.5)), gr...  15.2 us
    pallas_call x1, Pallas kernels, middle_call(): pl.pallas_call(middle_kernel, grid=(2,), in_specs=[by_row] * 3 + [full(mo...  4.42 us

profile of v9, /device:TPU:0, one launch (start us, length us, event | category | flops | bytes accessed | tf_op | source)
XLA Modules:
  0.0 189.4 jit_solution(8756502837903150236)
XLA Ops:
  0.7 20.5 %front.1 = (bf16[512,768]{1,0:T(8,128)(2,1)}, bf16[512,768]{1,0:T(8,128)(2,1)}, bf16[512,768]{1,0:T(8,128)(2,1)}, bf16[512,768]{1,0:T(8,128)(2,1)}, bf16[512,768...) custom-call(bf16[4,128,768]{2,1,0:T(8,128)(2,1)} %bitcast.4, ...), custom_call_target="tpu_custom_call" | custom-call | tf_op jit(solution)/shard_map/front/pallas_call | solution.py:894
  21.1 15.2 %attend_tiles.1 = (bf16[512,768]{1,0:T(8,128)(2,1)}, bf16[12,512,1024]{2,1,0:T(8,128)(2,1)}, f32[512,768]{1,0:T(8,128)}, bf16[512,768]{1,0:T(8,128)(2,1)}) custom-call(bf16[512,768]{1,0:T(8,128)(2,1)} %get-tuple-element.65.q_ref, bf16[512,768]{1,0:T(8,128)(2,1)} %get-tuple-element.66.k0_ref, bf16[512,768]{1,0:T(8,128)(2,1)} %get-tuple-element.67.k1_ref, ...), custom_call_target="tpu_custom_call" | custom-call | tf_op jit(solution)/shard_map/attend_tiles/pallas_call | solution.py:730
  36.3 4.4 %middle.1 = (bf16[512,768]{1,0:T(8,128)(2,1)}, f32[512,768]{1,0:T(8,128)}, bf16[512,768]{1,0:T(8,128)(2,1)}, bf16[768,512]{1,0:T(8,128)(2,1)}, bf16[512,768]{1,0:T(8,128)(2,1)}) custom-call(bf16[512,768]{1,0:T(8,128)(2,1)} %get-tuple-element.70.mix_ref, bf16[512,768]{1,0:T(8,128)(2,1)} %get-tuple-element.71.x_ref.x_hbm, ...), custom_call_target="tpu_custom_call" | custom-call | tf_op jit(solution)/shard_map/middle/pallas_call | solution.py:239
  40.8 43.8 %feed_turn.1 = (bf16[512,768]{1,0:T(8,128)(2,1)}, f32[512,768]{1,0:T(8,128)}, bf16[512,768]{1,0:T(8,128)(2,1)}, bf16[2,768,384]{2,1,0:T(8,128)(2,1)}, f32[2,8,76...) custom-call(bf16[512,768]{1,0:T(8,128)(2,1)} %get-tuple-element.75.h2_ref, ...), custom_call_target="tpu_custom_call" | custom-call | tf_op jit(solution)/shard_map/feed_turn/pallas_call | solution.py:656
  84.5 87.2 %back.1 = (bf16[4,128,768]{2,1,0:T(8,128)(2,1)}, bf16[4,128,768]{2,1,0:T(8,128)(2,1)}, bf16[2,4,3,192,256]{4,3,2,1,0:T(8,128)(2,1)}, bf16[2,4,4,48,384]{4,3,2,1,...) custom-call(bf16[512,768]{1,0:T(8,128)(2,1)} %get-tuple-element.65.q_ref, ...), custom_call_target="tpu_custom_call" | custom-call | tf_op jit(solution)/shard_map/back/pallas_call | solution.py:1388
  171.7 0.0 copy-start.1
  171.7 15.3 %finish.1 = (f32[4,768]{1,0:T(4,128)}, f32[1001,768]{1,0:T(8,128)}, f32[192,4608]{1,0:T(8,128)}, f32[1152]{0:T(1024)}, f32[192,2304]{1,0:T(8,128)}, /*index=5*/f...) custom-call(bf16[2,4,3,192,256]{4,3,2,1,0:T(8,128)(2,1)} %get-tuple-, ...), custom_call_target="tpu_custom_call" | custom-call | tf_op jit(solution)/shard_map/finish/pallas_call | solution.py:1557
  187.1 0.0 copy-start
  187.1 0.0 copy-done.1
  187.1 0.9 copy.35
  188.0 0.5 copy-done
  188.5 0.9 copy.36
Async XLA Ops:
  171.7 15.4 %copy-start.1 = (bf16[4,128,768]{2,1,0:T(8,128)(2,1)S(1)}, bf16[4,128,768]{2,1,0:T(8,128)(2,1)}, u32[]{:S(2)}) copy-start(bf16[4,128,768]{2,1,0:T(8,128)(2,1)} %get-tuple-element.94) | copy-start | bytes 2359300
  187.1 1.4 copy-start
